TPU v7x, 32 devices: a whole 2x2x4 slice. The times are simulated.
32 devices in a mesh: dp: 16 (over z, y, x), tensor: 2 (over core).
Axes of the slice: x: 2, y: 2, z: 4, core: 2. Of those that a mesh axis runs over, the one named last changes fastest.
Arguments:
- hidden_in: bfloat16 [2, 16384, 768], P(None, ('dp', 'tensor')), may hold values from -6 to 6
- segment_ids: int32 [2, 16384], P(None, 'dp'), may hold values from 0 to 53, never falling along the last dimension, each value on 1 to 800 neighbouring positions
- qkv_weight: bfloat16 [3, 768, 768], P(None, 'dp', 'tensor'), may hold values from -0.21875 to 0.21875
- out_weight: bfloat16 [768, 768], P('tensor', 'dp'), may hold values from -1.75 to 1.75
- mlp_weight: bfloat16 [2, 768, 1152], P(None, 'dp', 'tensor'), may hold values from -0.21875 to 0.21875
- down_weight: bfloat16 [1152, 768], P('tensor', 'dp'), may hold values from -0.1875 to 0.1875
- attn_gain: bfloat16 [768], P('dp'), may hold values from 0.099609375 to 1.8984375
- mlp_gain: bfloat16 [768], P('dp'), may hold values from 0.099609375 to 1.8984375
- cotangent: bfloat16 [2, 16384, 768], P(None, ('dp', 'tensor')), may hold values from -6 to 6
Outputs:
- layer_out: bfloat16 [2, 16384, 768], P(None, ('dp', 'tensor'))
- input_grad: float32 [2, 16384, 768], P(None, ('dp', 'tensor'))
- qkv_grad: float32 [3, 768, 768], P(None, 'dp', 'tensor')
- proj_grad: float32 [768, 768], P('tensor', 'dp')
- mlp_grad: float32 [2, 768, 1152], P(None, 'dp', 'tensor')
- down_grad: float32 [1152, 768], P('tensor', 'dp')
- attn_gain_grad: float32 [768], P('dp')
- mlp_gain_grad: float32 [768], P('dp')
Inputs may be any that keep to these rules, and one draw needn't show every extreme that they name: `segment_ids`: along each micro-batch's 16384 tokens the segment ids never fall; each document has 1 to 800 tokens and one has exactly 800.
All inputs are finite; a program needn't handle non-finite values.
Results may differ from a plain program's by a relative error of at most 0.018.
Values may be sent and summed in bfloat16 or wider, within the bound.
No kernel may reach another device: no remote copies, remote signals or barrier semaphores. Data moves between devices by JAX's collectives and lax.ppermute only.
A program may use at most 128 MiB of HBM per device.

v0:
```python
import jax
import jax.numpy as jnp
from jax import lax
from jax.sharding import PartitionSpec as P

HEAD_DIM = 64
MB = 2


theta_base = 160000.0
eps_norm = 1e-05


def positions_of(segments):
    indices = jnp.arange(segments.shape[0], dtype=jnp.int32)
    change = jnp.concatenate([jnp.ones((1,), dtype=jnp.bool_), segments[1:] != segments[:-1]])
    starts = lax.cummax(jnp.where(change, indices, jnp.zeros_like(indices)), axis=0)
    return indices - starts


def rotary_tables(segments):
    half_dim = HEAD_DIM // 2
    freqs = theta_base ** (-2.0 * jnp.arange(half_dim, dtype=jnp.float32) / HEAD_DIM)
    angles = positions_of(segments).astype(jnp.float32)[:, None] * freqs[None, :]
    return (jnp.cos(angles)[:, None, :], jnp.sin(angles)[:, None, :])


def rotate(values, cosine, sine):
    half_dim = values.shape[-1] // 2
    first_half = values[..., :half_dim]
    second_half = values[..., half_dim:]
    return jnp.concatenate(
        [first_half * cosine - second_half * sine, second_half * cosine + first_half * sine],
        axis=-1,
    )


def rotate_back(grads, cosine, sine):
    half_dim = grads.shape[-1] // 2
    first_half = grads[..., :half_dim]
    second_half = grads[..., half_dim:]
    return jnp.concatenate(
        [first_half * cosine + second_half * sine, second_half * cosine - first_half * sine],
        axis=-1,
    )


def normalize(values):
    center = values - jnp.mean(values, axis=-1, keepdims=True)
    inverse = lax.rsqrt(jnp.mean(center * center, axis=-1, keepdims=True) + eps_norm)
    return (center * inverse, inverse)


def norm_back(grad_normed, centered, inverse, gain):
    scaled = grad_normed * gain
    inner = (
        scaled
        - jnp.mean(scaled, axis=-1, keepdims=True)
        - centered * jnp.mean(scaled * centered, axis=-1, keepdims=True)
    )
    return (inverse * inner, jnp.sum(grad_normed * centered, axis=0))


def gelu_exact(values):
    return jax.nn.gelu(values, approximate=False)


def masked_scores(queries, keys, seg_rows, segments, scale):
    scores = jnp.einsum("qhe,khe->hqk", queries, keys, preferred_element_type=jnp.float32) * scale
    allowed = seg_rows[:, None] == segments[None, :]
    return jnp.where(allowed[None], scores, -1e30)


def attend_block(queries, seg_rows, keys, values, segments, scale):
    scores = masked_scores(queries, keys, seg_rows, segments, scale)
    peak = jnp.max(scores, axis=-1, keepdims=True)
    expo = jnp.exp(scores - peak)
    denominator = jnp.sum(expo, axis=-1, keepdims=True)
    probs = (expo / denominator).astype(jnp.bfloat16)
    outputs = jnp.einsum("hqk,khe->qhe", probs, values, preferred_element_type=jnp.float32).astype(
        jnp.bfloat16
    )
    return (outputs, (peak + jnp.log(denominator))[..., 0])


def attend_back(queries, grad_out, log_total, seg_rows, keys, values, segments, scale):
    scores = masked_scores(queries, keys, seg_rows, segments, scale)
    probs_full = jnp.exp(scores - log_total[..., None])
    grad_probs = jnp.einsum("qhe,khe->hqk", grad_out, values, preferred_element_type=jnp.float32)
    delta = jnp.sum(probs_full * grad_probs, axis=-1, keepdims=True)
    grad_scores = (probs_full * (grad_probs - delta)).astype(jnp.bfloat16)
    grad_queries = (
        jnp.einsum("hqk,khe->qhe", grad_scores, keys, preferred_element_type=jnp.float32) * scale
    )
    grad_keys = (
        jnp.einsum("hqk,qhe->khe", grad_scores, queries, preferred_element_type=jnp.float32) * scale
    )
    grad_values = jnp.einsum(
        "hqk,qhe->khe",
        probs_full.astype(jnp.bfloat16),
        grad_out,
        preferred_element_type=jnp.float32,
    )
    return (grad_queries, grad_keys, grad_values)


def local(
    hidden_in,
    segment_ids,
    qkv_weight,
    out_weight,
    mlp_weight,
    down_weight,
    attn_gain,
    mlp_gain,
    cotangent,
):
    seq_len = segment_ids.shape[1]
    width_here = qkv_weight.shape[2]
    heads_here = width_here // HEAD_DIM
    scale = HEAD_DIM ** (-0.5)
    block = min(seq_len, 512)
    blocks = seq_len // block
    local_weights = (qkv_weight, out_weight, mlp_weight, down_weight, attn_gain, mlp_gain)
    kept = (
        lax.all_gather(local_weights[0], "dp", axis=1, tiled=True),
        lax.all_gather(local_weights[1], "dp", axis=1, tiled=True),
        lax.all_gather(local_weights[2], "dp", axis=1, tiled=True),
        lax.all_gather(local_weights[3], "dp", axis=1, tiled=True),
        lax.all_gather(local_weights[4], "dp", axis=0, tiled=True),
        lax.all_gather(local_weights[5], "dp", axis=0, tiled=True),
    )
    layer_rows = []
    input_rows = []
    totals = ()
    for batch_index in range(MB):
        qkv_full, proj_full, mlp_full, down_full, gain_attn, gain_mlp = kept
        segments = segment_ids[batch_index]
        cosine, sine = rotary_tables(segments)
        rows_in = hidden_in[batch_index].astype(jnp.float32)
        centered_one, inverse_one = normalize(rows_in)
        normed_one = (centered_one * gain_attn.astype(jnp.float32)).astype(jnp.bfloat16)
        whole_one = lax.all_gather(normed_one, "tensor", axis=0, tiled=True)
        raw = jnp.einsum("rd,cde->cre", whole_one, qkv_full, preferred_element_type=jnp.float32)
        queries = rotate(raw[0].reshape(seq_len, heads_here, HEAD_DIM), cosine, sine).astype(
            jnp.bfloat16
        )
        keys = rotate(raw[1].reshape(seq_len, heads_here, HEAD_DIM), cosine, sine).astype(
            jnp.bfloat16
        )
        values = raw[2].reshape(seq_len, heads_here, HEAD_DIM).astype(jnp.bfloat16)
        query_blocks = queries.reshape(blocks, block, heads_here, HEAD_DIM)
        segment_blocks = segments.reshape(blocks, block)

        def run_block(pair):
            return attend_block(pair[0], pair[1], keys, values, segments, scale)

        attended_blocks, log_totals = lax.map(run_block, (query_blocks, segment_blocks))
        attended = attended_blocks.reshape(seq_len, width_here)
        middle = rows_in + lax.psum_scatter(
            jnp.dot(attended, proj_full, preferred_element_type=jnp.float32),
            "tensor",
            scatter_dimension=0,
            tiled=True,
        )
        centered_two, inverse_two = normalize(middle)
        normed_two = (centered_two * gain_mlp.astype(jnp.float32)).astype(jnp.bfloat16)
        whole_two = lax.all_gather(normed_two, "tensor", axis=0, tiled=True)
        gate_up = jnp.einsum("rd,cdf->crf", whole_two, mlp_full, preferred_element_type=jnp.float32)
        activated, gelu_pull = jax.vjp(gelu_exact, gate_up[0])
        mixed = (activated * gate_up[1]).astype(jnp.bfloat16)
        result_rows = middle + lax.psum_scatter(
            jnp.dot(mixed, down_full, preferred_element_type=jnp.float32).astype(jnp.bfloat16),
            "tensor",
            scatter_dimension=0,
            tiled=True,
        ).astype(jnp.float32)
        layer_rows.append(result_rows.astype(jnp.bfloat16))
        qkv_full, proj_full, mlp_full, down_full, gain_attn, gain_mlp = kept
        grad_result = cotangent[batch_index].astype(jnp.float32)
        whole_grad_out = lax.all_gather(
            grad_result.astype(jnp.bfloat16), "tensor", axis=0, tiled=True
        )
        down_term = jnp.einsum(
            "rf,rd->fd", mixed, whole_grad_out, preferred_element_type=jnp.float32
        )
        grad_mixed = jnp.einsum(
            "rd,fd->rf", whole_grad_out, down_full, preferred_element_type=jnp.float32
        )
        grad_gate = gelu_pull(grad_mixed * gate_up[1])[0]
        grad_gate_up = jnp.stack([grad_gate, grad_mixed * activated]).astype(jnp.bfloat16)
        mlp_term = jnp.einsum(
            "rd,crf->cdf", whole_two, grad_gate_up, preferred_element_type=jnp.float32
        )
        grad_normed_two = lax.psum_scatter(
            jnp.einsum(
                "crf,cdf->rd", grad_gate_up, mlp_full, preferred_element_type=jnp.float32
            ).astype(jnp.bfloat16),
            "tensor",
            scatter_dimension=0,
            tiled=True,
        ).astype(jnp.float32)
        grad_middle, mlp_gain_term = norm_back(
            grad_normed_two, centered_two, inverse_two, gain_mlp.astype(jnp.float32)
        )
        grad_middle = grad_result + grad_middle
        whole_grad_branch = lax.all_gather(
            grad_middle.astype(jnp.bfloat16), "tensor", axis=0, tiled=True
        )
        proj_term = jnp.einsum(
            "re,rd->ed", attended, whole_grad_branch, preferred_element_type=jnp.float32
        )
        grad_attended = jnp.einsum(
            "rd,ed->re", whole_grad_branch, proj_full, preferred_element_type=jnp.float32
        )
        grad_attended = grad_attended.astype(jnp.bfloat16).reshape(
            blocks, block, heads_here, HEAD_DIM
        )

        def back_step(carry, pieces):
            keys_sum, values_sum = carry
            grad_queries, grad_keys, grad_values = attend_back(
                pieces[0], pieces[1], pieces[2], pieces[3], keys, values, segments, scale
            )
            return ((keys_sum + grad_keys, values_sum + grad_values), grad_queries)

        empty = jnp.zeros((seq_len, heads_here, HEAD_DIM), jnp.float32)
        (grad_keys_all, grad_values_all), grad_query_blocks = lax.scan(
            back_step, (empty, empty), (query_blocks, grad_attended, log_totals, segment_blocks)
        )
        grad_queries_all = grad_query_blocks.reshape(seq_len, heads_here, HEAD_DIM)
        grad_raw = jnp.stack(
            [
                rotate_back(grad_queries_all, cosine, sine).reshape(seq_len, width_here),
                rotate_back(grad_keys_all, cosine, sine).reshape(seq_len, width_here),
                grad_values_all.reshape(seq_len, width_here),
            ]
        ).astype(jnp.bfloat16)
        qkv_term = jnp.einsum(
            "rd,cre->cde", whole_one, grad_raw, preferred_element_type=jnp.float32
        )
        grad_normed_one = lax.psum_scatter(
            jnp.einsum(
                "cre,cde->rd", grad_raw, qkv_full, preferred_element_type=jnp.float32
            ).astype(jnp.bfloat16),
            "tensor",
            scatter_dimension=0,
            tiled=True,
        ).astype(jnp.float32)
        grad_input, attn_gain_term = norm_back(
            grad_normed_one, centered_one, inverse_one, gain_attn.astype(jnp.float32)
        )
        input_rows.append(grad_middle + grad_input)
        terms = (qkv_term, proj_term, mlp_term, down_term, attn_gain_term, mlp_gain_term)
        if batch_index == 0:
            totals = terms
        else:
            totals = jax.tree.map(jnp.add, totals, terms)
    totals = (
        lax.psum_scatter(totals[0], "dp", scatter_dimension=1, tiled=True),
        lax.psum_scatter(totals[1], "dp", scatter_dimension=1, tiled=True),
        lax.psum_scatter(totals[2], "dp", scatter_dimension=1, tiled=True),
        lax.psum_scatter(totals[3], "dp", scatter_dimension=1, tiled=True),
        lax.psum_scatter(totals[4], "dp", scatter_dimension=0, tiled=True),
        lax.psum_scatter(totals[5], "dp", scatter_dimension=0, tiled=True),
    )
    gain_sums = lax.psum((totals[4], totals[5]), "tensor")
    return (
        jnp.stack(layer_rows),
        jnp.stack(input_rows),
        totals[0],
        totals[1],
        totals[2],
        totals[3],
        gain_sums[0],
        gain_sums[1],
    )


def solution(mesh):
    in_specs = (
        P(None, ("dp", "tensor"), None),
        P(None, "dp"),
        P(None, "dp", "tensor"),
        P("tensor", "dp"),
        P(None, "dp", "tensor"),
        P("tensor", "dp"),
        P("dp"),
        P("dp"),
        P(None, ("dp", "tensor"), None),
    )
    out_specs = (
        P(None, ("dp", "tensor"), None),
        P(None, ("dp", "tensor"), None),
        P(None, "dp", "tensor"),
        P("tensor", "dp"),
        P(None, "dp", "tensor"),
        P("tensor", "dp"),
        P("dp"),
        P("dp"),
    )
    return jax.shard_map(local, mesh=mesh, in_specs=in_specs, out_specs=out_specs, check_vma=False)
```

profile of v0, /device:TPU:0, one launch (start us, length us, event | category | flops | bytes accessed | tf_op | source)
XLA Modules:
  0.0 1222.7 jit_solution(11083971720489086673)
XLA Ops:
  11.0 44.1 %all-reduce.9 = (bf16[768]{0:T(1024)(128)(2,1)S(1)}, bf16[768]{0:T(1024)(128)(2,1)}) all-reduce(bf16[768]{0:T(1024)(128)(2,1)S(1)} %dynamic-update-slice, bf16[768]{0:T(1024)(128)(2,1)S(1)} %dynamic-update-slice.1), channel_id=1, replica_groups=mesh['dp'=16,'tensor'=2] {'dp'}, use_global_device_ids=true, to_apply=%add | all-reduce | flops 1536 | bytes 6144
  63.8 42.5 %all_gather.45 = bf16[384,768]{0,1:T(8,128)(2,1)} all-gather(bf16[384,48]{0,1:T(8,128)(2,1)S(1)} %copy-done.67), channel_id=1, replica_groups=mesh['dp'=16,'tensor'=2] {'dp'}, dimensions={1}, use_global_device_ids=true | all-gather | bytes 626688 | tf_op jit(solution)/shard_map/all_gather | solution.py:127
  106.3 21.9 %all-gather.15.cloned.1.call-done = bf16[3,768,384]{2,1,0:T(8,128)(2,1)} async-done(((bf16[3,48,384]{2,1,0:T(8,128)(2,1)}), bf16[3,768,384]{2,1,0:T(8,128)(2,1)}) %all-gather.15.cloned.1.call-update) | async-done | bytes 1769488 | tf_op jit(solution)/shard_map/all_gather | solution.py:126
  128.2 4.0 convolution_bitcast_fusion.1
  134.7 4.2 all-gather.13.cloned.1.call-done
  138.9 4.0 convolution_bitcast_fusion.3
  148.1 25.2 %while.55 = (s32[]{:T(128)}, bf16[2,512,6,64]{1,3,2,0:T(8,128)(2,1)S(1)}, f32[2,6,512]{2,1,0:T(8,128)S(1)}, s32[2,512]{1,0:T(2,128)S(1)}, s32[1,1024]{1,0:T(1,12...) while((s32[]{:T(128)}, ...), condition=%wide.region_19.20_spmd, body=%wide.region_16.19_spmd.sunk | while | flops 843772928 | bytes 42334324 | solution.py:158
  152.0 3.6 fusion.300
  155.7 5.1 fusion.301
  164.5 3.6 fusion.300
  168.2 5.1 fusion.301
  182.2 26.4 %while.54 = (s32[]{:T(128)}, bf16[2,512,6,64]{1,3,2,0:T(8,128)(2,1)S(1)}, f32[2,6,512]{2,1,0:T(8,128)}, s32[2,512]{1,0:T(2,128)S(1)}, s32[1,1024]{1,0:T(1,128)S(...) while((s32[]{:T(128)}, ...), condition=%wide.region_7.8_spmd, body=%wide.region_4.7_spmd.sunk | while | flops 843772928 | bytes 42326132 | solution.py:158
  186.2 3.6 fusion.295
  189.8 5.1 fusion.296
  199.3 3.6 fusion.295
  202.9 5.1 fusion.296
  216.8 8.6 reduce-scatter.11.cloned.1.call-done
  230.3 49.3 %all_gather.49 = bf16[576,768]{0,1:T(8,128)(2,1)S(1)} all-gather(bf16[576,48]{0,1:T(8,128)(2,1)S(1)} %copy-done.62), channel_id=1, replica_groups=mesh['dp'=16,'tensor'=2] {'dp'}, dimensions={1}, use_global_device_ids=true | all-gather | bytes 940032 | tf_op jit(solution)/shard_map/all_gather | solution.py:129
  279.7 4.3 fusion.166
  284.0 18.8 %all-gather.19.cloned.1.call-done = bf16[2,768,576]{2,1,0:T(8,128)(2,1)} async-done(((bf16[2,48,576]{2,1,0:T(8,128)(2,1)}), bf16[2,768,576]{2,1,0:T(8,128)(2,1)}) %all-gather.19.cloned.1.call-update) | async-done | bytes 1769488 | tf_op jit(solution)/shard_map/all_gather | solution.py:128
  302.8 10.0 all-gather.17.cloned.1.call-done
  312.8 4.3 convolution_bitcast_fusion.2
  317.1 5.6 fusion.183
  331.4 8.7 reduce-scatter.19.cloned.1.call-done
  343.8 8.8 all-gather.31.cloned.1.call-done
  352.6 4.2 fusion.162
  356.8 9.0 all-gather.23.cloned.1.call-done
  365.8 4.3 convolution_bitcast_fusion
  370.1 5.6 fusion.184
  382.7 4.2 convolution_convert_fusion.1
  386.9 4.2 convolution_convert_fusion
  395.5 10.0 reduce-scatter.13.cloned.1.call-done
  405.6 13.1 %reduce-scatter.17.cloned.1.call-done = bf16[512,768]{1,0:T(8,128)(2,1)} async-done(((bf16[1024,768]{1,0:T(8,128)(2,1)}), bf16[512,768]{1,0:T(8,128)(2,1)}) %reduce-scatter.17.cloned.1.call-update) | async-done | bytes 786448 | tf_op jit(solution)/shard_map/reduce_scatter | solution.py:172
  418.6 5.0 fusion.201
  424.3 10.5 all-gather.27.cloned.1.call-done
  443.2 3.9 all-gather.25.cloned.1.call-done
  457.1 89.4 %while.57 = (s32[]{:T(128)}, f32[1024,6,64]{0,2,1:T(8,128)S(1)}, f32[1024,6,64]{0,2,1:T(8,128)}, f32[2,512,6,64]{1,0,3,2:T(2,128)}, bf16[2,512,6,64]{1,3,2,0:T(8...) while((s32[]{:T(128)}, f32[1024,6,64]{0,2,1:T(8,128)S(1)}, ...), condition=%wide.region_38.39_spmd.clone, body=%wide.region_36.38_spmd.clone.sunk | while | flops 2063135744 | bytes 110721200 | solution.py:228
  460.8 5.5 bitcast_add_fusion.11
  466.3 8.3 multiply_reduce_fusion.7
  474.6 6.9 multiply_convert_fusion.11
  486.7 15.0 %dynamic_update_slice.38 = f32[2,512,6,64]{1,0,3,2:T(2,128)} dynamic-update-slice(f32[2,512,6,64]{1,0,3,2:T(2,128)} %get-tuple-element.926, f32[1,512,6,64]{1,0,3,2:T(1,128)S(1)} %copy.118, s32[]{:T(128)S(6)} %copy.163, s32[]{:T(128)} %constant.72.clone.1..sunk.1, s32[]{:T(128)} %constant.72.clone.1..sunk.1, s32[]{:T(128)} %constant.72.clone.1..sunk.1) | dynamic-update-slice | bytes 1572868 | tf_op jit(solution)/shard_map/while/body/jit(dynamic_update_index_in_dim)/dynamic_update_slice | solution.py:228
  504.9 6.1 bitcast_add_fusion.11
  511.0 8.3 multiply_reduce_fusion.7
  519.3 6.9 multiply_convert_fusion.11
  531.4 15.0 %dynamic_update_slice.38 = f32[2,512,6,64]{1,0,3,2:T(2,128)} dynamic-update-slice(f32[2,512,6,64]{1,0,3,2:T(2,128)} %get-tuple-element.926, f32[1,512,6,64]{1,0,3,2:T(1,128)S(1)} %copy.118, s32[]{:T(128)S(6)} %copy.163, s32[]{:T(128)} %constant.72.clone.1..sunk.1, s32[]{:T(128)} %constant.72.clone.1..sunk.1, s32[]{:T(128)} %constant.72.clone.1..sunk.1) | dynamic-update-slice | bytes 1572868 | tf_op jit(solution)/shard_map/while/body/jit(dynamic_update_index_in_dim)/dynamic_update_slice | solution.py:228
  555.0 5.2 bitcast_convert_fusion
  562.4 90.5 %while.56 = (s32[]{:T(128)}, f32[1024,6,64]{0,2,1:T(8,128)S(1)}, f32[1024,6,64]{0,2,1:T(8,128)}, f32[2,512,6,64]{1,0,3,2:T(2,128)}, bf16[2,512,6,64]{1,3,2,0:T(8...) while((s32[]{:T(128)}, f32[1024,6,64]{0,2,1:T(8,128)S(1)}, ...), condition=%wide.region_29.30_spmd.clone, body=%wide.region_27.29_spmd.clone.sunk | while | flops 2063135744 | bytes 110721200 | solution.py:228
  566.3 5.5 bitcast_add_fusion.9
  571.8 8.3 multiply_reduce_fusion.6
  580.2 6.9 multiply_convert_fusion.10
  592.2 14.9 %dynamic_update_slice.37 = f32[2,512,6,64]{1,0,3,2:T(2,128)} dynamic-update-slice(f32[2,512,6,64]{1,0,3,2:T(2,128)} %get-tuple-element.887, f32[1,512,6,64]{1,0,3,2:T(1,128)S(1)} %copy.117, s32[]{:T(128)S(6)} %copy.151, s32[]{:T(128)} %constant.72.clone.1..sunk, s32[]{:T(128)} %constant.72.clone.1..sunk, s32[]{:T(128)} %constant.72.clone.1..sunk) | dynamic-update-slice | bytes 1572868 | tf_op jit(solution)/shard_map/while/body/jit(dynamic_update_index_in_dim)/dynamic_update_slice | solution.py:228
  611.1 6.1 bitcast_add_fusion.9
  617.2 8.3 multiply_reduce_fusion.6
  625.5 6.9 multiply_convert_fusion.10
  637.6 14.9 %dynamic_update_slice.37 = f32[2,512,6,64]{1,0,3,2:T(2,128)} dynamic-update-slice(f32[2,512,6,64]{1,0,3,2:T(2,128)} %get-tuple-element.887, f32[1,512,6,64]{1,0,3,2:T(1,128)S(1)} %copy.117, s32[]{:T(128)S(6)} %copy.151, s32[]{:T(128)} %constant.72.clone.1..sunk, s32[]{:T(128)} %constant.72.clone.1..sunk, s32[]{:T(128)} %constant.72.clone.1..sunk) | dynamic-update-slice | bytes 1572868 | tf_op jit(solution)/shard_map/while/body/jit(dynamic_update_index_in_dim)/dynamic_update_slice | solution.py:228
  662.7 5.5 bitcast_convert_fusion.2
  668.3 3.5 fusion.172
  673.9 5.4 copy.76
  679.4 4.4 fusion.175
  686.1 4.0 copy.75
  707.5 45.3 %all-reduce.6 = (f32[768]{0:T(1024)S(1)}, f32[768]{0:T(1024)S(1)}) all-reduce(f32[768]{0:T(1024)S(1)} %add.218, f32[768]{0:T(1024)S(1)} %add.219), channel_id=16, replica_groups=mesh['dp'=16,'tensor'=2] {'dp'}, use_global_device_ids=true, to_apply=%region_48.49.clone | all-reduce | flops 1536 | bytes 12288
  760.4 196.3 %all-reduce.12.cloned.1.call-done = (f32[3,768,384]{2,0,1:T(4,128)}, f32[2,768,576]{2,0,1:T(2,128)}) async-done(((f32[3,768,384]{2,0,1:T(4,128)}, f32[2,768,576]{2,0,1:T(2,128)}), (f32[3,768,384]{2,0,1:T(4,128)}, f32[2,768,576]{2,0,1:T(2,128)})) %all-reduce.12.cloned.1.call-update) | async-done | bytes 7077904
  960.1 127.5 %reduce-scatter.29.cloned.1.call-done = f32[576,48]{0,1:T(8,128)} async-done(((f32[576,768]{0,1:T(8,128)}), f32[576,48]{0,1:T(8,128)}) %reduce-scatter.29.cloned.1.call-update) | async-done | bytes 110608 | tf_op jit(solution)/shard_map/reduce_scatter | solution.py:263
  1087.7 128.0 %reduce-scatter.27.cloned.1.call-done = f32[384,48]{0,1:T(8,128)} async-done(((f32[384,768]{0,1:T(8,128)}), f32[384,48]{0,1:T(8,128)}) %reduce-scatter.27.cloned.1.call-update) | async-done | bytes 73744 | tf_op jit(solution)/shard_map/reduce_scatter | solution.py:261
  (376 shorter events, 187.0 us)
Async XLA Ops:
  7.2 49.5 %copy-start.5 = (bf16[2,512,768]{2,1,0:T(8,128)(2,1)S(1)}, bf16[2,512,768]{2,1,0:T(8,128)(2,1)}, u32[]{:S(2)}) copy-start(bf16[2,512,768]{2,1,0:T(8,128)(2,1)} %param.17) | copy-start | bytes 4718596
  7.2 99.1 %all-gather.21.cloned.1.call-start = ((), (), s32[]{:S(2)}) async-start(), calls=%async_computation.16 | async-start | bytes 2359296 | tf_op jit(solution)/shard_map/all_gather | solution.py:143
  55.0 4.1 copy-start.60
  57.4 3.3 copy-start.59
  57.4 6.4 copy-start.67
  59.1 69.1 %all-gather.15.cloned.1.call-start = ((), (), s32[]{:S(2)}) async-start(), calls=%async_computation.11 | async-start | bytes 1880064 | tf_op jit(solution)/shard_map/all_gather | solution.py:126
  59.9 79.0 %all-gather.13.cloned.1.call-start = ((), (), s32[]{:S(2)}) async-start(), calls=%async_computation.10 | async-start | bytes 2359296 | tf_op jit(solution)/shard_map/all_gather | solution.py:143
  60.6 156.1 %reduce-scatter.15.cloned.1.call-start = ((), (), s32[]{:S(2)}) async-start(), calls=%async_computation.17 | async-start | bytes 4718592 | tf_op jit(solution)/shard_map/reduce_scatter | solution.py:160
  63.8 81.6 %copy-start.35 = (f32[1024,32]{0,1:T(8,128)}, f32[1024,32]{0,1:T(8,128)S(1)}, u32[]{:S(2)}) copy-start(f32[1024,32]{0,1:T(8,128)S(1)} %get-tuple-element.563) | copy-start | bytes 393220
  63.8 114.2 %copy-start.33 = (f32[1024,32]{0,1:T(8,128)}, f32[1024,32]{0,1:T(8,128)S(1)}, u32[]{:S(2)}) copy-start(f32[1024,32]{0,1:T(8,128)S(1)} %get-tuple-element.556) | copy-start | bytes 393220
  63.8 114.2 %copy-start.34 = (f32[1024,32]{0,1:T(8,128)}, f32[1024,32]{0,1:T(8,128)S(1)}, u32[]{:S(2)}) copy-start(f32[1024,32]{0,1:T(8,128)S(1)} %get-tuple-element.557) | copy-start | bytes 393220
  173.2 4.7 copy-start.2
  173.3 4.7 copy-start.51
  173.3 4.7 copy-start.53
  173.3 4.7 copy-start.57
  178.0 47.4 %reduce-scatter.11.cloned.1.call-start = ((), (), s32[]{:S(2)}) async-start(), calls=%async_computation.12 | async-start | bytes 4718592 | tf_op jit(solution)/shard_map/reduce_scatter | solution.py:160
  208.6 4.5 copy-start
  208.6 4.5 copy-start.49
  208.6 4.5 copy-start.55
  213.2 3.5 copy-start.74
  213.2 12.2 copy-start.6
  213.2 66.4 %all-gather.29.cloned.1.call-start = ((), (), s32[]{:S(2)}) async-start(), calls=%async_computation.28 | async-start | bytes 2359296 | tf_op jit(solution)/shard_map/all_gather | solution.py:181
  215.9 86.8 %all-gather.19.cloned.1.call-start = ((), (), s32[]{:S(2)}) async-start(), calls=%async_computation.14 | async-start | bytes 2088960 | tf_op jit(solution)/shard_map/all_gather | solution.py:128
  216.7 96.1 %all-gather.17.cloned.1.call-start = ((), (), s32[]{:S(2)}) async-start(), calls=%async_computation.13 | async-start | bytes 2359296 | tf_op jit(solution)/shard_map/all_gather | solution.py:168
  230.3 109.8 %reduce-scatter.19.cloned.1.call-start = ((), (), s32[]{:S(2)}) async-start(), calls=%async_computation.20 | async-start | bytes 2359296 | tf_op jit(solution)/shard_map/reduce_scatter | solution.py:195
  279.6 4.3 copy-start.41
  312.8 4.3 copy-start.9
  322.7 3.4 copy-start.75
  329.7 22.9 %all-gather.31.cloned.1.call-start = ((), (), s32[]{:S(2)}) async-start(), calls=%async_computation.29 | async-start | bytes 2359296 | tf_op jit(solution)/shard_map/all_gather | solution.py:181
  330.3 35.5 %all-gather.23.cloned.1.call-start = ((), (), s32[]{:S(2)}) async-start(), calls=%async_computation.18 | async-start | bytes 2359296 | tf_op jit(solution)/shard_map/all_gather | solution.py:168
  343.5 49.5 %reduce-scatter.23.cloned.1.call-start = ((), (), s32[]{:S(2)}) async-start(), calls=%async_computation.23 | async-start | bytes 2359296 | tf_op jit(solution)/shard_map/reduce_scatter | solution.py:195
  365.8 4.3 copy-start.10
  375.8 3.4 copy-start.76
  382.7 22.9 %reduce-scatter.13.cloned.1.call-start = ((), (), s32[]{:S(2)}) async-start(), calls=%async_computation.15 | async-start | bytes 2359296 | tf_op jit(solution)/shard_map/reduce_scatter | solution.py:172
  386.9 31.8 %reduce-scatter.17.cloned.1.call-start = ((), (), s32[]{:S(2)}) async-start(), calls=%async_computation.19 | async-start | bytes 2359296 | tf_op jit(solution)/shard_map/reduce_scatter | solution.py:172
  391.1 43.7 %all-gather.27.cloned.1.call-start = ((), (), s32[]{:S(2)}) async-start(), calls=%async_computation.24 | async-start | bytes 2359296 | tf_op jit(solution)/shard_map/all_gather | solution.py:207
  423.6 23.6 %all-gather.25.cloned.1.call-start = ((), (), s32[]{:S(2)}) async-start(), calls=%async_computation.21 | async-start | bytes 2359296 | tf_op jit(solution)/shard_map/all_gather | solution.py:207
  424.2 280.3 %reduce-scatter.25.cloned.1.call-start = ((), (), s32[]{:S(2)}) async-start(), calls=%async_computation.25 | async-start | bytes 2359296 | tf_op jit(solution)/shard_map/reduce_scatter | solution.py:242
  438.2 9.0 copy-start.19
  451.9 5.2 copy-start.3
  451.9 5.2 copy-start.52
  451.9 5.2 copy-start.54
  451.9 5.2 copy-start.58
  551.8 3.2 copy-start.42
  555.0 5.2 copy-start.46
  560.3 144.3 %reduce-scatter.21.cloned.1.call-start = ((), (), s32[]{:S(2)}) async-start(), calls=%async_computation.22 | async-start | bytes 2359296 | tf_op jit(solution)/shard_map/reduce_scatter | solution.py:242
  658.2 4.5 copy-start.48
  662.7 5.6 copy-start.29
  662.7 5.6 copy-start.38
  668.2 288.5 %all-reduce.12.cloned.1.call-start = ((), (), s32[]{:S(2)}) async-start(), calls=%async_computation.30 | async-start | bytes 17301504
  668.3 3.6 copy-start.32
  668.3 3.6 copy-start.40
  668.3 3.6 copy-start.79
  679.4 4.4 copy-start.43
  679.4 4.4 copy-start.45
  679.4 4.4 copy-start.47
  679.4 4.5 copy-start.77
  690.1 4.3 copy-start.27
  690.1 397.6 %reduce-scatter.29.cloned.1.call-start = ((), (), s32[]{:S(2)}) async-start(), calls=%async_computation.27 | async-start | bytes 2088960 | tf_op jit(solution)/shard_map/reduce_scatter | solution.py:263
  691.3 3.0 copy-start.78
  697.1 3.0 copy-start.12
  697.2 518.5 %reduce-scatter.27.cloned.1.call-start = ((), (), s32[]{:S(2)}) async-start(), calls=%async_computation.26 | async-start | bytes 1253376 | tf_op jit(solution)/shard_map/reduce_scatter | solution.py:261
  700.2 3.0 copy-start.20
  704.5 51.4 %copy-start.16 = (f32[512,768]{1,0:T(8,128)S(1)}, f32[512,768]{1,0:T(8,128)}, u32[]{:S(2)}) copy-start(f32[512,768]{1,0:T(8,128)} %get-tuple-element.491) | copy-start | bytes 4718596
  (37 other events, 71.5 us)
Sparse Core Ops, SparseCore 0:
  59.3 5.6 all-gather.20
  67.7 60.4 all-gather.14
  130.3 8.5 all-gather.12
  178.1 12.0 reduce-scatter.14
  213.3 12.0 reduce-scatter.10
  226.8 10.9 all-gather.28
  240.5 62.2 all-gather.18
  304.3 8.4 all-gather.16
  329.8 10.2 reduce-scatter.18
  341.6 10.9 all-gather.30
  354.8 10.9 all-gather.22
  382.8 10.2 reduce-scatter.22
  395.3 10.2 reduce-scatter.12
  408.3 10.2 reduce-scatter.16
  423.7 10.9 all-gather.26
  436.2 10.9 all-gather.24
  560.4 10.2 reduce-scatter.24
  668.3 10.2 reduce-scatter.20
  690.2 266.4 all-reduce.11
  962.8 124.8 reduce-scatter.28
  1093.0 122.6 reduce-scatter.26
where the time goes:
time: 1240 us; the launch traced here: 1220 us
  waiting for transfers between devices  585 us (47%)
  matrix products  206 us (17%)
  blocking collectives  184 us (15%)
  local copies, waits for them, and re-layouts  126 us (10%)
  other arithmetic  102 us (8%)
  between operations  17.1 us (1%)
    unnamed x22, waiting for transfers between devices  200 us
    reduce_scatter x1, waiting for transfers between devices, local(): lax.psum_scatter(totals[1], 'dp', scatter_dimension=1, tiled=True)  128 us
    reduce_scatter x1, waiting for transfers between devices, local(): lax.psum_scatter(totals[3], 'dp', scatter_dimension=1, tiled=True)  128 us
    unnamed x2, blocking collectives  89.4 us
    dynamic_update_slice x8, local copies, waits for them, and re-layouts, local(): lax.scan(back_step, (empty, empty), (query_blocks, grad_attended, log_tot...  63.1 us
    all_gather x1, blocking collectives, local(): lax.all_gather(local_weights[3], 'dp', axis=1, tiled=True)  49.3 us
    all_gather x1, blocking collectives, local(): lax.all_gather(local_weights[1], 'dp', axis=1, tiled=True)  42.5 us
    dot_general x4, matrix products, attend_back(): jnp.einsum('qhe,khe->hqk', grad_out, values, preferred_element_type=jnp.f...  33.4 us
  transfers between devices with their start and end apart: 21, of which 16 were waited for; matrix products, arithmetic and copies ran while one was open for 19% of the time, Pallas kernels for 0%

commit v1 on v0

v1 whole, which is shorter than its diff:
```python
import functools

import jax
import jax.numpy as jnp
from jax import lax
from jax.experimental import pallas as pl
from jax.experimental.pallas import tpu as pltpu
from jax.sharding import PartitionSpec as P

HEAD_DIM = 64
LANES = 128
QB = 256
TB = 256
VMEM = 56 << 20
THETA = 160000.0
EPS = 1e-05
BF = jnp.bfloat16
F32 = jnp.float32

ORDER_A = (0, 4, 8, 12, 1, 5, 9, 13, 2, 6, 10, 14, 3, 7, 11, 15)
ORDER_B = (0, 4, 8, 12, 2, 6, 10, 14, 1, 5, 9, 13, 3, 7, 11, 15)


def nn(a, b):
    return lax.dot_general(a, b, (((1,), (0,)), ((), ())), preferred_element_type=F32)


def nt(a, b):
    return lax.dot_general(a, b, (((1,), (1,)), ((), ())), preferred_element_type=F32)


def tn(a, b):
    return lax.dot_general(a, b, (((0,), (0,)), ((), ())), preferred_element_type=F32)


def up_to(n):
    return -(-n // LANES) * LANES


def rotate(u, cos, sin, sign):
    lane = lax.broadcasted_iota(jnp.int32, u.shape, 1)
    half = HEAD_DIM // 2
    partner = jnp.where(
        (lane % HEAD_DIM) < half, pltpu.roll(u, LANES - half, 1), pltpu.roll(u, half, 1)
    )
    return u * cos + partner * sin if sign > 0 else u * cos - partner * sin


def norm(x):
    center = x - jnp.mean(x, axis=-1, keepdims=True)
    inverse = lax.rsqrt(jnp.mean(center * center, axis=-1, keepdims=True) + EPS)
    return center * inverse, inverse


def norm_back(grad, xhat, inverse, gain):
    z = grad * gain
    inner = z - jnp.mean(z, axis=-1, keepdims=True) - xhat * jnp.mean(z * xhat, axis=-1, keepdims=True)
    return inverse * inner


def staged(count, stages):
    live = [None] * len(stages)
    for step in range(count + len(stages) - 1):
        new = [None] * len(stages)
        for s, stage in enumerate(stages):
            if 0 <= step - s < count:
                new[s] = stage(step - s, live[s - 1] if s else None)
        live = new


def call(kernel, name, grid, in_specs, out_specs, out_shape, scratch=(), prefetch=1):
    return pl.pallas_call(
        kernel,
        grid_spec=pltpu.PrefetchScalarGridSpec(
            num_scalar_prefetch=prefetch,
            grid=grid,
            in_specs=in_specs,
            out_specs=out_specs,
            scratch_shapes=list(scratch),
        ),
        out_shape=out_shape,
        compiler_params=pltpu.CompilerParams(vmem_limit_bytes=VMEM),
        name=name,
    )


ANY = pl.BlockSpec(memory_space=pl.ANY)


def load_weights(info, pieces, layout, rows, dest, sems):
    copies = []
    for ref, (r, col, order) in zip(pieces, layout, strict=True):
        cols = pl.ds(col, ref.shape[1])
        if order is None:
            copies.append((ref, dest.at[r, :, cols]))
            continue
        for i, k in enumerate(order):
            row = pl.multiple_of((info[1] ^ k) * rows, rows)
            copies.append((ref.at[pl.ds(i * rows, rows), :], dest.at[r, pl.ds(row, rows), cols]))
    copies = [pltpu.make_async_copy(a, b, sems.at[i]) for i, (a, b) in enumerate(copies)]
    for c in copies:
        c.start()
    for c in copies:
        c.wait()


def copies_of(layout):
    return sum(1 if order is None else len(order) for _, _, order in layout)


def store_rows(info, value_ref, out_ref, cols, order, rows):
    if order is None:
        out_ref[:, cols] = value_ref[...].astype(BF)
        return
    for i, k in enumerate(order):
        row = pl.multiple_of((info[1] ^ k) * rows, rows)
        out_ref[i * rows : (i + 1) * rows, cols] = value_ref[pl.ds(row, rows), :].astype(BF)


def own_block(info, half):
    return pl.program_id(0) // half == info[0]


def qkv_kernel(info, *refs, layout, rows, width, half):
    n = len(layout)
    pieces, (x_ref, recv_ref, cos_ref, sin_ref, qkv_ref, h_ref, gain_ref, w_ref, sems) = refs[:n], refs[n:]

    @pl.when(pl.program_id(0) == 0)
    def _():
        load_weights(info, pieces, layout, rows, w_ref, sems)
        gain_ref[...] = w_ref[0, :, 3 * width :].astype(F32).T[:8]

    x = jnp.where(own_block(info, half), x_ref[...], recv_ref[...]).astype(F32)
    xhat, _ = norm(x)
    h = (xhat * gain_ref[0:1, :]).astype(BF)
    h_ref[...] = h
    cos, sin = cos_ref[...], sin_ref[...]
    for r in range(2):
        raw = nn(h, w_ref[r, :, : 3 * width])
        for b in range(2 * width // LANES):
            cols = slice(b * LANES, (b + 1) * LANES)
            u = rotate(raw[:, cols], cos, sin, 1)
            if b < width // LANES:
                u = u * HEAD_DIM**-0.5
            qkv_ref[r, :, cols] = u.astype(BF)
        qkv_ref[r, :, 2 * width :] = raw[:, 2 * width :].astype(BF)


def token_specs(d, half):
    def clip(b, first):
        return jnp.clip(b - first, 0, half - 1)

    held = pl.BlockSpec((None, TB, d), lambda b, i: (i[0], b % half, 0))
    recv = pl.BlockSpec((TB, d), lambda b, i: (b % half, 0))
    rows = pl.BlockSpec((TB, d), lambda b, i: (b, 0))
    own = pl.BlockSpec((TB, d), lambda b, i: (clip(b, half * i[0]), 0))
    other = pl.BlockSpec((TB, d), lambda b, i: (clip(b, half * (1 - i[0])), 0))
    return held, recv, rows, own, other


def qkv_call(info, pieces, layout, rows, width, x, recv, cos, sin):
    d, s = x.shape[2], cos.shape[0]
    half = s // TB // 2
    held, received, block, _, _ = token_specs(d, half)
    table = pl.BlockSpec((TB, LANES), lambda b, i: (b, 0))
    cols = 3 * width + LANES
    return call(
        functools.partial(qkv_kernel, layout=layout, rows=rows, width=width, half=half),
        "qkv",
        (s // TB,),
        [ANY] * len(layout) + [held, received, table, table],
        [
            pl.BlockSpec((2, TB, 3 * width), lambda b, i: (0, b, 0)),
            block,
            pl.BlockSpec((8, d), lambda b, i: (0, 0)),
        ],
        [
            jax.ShapeDtypeStruct((2, s, 3 * width), BF),
            jax.ShapeDtypeStruct((s, d), BF),
            jax.ShapeDtypeStruct((8, d), F32),
        ],
        [pltpu.VMEM((2, d, cols), BF), pltpu.SemaphoreType.DMA((copies_of(layout),))],
    )(info, *pieces, x, recv, cos, sin)


def same_segment(col, row):
    parts = [
        jnp.where(col == row[:, i * LANES : (i + 1) * LANES], 0.0, -1e30).astype(F32)
        for i in range(row.shape[1] // LANES)
    ]
    return jnp.concatenate(parts, 1)


def by_range(ranges, blocks, run):
    i = pl.program_id(1)
    for n in range(1, blocks + 1):

        @pl.when(ranges[i, 1] == n)
        def _(n=n):
            run(n, pl.ds(pl.multiple_of(ranges[i, 0], QB) if n < blocks else 0, n * QB))


def attend_kernel(ranges, col_ref, row_ref, q_ref, k_ref, v_ref, o_ref, lse_ref, vt_ref):
    s, width = k_ref.shape
    heads = width // HEAD_DIM

    @pl.when(pl.program_id(1) == 0)
    def _():
        vt_ref[...] = v_ref[...].T

    def run(n, keys):
        bias = same_segment(col_ref[keys, :], row_ref[0:1, :])
        outs = [None] * heads

        def lanes(h):
            return slice(h * HEAD_DIM, (h + 1) * HEAD_DIM)

        def scores(h, _):
            x = nn(k_ref[keys, lanes(h)], q_ref[:, lanes(h)].T) + bias
            return x, jnp.max(x, axis=0, keepdims=True)

        def expo(h, a):
            e = jnp.exp(a[0] - a[1])
            return e.astype(BF), jnp.sum(e, axis=0, keepdims=True), a[1]

        def out(h, a):
            outs[h] = nn(vt_ref[lanes(h), keys], a[0]) * (1.0 / a[1])
            lse_ref[h : h + 1, :] = a[2] + jnp.log(a[1])

        staged(heads, [scores, expo, out])
        o_ref[...] = jnp.concatenate(outs, axis=0).T.astype(BF)

    by_range(ranges, s // QB, run)


def attend_call(ranges, col, row, qkv):
    _, s, w3 = qkv.shape
    width = w3 // 3

    def whole(c):
        return pl.BlockSpec((None, s, width), lambda r, i, g: (r, 0, c))

    block = pl.BlockSpec((None, QB, width), lambda r, i, g: (r, i, 0))
    return call(
        attend_kernel,
        "attend",
        (2, s // QB),
        [
            pl.BlockSpec((s, LANES), lambda r, i, g: (0, 0)),
            pl.BlockSpec((8, QB), lambda r, i, g: (0, i)),
            block,
            whole(1),
            whole(2),
        ],
        [block, pl.BlockSpec((None, 8, QB), lambda r, i, g: (r, 0, i))],
        [jax.ShapeDtypeStruct((2, s, width), BF), jax.ShapeDtypeStruct((2, 8, s), F32)],
        [pltpu.VMEM((width, s), BF)],
    )(ranges, col, row, qkv, qkv, qkv)


def attend_back_kernel(
    ranges, col_ref, row_ref, q_ref, k_ref, v_ref, do_ref, o_ref, lse_ref, cos_ref, sin_ref,
    dq_ref, dkv_ref, qt_ref, dot_ref, dqt_ref, delta_ref,
):
    s, width = q_ref.shape
    heads, blocks = width // HEAD_DIM, s // QB
    c = pl.program_id(1)

    def lanes(h):
        return slice(h * HEAD_DIM, (h + 1) * HEAD_DIM)

    @pl.when(c == 0)
    def _():
        qt_ref[...] = q_ref[...].T
        dqt_ref[...] = jnp.zeros_like(dqt_ref)
        for i in range(blocks):
            at = slice(i * QB, (i + 1) * QB)
            dot = do_ref[at, :].astype(F32).T
            dot_ref[:, at] = dot.astype(BF)
            both = dot * o_ref[at, :].astype(F32).T
            for h in range(heads):
                delta_ref[h : h + 1, at] = jnp.sum(both[lanes(h)], axis=0, keepdims=True)

    def run(n, queries):
        bias = same_segment(col_ref[...], row_ref[0:1, queries])
        dks, dvs = [None] * heads, [None] * heads

        def products(h, _):
            return (
                nn(k_ref[:, lanes(h)], qt_ref[lanes(h), queries]) + bias,
                nn(v_ref[:, lanes(h)], dot_ref[lanes(h), queries]),
            )

        def scores(h, a):
            p = jnp.exp(a[0] - lse_ref[h : h + 1, queries])
            return p.astype(BF), (p * (a[1] - delta_ref[h : h + 1, queries])).astype(BF)

        def grads(h, a):
            dvs[h] = nt(dot_ref[lanes(h), queries], a[0])
            dks[h] = nt(qt_ref[lanes(h), queries], a[1])
            dqt_ref[lanes(h), queries] += nn(k_ref[:, lanes(h)].T, a[1])

        staged(heads, [products, scores, grads])
        here = pl.ds(pl.multiple_of(c * QB, QB), QB)
        cos, sin = cos_ref[here, :], sin_ref[here, :]
        for b in range(width // LANES):
            dk = jnp.concatenate(dks[2 * b : 2 * b + 2], 0).T
            dv = jnp.concatenate(dvs[2 * b : 2 * b + 2], 0).T
            dkv_ref[:, b * LANES : (b + 1) * LANES] = rotate(dk, cos, sin, -1).astype(BF)
            dkv_ref[:, width + b * LANES : width + (b + 1) * LANES] = dv.astype(BF)

    by_range(ranges, blocks, run)

    @pl.when(c == blocks - 1)
    def _():
        for i in range(blocks):
            at = slice(i * QB, (i + 1) * QB)
            for b in range(width // LANES):
                cols = slice(b * LANES, (b + 1) * LANES)
                dq = dqt_ref[cols, at].T * HEAD_DIM**-0.5
                dq_ref[at, cols] = rotate(dq, cos_ref[at, :], sin_ref[at, :], -1).astype(BF)


def attend_back_call(ranges, col, row, qkv, do, o, lse, cos, sin):
    _, s, w3 = qkv.shape
    width = w3 // 3
    whole = pl.BlockSpec((None, s, width), lambda r, c, g: (r, 0, 0))
    table = pl.BlockSpec((s, LANES), lambda r, c, g: (0, 0))

    def block(n):
        return pl.BlockSpec((None, QB, width), lambda r, c, g: (r, c, n))

    return call(
        attend_back_kernel,
        "attend_back",
        (2, s // QB),
        [
            pl.BlockSpec((QB, LANES), lambda r, c, g: (c, 0)),
            pl.BlockSpec((8, s), lambda r, c, g: (0, 0)),
            whole,
            block(1),
            block(2),
            whole,
            whole,
            pl.BlockSpec((None, 8, s), lambda r, c, g: (r, 0, 0)),
            table,
            table,
        ],
        [whole, pl.BlockSpec((None, QB, 2 * width), lambda r, c, g: (r, c, 0))],
        [jax.ShapeDtypeStruct((2, s, width), BF), jax.ShapeDtypeStruct((2, s, 2 * width), BF)],
        [
            pltpu.VMEM((width, s), BF),
            pltpu.VMEM((width, s), BF),
            pltpu.VMEM((width, s), F32),
            pltpu.VMEM((8, s), F32),
        ],
    )(ranges, col, row, qkv, qkv, qkv, do, o, lse, cos, sin)


def mlp_kernel(info, *refs, layout, rows, width, units, half):
    n = len(layout)
    (x_ref, xr_ref, dy_ref, dyr_ref, o_ref, gain_ref,
     own_ref, other_ref, dr_ref, do_ref, h_ref, dyo_ref, da_ref, dgu_ref, m_ref, gg_ref,
     w_ref, sems) = refs[n:]
    own = own_block(info, half)

    @pl.when(pl.program_id(0) == 0)
    def _():
        load_weights(info, refs[:n], layout, rows, w_ref, sems)
        gg_ref[...] = jnp.zeros_like(gg_ref)

    c0, c1, c2, c3 = width, width + units, width + 2 * units, width + 3 * units
    gain = gain_ref[1:2, :]
    x = jnp.where(own, x_ref[...], xr_ref[...]).astype(F32)
    dyb = jnp.where(own, dy_ref[...], dyr_ref[...])
    dyo_ref[...] = dyb
    dy = dyb.astype(F32)
    r1 = x + nt(o_ref[0], w_ref[0, :, :c0]) + nt(o_ref[1], w_ref[1, :, :c0])
    xhat, inverse = norm(r1)
    h = (xhat * gain).astype(BF)
    h_ref[...] = h
    out, dh = 0.0, 0.0
    for r in range(2):
        gate = nn(h, w_ref[r, :, c0:c1])
        up = nn(h, w_ref[r, :, c1:c2])
        dm = nn(dyb, w_ref[r, :, c2:c3])
        phi = 0.5 + 0.5 * lax.erf(gate * 0.7071067811865476)
        density = jnp.exp(-0.5 * gate * gate) * 0.3989422804014327
        gelu = gate * phi
        m = (gelu * up).astype(BF)
        dgate = (dm * up * (phi + gate * density)).astype(BF)
        dup = (dm * gelu).astype(BF)
        m_ref[r] = m
        dgu_ref[r, :, :units] = dgate
        dgu_ref[r, :, units:] = dup
        out = out + nt(m, w_ref[r, :, c2:c3])
        dh = dh + nt(dgate, w_ref[r, :, c0:c1]) + nt(dup, w_ref[r, :, c1:c2])
    out = (r1 + out).astype(BF)

    @pl.when(own)
    def _():
        own_ref[...] = out

    @pl.when(jnp.logical_not(own))
    def _():
        other_ref[...] = out

    gg_ref[0:1, :] += jnp.sum(dh * xhat, axis=0, keepdims=True)
    dr = dy + norm_back(dh, xhat, inverse, gain)
    dr_ref[...] = dr
    da = dr.astype(BF)
    da_ref[...] = da
    for r in range(2):
        do_ref[r] = nn(da, w_ref[r, :, :c0]).astype(BF)


def mlp_call(info, pieces, layout, rows, width, units, x, xr, dy, dyr, o, gains):
    d, s = x.shape[2], o.shape[1]
    half = s // TB // 2
    held, received, block, own, other = token_specs(d, half)

    def pair(w):
        return pl.BlockSpec((2, TB, w), lambda b, i: (0, b, 0))

    row = pl.BlockSpec((8, d), lambda b, i: (0, 0))
    return call(
        functools.partial(mlp_kernel, layout=layout, rows=rows, width=width, units=units, half=half),
        "mlp",
        (s // TB,),
        [ANY] * len(layout) + [held, received, held, received, pair(width), row],
        [own, other, block, pair(width), block, block, block, pair(2 * units), pair(units), row],
        [
            jax.ShapeDtypeStruct((s // 2, d), BF),
            jax.ShapeDtypeStruct((s // 2, d), BF),
            jax.ShapeDtypeStruct((s, d), F32),
            jax.ShapeDtypeStruct((2, s, width), BF),
            jax.ShapeDtypeStruct((s, d), BF),
            jax.ShapeDtypeStruct((s, d), BF),
            jax.ShapeDtypeStruct((s, d), BF),
            jax.ShapeDtypeStruct((2, s, 2 * units), BF),
            jax.ShapeDtypeStruct((2, s, units), BF),
            jax.ShapeDtypeStruct((8, d), F32),
        ],
        [pltpu.VMEM((2, d, width + 3 * units), BF), pltpu.SemaphoreType.DMA((copies_of(layout),))],
    )(info, *pieces, x, xr, dy, dyr, o, gains)


def weight_grad_kernel(info, *refs, products, orders, rows):
    n = 1 + max(max(a, b) for a, b, _ in products)
    outs, g_ref = refs[n : n + 2], refs[n + 2]
    for a, b, col in products:
        left, right = refs[a], refs[b]
        for first, out_ref, order, base in zip((0, 1), outs, orders, (0, outs[0].shape[1])):
            start, stop = max(col, base), min(col + right.shape[1], base + out_ref.shape[1])
            if start >= stop:
                continue
            value = g_ref.at[:, pl.ds(0, stop - start)]
            value[...] = tn(left[...], right[:, start - col : stop - col])
            store_rows(info, value, out_ref, slice(start - base, stop - base), order, rows)


def weight_grad_call(name, info, rows, orders, operands, products, split, total):
    specs, arrays = [], []
    for array, lead in operands:
        arrays.append(array)
        if lead is None:
            specs.append(pl.BlockSpec(array.shape, lambda g, i: (0, 0)))
        else:
            specs.append(pl.BlockSpec((None,) + array.shape[1:], lambda g, i, lead=lead: (lead, 0, 0)))
    d = operands[0][0].shape[-1]
    widest = max(a.shape[-1] for a in arrays)
    shapes = [(d, split), (d, total - split)]
    return call(
        functools.partial(weight_grad_kernel, products=products, orders=orders, rows=rows),
        name,
        (1,),
        specs,
        [pl.BlockSpec(shape, lambda g, i: (0, 0)) for shape in shapes],
        [jax.ShapeDtypeStruct(shape, BF) for shape in shapes],
        [pltpu.VMEM((d, widest), F32)],
    )(info, *arrays)


def input_kernel(info, *refs, layout, rows, width, half, order):
    n = len(layout)
    (x_ref, xr_ref, dq_ref, dkv_ref, dr_ref, gain_ref, gg_ref,
     own_ref, other_ref, gcol_ref, w_ref, acc_ref, col_ref, sems) = refs[n:]
    own = own_block(info, half)

    @pl.when(pl.program_id(0) == 0)
    def _():
        load_weights(info, refs[:n], layout, rows, w_ref, sems)
        acc_ref[...] = jnp.zeros_like(acc_ref)
        acc_ref[1:2, :] = gg_ref[0:1, :]

    gain = gain_ref[0:1, :]
    x = jnp.where(own, x_ref[...], xr_ref[...]).astype(F32)
    xhat, inverse = norm(x)
    dh = 0.0
    for r in range(2):
        dh = dh + nt(dq_ref[r], w_ref[r, :, :width]) + nt(dkv_ref[r], w_ref[r, :, width : 3 * width])
    acc_ref[0:1, :] += jnp.sum(dh * xhat, axis=0, keepdims=True)
    grad = dr_ref[...] + norm_back(dh, xhat, inverse, gain)

    @pl.when(own)
    def _():
        own_ref[...] = grad

    @pl.when(jnp.logical_not(own))
    def _():
        other_ref[...] = grad

    @pl.when(pl.program_id(0) == pl.num_programs(0) - 1)
    def _():
        col_ref[...] = acc_ref[...].T
        store_rows(info, col_ref, gcol_ref, slice(0, LANES), order, rows)


def input_call(info, pieces, layout, rows, width, x, xr, dq, dkv, dr, gains, gg, order):
    d, s = x.shape[2], dq.shape[1]
    half = s // TB // 2
    held, received, block, own, other = token_specs(d, half)

    def pair(w):
        return pl.BlockSpec((2, TB, w), lambda b, i: (0, b, 0))

    row = pl.BlockSpec((8, d), lambda b, i: (0, 0))
    return call(
        functools.partial(input_kernel, layout=layout, rows=rows, width=width, half=half, order=order),
        "input_back",
        (s // TB,),
        [ANY] * len(layout) + [held, received, pair(width), pair(2 * width), block, row, row],
        [own, other, pl.BlockSpec((d, LANES), lambda b, i: (0, 0))],
        [
            jax.ShapeDtypeStruct((s // 2, d), F32),
            jax.ShapeDtypeStruct((s // 2, d), F32),
            jax.ShapeDtypeStruct((d, LANES), BF),
        ],
        [
            pltpu.VMEM((2, d, 3 * width + LANES), BF),
            pltpu.VMEM((LANES, d), F32),
            pltpu.VMEM((d, LANES), F32),
            pltpu.SemaphoreType.DMA((copies_of(layout),)),
        ],
    )(info, *pieces, x, xr, dq, dkv, dr, gains, gg)


def swap(x):
    return lax.ppermute(x, "tensor", [(0, 1), (1, 0)])


def peer(x, k):
    return lax.ppermute(x, "dp", [(i, i ^ k) for i in range(16)])


def gather(slab, split, cube):
    if not cube:
        whole = lax.all_gather(slab, "dp", axis=0, tiled=True)
        return [whole, swap(whole)], [(0, 0, None), (1, 0, None)]
    block = jnp.concatenate([slab] + [peer(slab, k) for k in (4, 8, 12)], 0)
    a, b = block[:, :split], block[:, split:]
    a = jnp.concatenate([a, peer(a, 1)], 0)
    b = jnp.concatenate([b, peer(b, 2)], 0)
    own = [a, b, peer(a, 2), peer(b, 1)]
    where = [
        (0, ORDER_A[:8]),
        (split, ORDER_B[:8]),
        (0, ORDER_A[8:]),
        (split, ORDER_B[8:]),
    ]
    layout = [(r, col, order) for r in range(2) for col, order in where]
    return own + [swap(p) for p in own], layout


def add(*terms):
    return functools.reduce(jnp.add, [t.astype(F32) for t in terms])


def scatter(a, b, cube):
    if not cube:
        both = jnp.concatenate([add(*a), add(*b)], 1)
        return lax.psum_scatter(both, "dp", scatter_dimension=0, tiled=True)
    n = a[0].shape[0] // 2
    ra = peer(add(*(t[n:] for t in a)).astype(BF), 2)
    rb = peer(add(*(t[n:] for t in b)).astype(BF), 1)
    a, b = [t[:n] for t in a] + [ra], [t[:n] for t in b] + [rb]
    n = n // 2
    ra = peer(add(*(t[n:] for t in a)).astype(BF), 1)
    rb = peer(add(*(t[n:] for t in b)).astype(BF), 2)
    both = jnp.concatenate([add(*(t[:n] for t in a), ra[:n]), add(*(t[:n] for t in b), rb[:n])], 1)
    n = n // 4
    send = both.astype(BF)
    got = [peer(send[i * n : (i + 1) * n], 4 * i) for i in (1, 2, 3)]
    return add(both[:n], *got)


def local(
    hidden_in, segment_ids, qkv_weight, out_weight, mlp_weight, down_weight, attn_gain, mlp_gain,
    cotangent, *, cube,
):
    t, me = lax.axis_index("tensor"), lax.axis_index("dp")
    info = jnp.stack([t, me]).astype(jnp.int32)
    rows, width = qkv_weight.shape[1:]
    d = hidden_in.shape[2]
    units_here = mlp_weight.shape[2]
    units = up_to(units_here)
    s = segment_ids.shape[1]

    def other_half(x):
        return swap(lax.dynamic_index_in_dim(x, 1 - t, 0, False))

    def placed(own, got):
        first = t == 0
        return jnp.stack([jnp.where(first, own, got), jnp.where(first, got, own)])

    x_recv = other_half(hidden_in)
    gain_cols = jnp.stack([attn_gain, mlp_gain], 1)
    gain_cols = jnp.pad(gain_cols, ((0, 0), (0, LANES - 2)))
    slab1 = jnp.concatenate([qkv_weight[0], qkv_weight[1], qkv_weight[2], gain_cols], 1)

    def wide(w):
        return jnp.pad(w, ((0, 0), (0, units - units_here)))

    slab2 = jnp.concatenate(
        [out_weight.T, wide(mlp_weight[0]), wide(mlp_weight[1]), wide(down_weight.T)], 1
    )
    total1, total2 = slab1.shape[1], slab2.shape[1]
    split1, split2 = total1 // 2 // LANES * LANES, total2 // 2 // LANES * LANES
    w1, layout1 = gather(slab1, split1, cube)
    w2, layout2 = gather(slab2, split2, cube)
    dy_recv = other_half(cotangent)

    seg = lax.dynamic_index_in_dim(segment_ids, t, 0, False)
    index = jnp.arange(s, dtype=jnp.int32)
    start = jnp.sum((seg[None, :] < seg[:, None]).astype(jnp.int32), axis=1)
    freqs = THETA ** (-2.0 * jnp.arange(HEAD_DIM // 2, dtype=F32) / HEAD_DIM)
    angles = (index - start).astype(F32)[:, None] * freqs[None, :]
    cos, sin = jnp.cos(angles), jnp.sin(angles)
    cos = jnp.concatenate([cos, cos, cos, cos], 1)
    sin = jnp.concatenate([-sin, sin, -sin, sin], 1)
    col = jnp.broadcast_to(seg[:, None], (s, LANES))
    row = jnp.broadcast_to(seg[None, :], (8, s))
    ends = seg.reshape(s // QB, QB)
    first, last = ends[:, 0], ends[:, -1]
    meet = (first[:, None] <= last[None, :]) & (first[None, :] <= last[:, None])
    block = jnp.arange(s // QB, dtype=jnp.int32)[None, :]
    low = jnp.min(jnp.where(meet, block, s), axis=1)
    high = jnp.max(jnp.where(meet, block, -1), axis=1)
    ranges = jnp.stack([low * QB, high - low + 1], 1).astype(jnp.int32)

    qkv, h1, gains = qkv_call(info, w1, layout1, rows, width, hidden_in, x_recv, cos, sin)
    o, lse = attend_call(ranges, col, row, qkv)
    out_own, out_other, dr, do, h2, dy, da, dgu, m, gg = mlp_call(
        info, w2, layout2, rows, width, units, hidden_in, x_recv, cotangent, dy_recv, o, gains
    )
    layer_out = placed(out_own, swap(out_other))

    orders = (ORDER_A, ORDER_B) if cube else (None, None)

    def grads2(r):
        return weight_grad_call(
            "mlp_weight_grad", info, rows, orders,
            [(da, None), (h2, None), (dy, None), (o, r), (dgu, r), (m, r)],
            [(0, 3, 0), (1, 4, width), (2, 5, width + 2 * units)], split2, total2,
        )

    theirs = [swap(g) for g in grads2(1)]
    mine = grads2(0)
    sum2 = scatter((mine[0], theirs[0]), (mine[1], theirs[1]), cube)

    dq, dkv = attend_back_call(ranges, col, row, qkv, do, o, lse, cos, sin)

    def grads1(r):
        return weight_grad_call(
            "qkv_weight_grad", info, rows, orders,
            [(h1, None), (dq, r), (dkv, r)],
            [(0, 1, 0), (0, 2, width)], split1, total1 - LANES,
        )

    theirs = [swap(g) for g in grads1(1)]
    mine = grads1(0)
    in_own, in_other, gcol = input_call(
        info, w1, layout1, rows, width, hidden_in, x_recv, dq, dkv, dr, gains, gg, orders[1]
    )
    input_grad = placed(in_own, swap(in_other))
    gcol_got = swap(gcol)
    sum1 = scatter(
        (mine[0], theirs[0]),
        (
            jnp.concatenate([mine[1], gcol], 1),
            jnp.concatenate([theirs[1], gcol_got], 1),
        ),
        cube,
    )
    qkv_grad = sum1[:, : 3 * width].reshape(rows, 3, width).transpose(1, 0, 2)
    c = width
    proj_grad = sum2[:, :c].T
    mlp_grad = jnp.stack([sum2[:, c : c + units_here], sum2[:, c + units : c + units + units_here]])
    down_grad = sum2[:, c + 2 * units : c + 2 * units + units_here].T
    return (
        layer_out,
        input_grad,
        qkv_grad,
        proj_grad,
        mlp_grad,
        down_grad,
        sum1[:, 3 * width],
        sum1[:, 3 * width + 1],
    )


def solution(mesh):
    rows = P(None, ("dp", "tensor"), None)
    in_specs = (
        rows,
        P(None, "dp"),
        P(None, "dp", "tensor"),
        P("tensor", "dp"),
        P(None, "dp", "tensor"),
        P("tensor", "dp"),
        P("dp"),
        P("dp"),
        rows,
    )
    out_specs = (
        rows,
        rows,
        P(None, "dp", "tensor"),
        P("tensor", "dp"),
        P(None, "dp", "tensor"),
        P("tensor", "dp"),
        P("dp"),
        P("dp"),
    )
    cube = mesh.shape["dp"] == 16
    return jax.shard_map(
        functools.partial(local, cube=cube), mesh=mesh, in_specs=in_specs, out_specs=out_specs, check_vma=False
    )
```

time: 1240 us -> 342 us (0.28)
  waiting for transfers between devices: 585 us -> 98.9 us
  matrix products: 206 us -> 0 us
  blocking collectives: 184 us -> 0 us
  Pallas kernels: 0 us -> 147 us
  local copies, waits for them, and re-layouts: 126 us -> 18.4 us
  other arithmetic: 102 us -> 17.1 us
  starting transfers between devices: 1.03 us -> 53.2 us
  between operations: 17.1 us -> 1.53 us
    reduce_scatter x10 -> x0, waiting for transfers between devices: 298 us -> none  [the longest x1 128 us: local(): lax.psum_scatter(totals[1], 'dp', scatter_dimension=1, tiled=True)]
    dot_general x52 -> x0, matrix products: 206 us -> none  [the longest x4 33.4 us: attend_back(): jnp.einsum('qhe,khe->hqk', grad_out, values, preferred_element_type=jnp.f...]
    unnamed x22 -> x0, waiting for transfers between devices: 200 us -> none
    pallas_call x0 -> x9, Pallas kernels: none -> 147 us  [the longest x1 36.1 us: attend_back_call(): call(attend_back_kernel, 'attend_back', (2, s // QB), [pl.BlockSpec((QB,...]
    ppermute x0 -> x45, waiting for transfers between devices: none -> 98.9 us  [the longest x28 98.8 us: peer(): return lax.ppermute(x, 'dp', [(i, i ^ k) for i in range(16)])]
    all_gather x2 -> x0, blocking collectives: 91.8 us -> none  [the longest x1 49.3 us: local(): lax.all_gather(local_weights[3], 'dp', axis=1, tiled=True)]
    unnamed x2 -> x0, blocking collectives: 89.4 us -> none
    all_gather x10 -> x0, waiting for transfers between devices: 87.2 us -> none  [the longest x1 21.9 us: local(): lax.all_gather(local_weights[0], 'dp', axis=1, tiled=True)]
  transfers between devices with their start and end apart: 21 -> 45, of which waited for: 16 -> 15; matrix products, arithmetic and copies ran while one was open for 19% -> 8% of each run, Pallas kernels for 0% -> 22%
where the time goes in v1:
time: 342 us; the launch traced here: 336 us
  Pallas kernels  147 us (43%)
  waiting for transfers between devices  98.9 us (29%)
  starting transfers between devices  53.2 us (16%)
  local copies, waits for them, and re-layouts  18.4 us (5%)
  other arithmetic  17.1 us (5%)
    ppermute x28, waiting for transfers between devices, peer(): return lax.ppermute(x, 'dp', [(i, i ^ k) for i in range(16)])  98.8 us
    ppermute x28, starting transfers between devices, peer(): return lax.ppermute(x, 'dp', [(i, i ^ k) for i in range(16)])  36.9 us
    pallas_call x1, Pallas kernels, attend_back_call(): call(attend_back_kernel, 'attend_back', (2, s // QB), [pl.BlockSpec((QB,...  36.1 us
    pallas_call x4, Pallas kernels, weight_grad_call(): call(functools.partial(weight_grad_kernel, products=products, orders=orde...  32.4 us
    pallas_call x1, Pallas kernels, mlp_call(): call(functools.partial(mlp_kernel, layout=layout, rows=rows, width=width,...  32.1 us
    pallas_call x1, Pallas kernels, attend_call(): call(attend_kernel, 'attend', (2, s // QB), [pl.BlockSpec((s, LANES), lam...  20.7 us
    ppermute x17, starting transfers between devices, swap(): return lax.ppermute(x, 'tensor', [(0, 1), (1, 0)])  16.3 us
    pallas_call x1, Pallas kernels, input_call(): call(functools.partial(input_kernel, layout=layout, rows=rows, width=widt...  13.7 us
  transfers between devices with their start and end apart: 45, of which 15 were waited for; matrix products, arithmetic and copies ran while one was open for 8% of the time, Pallas kernels for 22%

profile of v1, /device:TPU:0, one launch (start us, length us, event | category | flops | bytes accessed | tf_op | source)
XLA Modules:
  0.0 336.5 jit_solution(912557723151144883)
XLA Ops:
  0.6 0.7 pad_maximum_fusion.15
  1.4 0.8 slice_bitcast_fusion.8
  2.3 5.1 %collective-permute-start.15 = (bf16[48,1280]{1,0:T(8,128)(2,1)S(1)}, bf16[48,1280]{1,0:T(8,128)(2,1)S(1)}, u32[]{:S(2)}, u32[]{:S(2)}) collective-permute-start(bf16[48,1280]{1,0:T(8,128)(2,1)S(1)} %pad_maximum_fusion.14), channel_id=1, source_target_pairs={{0,24},{2,26},{4,28},{6,30},{8,16},{10,18},{12,20},{14,22},{16,8},... | collective-permute-start | bytes 368648 | tf_op jit(solution)/shard_map/ppermute | solution.py:553
  8.0 0.8 pad.16
  8.9 0.9 slice_bitcast_fusion.5
  9.8 0.8 pad_maximum_fusion.13
  10.6 3.8 %collective-permute-start.2 = (bf16[48,2304]{1,0:T(8,128)(2,1)S(1)}, bf16[48,2304]{1,0:T(8,128)(2,1)S(1)}, u32[]{:S(2)}, u32[]{:S(2)}) collective-permute-start(bf16[48,2304]{1,0:T(8,128)(2,1)S(1)} %pad_maximum_fusion.13), channel_id=1, source_target_pairs={{0,24},{2,26},{4,28},{6,30},{8,16},{10,18},{12,20},{14,22},{16,8},... | collective-permute-start | bytes 663560 | tf_op jit(solution)/shard_map/ppermute | solution.py:553
  14.4 3.1 collective-permute-start
  17.5 10.7 %collective-permute-done.14 = bf16[48,1280]{1,0:T(8,128)(2,1)S(1)} collective-permute-done((bf16[48,1280]{1,0:T(8,128)(2,1)S(1)}, bf16[48,1280]{1,0:T(8,128)(2,1)S(1)}, u32[]{:S(2)}, u32[]{:S(2)}) %collective-permute-start.14) | collective-permute-done | bytes 122912 | tf_op jit(solution)/shard_map/ppermute | solution.py:553
  28.3 1.6 collective-permute-start.16
  29.9 6.8 %collective-permute-done.1 = bf16[48,2304]{1,0:T(8,128)(2,1)S(1)} collective-permute-done((bf16[48,2304]{1,0:T(8,128)(2,1)S(1)}, bf16[48,2304]{1,0:T(8,128)(2,1)S(1)}, u32[]{:S(2)}, u32[]{:S(2)}) %collective-permute-start.1) | collective-permute-done | bytes 221216 | tf_op jit(solution)/shard_map/ppermute | solution.py:553
  36.9 1.6 collective-permute-start.3
  38.5 1.5 collective-permute-start.17
  40.0 0.9 dynamic-slice_bitcast_fusion.1
  41.4 1.0 pad_maximum_fusion.10.refs_0_
  42.7 3.7 %collective-permute-done.17 = bf16[192,640]{1,0:T(8,128)(2,1)} collective-permute-done((bf16[192,640]{1,0:T(8,128)(2,1)S(1)}, bf16[192,640]{1,0:T(8,128)(2,1)}, u32[]{:S(2)}, u32[]{:S(2)}) %collective-permute-start.17) | collective-permute-done | bytes 245792 | tf_op jit(solution)/shard_map/ppermute | solution.py:553
  46.4 2.6 collective-permute-start.18
  49.0 1.1 pad_maximum_fusion.11.refs_1_
  50.7 1.1 pad_maximum_fusion.5.refs_0_
  51.8 4.0 %collective-permute-done.4 = bf16[192,1152]{1,0:T(8,128)(2,1)S(1)} collective-permute-done((bf16[192,1152]{1,0:T(8,128)(2,1)S(1)}, bf16[192,1152]{1,0:T(8,128)(2,1)S(1)}, u32[]{:S(2)}, u32[]{:S(2)}) %collective-permute-start.4) | collective-permute-done | bytes 442400 | tf_op jit(solution)/shard_map/ppermute | solution.py:553
  55.9 2.5 collective-permute-start.5
  59.6 1.4 fusion.11
  61.5 4.9 %collective-permute-done.18.refs_2_ = bf16[384,640]{1,0:T(8,128)(2,1)} collective-permute-done((bf16[384,640]{1,0:T(8,128)(2,1)S(1)}, bf16[384,640]{1,0:T(8,128)(2,1)}, u32[]{:S(2)}, u32[]{:S(2)}) %collective-permute-start.18) | collective-permute-done | bytes 491552 | tf_op jit(solution)/shard_map/ppermute | solution.py:553
  67.8 2.1 dynamic-slice_bitcast_fusion
  70.4 13.9 %collective-permute-done.5.refs_2_ = bf16[384,1152]{1,0:T(8,128)(2,1)} collective-permute-done((bf16[384,1152]{1,0:T(8,128)(2,1)S(1)}, bf16[384,1152]{1,0:T(8,128)(2,1)}, u32[]{:S(2)}, u32[]{:S(2)}) %collective-permute-start.5) | collective-permute-done | bytes 884768 | tf_op jit(solution)/shard_map/ppermute | solution.py:553
  84.8 0.7 pad_add_fusion.1.info
  86.0 1.9 fusion.10
  87.9 1.9 pad_maximum_fusion.7
  89.8 12.4 %qkv.1 = (bf16[2,1024,1152]{2,1,0:T(8,128)(2,1)}, bf16[1024,768]{1,0:T(8,128)(2,1)}, f32[8,768]{1,0:T(8,128)}) custom-call(s32[2]{0:T(128)} %pad_add_fusion.1.info, bf16[384,640]{1,0:T(8,128)(2,1)} %copy-done.2, bf16[384,640]{1,0:T(8,128)(2,1)} %copy-done.3, bf16[384,640]{1,0:T(8,128)(2,1)} %collective-permute-done.18.refs_2_, ...), custom_call_target="tpu_custom_call" | custom-call | tf_op jit(solution)/shard_map/qkv/pallas_call | solution.py:167
  102.8 1.0 broadcast_in_dim.44.col_ref
  103.8 20.7 %attend.1 = (bf16[2,1024,384]{2,1,0:T(8,128)(2,1)}, f32[2,8,1024]{2,1,0:T(8,128)}) custom-call(s32[4,2]{1,0:T(4,128)} %pad_add_fusion.ranges, s32[1024,128]{1,0:T(8,128)} %broadcast_in_dim.44.col_ref, s32[8,1024]{1,0:T(8,128)} %broadcast_in_dim.45.row_ref, bf16[2,1024,1152]{2,1,0:T(8,128)(2,1)} %get-tuple-element.36.q_ref.k_ref.v_ref, ...), custom_call_target="tpu_custom_call" | custom-call | tf_op jit(solution)/shard_map/attend/pallas_call | solution.py:244
  124.6 0.8 copy-done.18
  126.6 32.1 %mlp.1 = (bf16[512,768]{1,0:T(8,128)(2,1)}, bf16[512,768]{1,0:T(8,128)(2,1)}, f32[1024,768]{1,0:T(8,128)}, bf16[2,1024,384]{2,1,0:T(8,128)(2,1)}, bf16[1024,768]...) custom-call(s32[2]{0:T(128)} %pad_add_fusion.1.info, ...), custom_call_target="tpu_custom_call" | custom-call | tf_op jit(solution)/shard_map/mlp/pallas_call | solution.py:426
  158.7 36.1 %attend_back.1 = (bf16[2,1024,384]{2,1,0:T(8,128)(2,1)}, bf16[2,1024,768]{2,1,0:T(8,128)(2,1)}) custom-call(s32[4,2]{1,0:T(4,128)} %pad_add_fusion.ranges, s32[1024,128]{1,0:T(8,128)} %broadcast_in_dim.44.col_ref, s32[8,1024]{1,0:T(8,128)} %broadcast_in_dim.45.row_ref, bf16[2,1024,1152]{2,1,0:T(8,128)(2,1)} %get-tuple-element.36.q_ref.k_ref.v_ref, ...), custom_call_target="tpu_custom_call" | custom-call | tf_op jit(solution)/shard_map/attend_back/pallas_call | solution.py:333
  194.8 6.1 %qkv_weight_grad.3 = (bf16[768,640]{1,0:T(8,128)(2,1)}, bf16[768,512]{1,0:T(8,128)(2,1)}) custom-call(s32[2]{0:T(128)} %pad_add_fusion.1.info, bf16[1024,768]{1,0:T(8,128)(2,1)} %get-tuple-element.49.refs_0_, bf16[2,1024,384]{2,1,0:T(8,128)(2,1)} %get-tuple-element.43.refs_10_.refs_1_, bf16[2,1024,768]{2,1,0:T(8,128)(2,1)} %get-tuple-element.44.refs_11_.refs_2_), custom_call_target="tpu_custom_call" | custom-call | tf_op jit(solution)/shard_map/qkv_weight_grad/pallas_call | solution.py:473
  200.9 12.9 %collective-permute-start.29 = (bf16[768,512]{1,0:T(8,128)(2,1)}, bf16[768,512]{1,0:T(8,128)(2,1)S(1)}, u32[]{:S(2)}, u32[]{:S(2)}) collective-permute-start(bf16[768,512]{1,0:T(8,128)(2,1)} %get-tuple-element.54), channel_id=1, source_target_pairs={{0,1},{1,0},{2,3},{3,2},{4,5},{5,4},{6,7},{7,6},{8,9},{9,8},{10,11... | collective-permute-start | bytes 2359304 | tf_op jit(solution)/shard_map/ppermute | solution.py:549
  213.8 6.1 %qkv_weight_grad.2 = (bf16[768,640]{1,0:T(8,128)(2,1)}, bf16[768,512]{1,0:T(8,128)(2,1)}) custom-call(s32[2]{0:T(128)} %pad_add_fusion.1.info, bf16[1024,768]{1,0:T(8,128)(2,1)} %get-tuple-element.49.refs_0_, bf16[2,1024,384]{2,1,0:T(8,128)(2,1)} %get-tuple-element.43.refs_10_.refs_1_, bf16[2,1024,768]{2,1,0:T(8,128)(2,1)} %get-tuple-element.44.refs_11_.refs_2_), custom_call_target="tpu_custom_call" | custom-call | tf_op jit(solution)/shard_map/qkv_weight_grad/pallas_call | solution.py:473
  219.9 10.1 %mlp_weight_grad.3 = (bf16[768,1152]{1,0:T(8,128)(2,1)}, bf16[768,1152]{1,0:T(8,128)(2,1)}) custom-call(s32[2]{0:T(128)} %pad_add_fusion.1.info, bf16[1024,768]{1,0:T(8,128)(2,1)} %get-tuple-element.55.refs_0_, bf16[1024,768]{1,0:T(8,128)(2,1)} %get-tuple-element.56.refs_1_, bf16[1024,768]{1,0:T(8,128)(2,1)} %get-tuple-element.57.refs_2_, ...), custom_call_target="tpu_custom_call" | custom-call | tf_op jit(solution)/shard_map/mlp_weight_grad/pallas_call | solution.py:473
  230.0 10.1 %mlp_weight_grad.2 = (bf16[768,1152]{1,0:T(8,128)(2,1)}, bf16[768,1152]{1,0:T(8,128)(2,1)}) custom-call(s32[2]{0:T(128)} %pad_add_fusion.1.info, bf16[1024,768]{1,0:T(8,128)(2,1)} %get-tuple-element.55.refs_0_, bf16[1024,768]{1,0:T(8,128)(2,1)} %get-tuple-element.56.refs_1_, bf16[1024,768]{1,0:T(8,128)(2,1)} %get-tuple-element.57.refs_2_, ...), custom_call_target="tpu_custom_call" | custom-call | tf_op jit(solution)/shard_map/mlp_weight_grad/pallas_call | solution.py:473
  240.1 13.7 %input_back.1 = (f32[512,768]{1,0:T(8,128)}, f32[512,768]{1,0:T(8,128)}, bf16[768,128]{1,0:T(8,128)(2,1)}) custom-call(s32[2]{0:T(128)} %pad_add_fusion.1.info, bf16[384,640]{1,0:T(8,128)(2,1)} %copy-done.2, bf16[384,640]{1,0:T(8,128)(2,1)} %copy-done.3, bf16[384,640]{1,0:T(8,128)(2,1)} %collective-permute-done.18.refs_2_, ...), custom_call_target="tpu_custom_call" | custom-call | tf_op jit(solution)/shard_map/input_back/pallas_call | solution.py:528
  255.0 1.1 constant_dynamic-update-slice_fusion
  257.8 1.3 pad_maximum_fusion.2
  259.0 11.4 %collective-permute-done.31 = bf16[384,640]{1,0:T(8,128)(2,1)S(1)} collective-permute-done((bf16[384,640]{1,0:T(8,128)(2,1)S(1)}, bf16[384,640]{1,0:T(8,128)(2,1)S(1)}, u32[]{:S(2)}, u32[]{:S(2)}) %collective-permute-start.31) | collective-permute-done | bytes 491552 | tf_op jit(solution)/shard_map/ppermute | solution.py:553
  270.9 1.7 collective-permute-start.28
  272.6 5.4 %collective-permute-done.32 = bf16[192,640]{1,0:T(8,128)(2,1)S(1)} collective-permute-done((bf16[192,640]{1,0:T(8,128)(2,1)S(1)}, bf16[192,640]{1,0:T(8,128)(2,1)S(1)}, u32[]{:S(2)}, u32[]{:S(2)}) %collective-permute-start.32) | collective-permute-done | bytes 245792 | tf_op jit(solution)/shard_map/ppermute | solution.py:553
  278.3 1.9 pad_maximum_fusion
  280.4 1.3 copy-done.10
  282.5 0.7 collective-permute-start.40
  283.3 3.3 collective-permute-start.35
  287.0 15.0 %collective-permute-done.37 = bf16[384,1152]{1,0:T(8,128)(2,1)S(1)} collective-permute-done((bf16[384,1152]{1,0:T(8,128)(2,1)S(1)}, bf16[384,1152]{1,0:T(8,128)(2,1)S(1)}, u32[]{:S(2)}, u32[]{:S(2)}) %collective-permute-start.37) | collective-permute-done | bytes 884768 | tf_op jit(solution)/shard_map/ppermute | solution.py:553
  302.2 1.0 collective-permute-start.38
  303.4 1.5 collective-permute-start.41
  305.0 7.2 %collective-permute-done.38 = bf16[192,1152]{1,0:T(8,128)(2,1)S(1)} collective-permute-done((bf16[192,1152]{1,0:T(8,128)(2,1)S(1)}, bf16[192,1152]{1,0:T(8,128)(2,1)S(1)}, u32[]{:S(2)}, u32[]{:S(2)}) %collective-permute-start.38) | collective-permute-done | bytes 442400 | tf_op jit(solution)/shard_map/ppermute | solution.py:553
  312.4 0.9 collective-permute-done.41
  313.6 0.8 fusion.12
  314.4 1.8 collective-permute-start.44
  316.2 1.6 collective-permute-start.43
  318.1 0.7 copy.44
  318.8 0.7 slice_reduce_fusion
  319.5 3.8 %collective-permute-done.42 = bf16[48,2304]{1,0:T(8,128)(2,1)S(1)} collective-permute-done((bf16[48,2304]{1,0:T(8,128)(2,1)}, bf16[48,2304]{1,0:T(8,128)(2,1)S(1)}, u32[]{:S(2)}, u32[]{:S(2)}) %collective-permute-start.42) | collective-permute-done | bytes 221216 | tf_op jit(solution)/shard_map/ppermute | solution.py:553
  323.3 3.3 collective-permute-done.44
  326.6 7.5 %collective-permute-done.43 = bf16[48,2304]{1,0:T(8,128)(2,1)S(1)} collective-permute-done((bf16[48,2304]{1,0:T(8,128)(2,1)S(1)}, bf16[48,2304]{1,0:T(8,128)(2,1)S(1)}, u32[]{:S(2)}, u32[]{:S(2)}) %collective-permute-start.43) | collective-permute-done | bytes 221216 | tf_op jit(solution)/shard_map/ppermute | solution.py:553
  334.8 0.7 slice_bitcast_fusion
  335.5 0.7 pad_maximum_fusion.12
  (155 shorter events, 15.7 us)
Async XLA Ops:
  1.3 35.4 %copy-start.21 = (bf16[384,48]{0,1:T(8,128)(2,1)S(1)}, bf16[384,48]{0,1:T(8,128)(2,1)}, u32[]{:S(2)}) copy-start(bf16[384,48]{0,1:T(8,128)(2,1)} %param.12) | copy-start | bytes 110596
  2.3 12.1 %collective-permute-start.15 = (bf16[48,1280]{1,0:T(8,128)(2,1)S(1)}, bf16[48,1280]{1,0:T(8,128)(2,1)S(1)}, u32[]{:S(2)}, u32[]{:S(2)}) collective-permute-start(bf16[48,1280]{1,0:T(8,128)(2,1)S(1)} %pad_maximum_fusion.14), channel_id=1, source_target_pairs={{0,24},{2,26},{4,28},{6,30},{8,16},{10,18},{12,20},{14,22},{16,8},... | collective-permute-start | bytes 368648 | tf_op jit(solution)/shard_map/ppermute | solution.py:553
  7.4 20.8 %collective-permute-start.14 = (bf16[48,1280]{1,0:T(8,128)(2,1)S(1)}, bf16[48,1280]{1,0:T(8,128)(2,1)S(1)}, u32[]{:S(2)}, u32[]{:S(2)}) collective-permute-start(bf16[48,1280]{1,0:T(8,128)(2,1)S(1)} %pad_maximum_fusion.14), channel_id=1, source_target_pairs={{0,16},{2,18},{4,20},{6,22},{8,24},{10,26},{12,28},{14,30},{16,0},... | collective-permute-start | bytes 368648 | tf_op jit(solution)/shard_map/ppermute | solution.py:553
  7.4 20.8 %collective-permute-start.13 = (bf16[48,1280]{1,0:T(8,128)(2,1)S(1)}, bf16[48,1280]{1,0:T(8,128)(2,1)S(1)}, u32[]{:S(2)}, u32[]{:S(2)}) collective-permute-start(bf16[48,1280]{1,0:T(8,128)(2,1)S(1)} %pad_maximum_fusion.14), channel_id=1, source_target_pairs={{0,8},{2,10},{4,12},{6,14},{8,0},{10,2},{12,4},{14,6},{16,24},{18,... | collective-permute-start | bytes 368648 | tf_op jit(solution)/shard_map/ppermute | solution.py:553
  10.6 19.3 %collective-permute-start.2 = (bf16[48,2304]{1,0:T(8,128)(2,1)S(1)}, bf16[48,2304]{1,0:T(8,128)(2,1)S(1)}, u32[]{:S(2)}, u32[]{:S(2)}) collective-permute-start(bf16[48,2304]{1,0:T(8,128)(2,1)S(1)} %pad_maximum_fusion.13), channel_id=1, source_target_pairs={{0,24},{2,26},{4,28},{6,30},{8,16},{10,18},{12,20},{14,22},{16,8},... | collective-permute-start | bytes 663560 | tf_op jit(solution)/shard_map/ppermute | solution.py:553
  14.4 22.3 %collective-permute-start.1 = (bf16[48,2304]{1,0:T(8,128)(2,1)S(1)}, bf16[48,2304]{1,0:T(8,128)(2,1)S(1)}, u32[]{:S(2)}, u32[]{:S(2)}) collective-permute-start(bf16[48,2304]{1,0:T(8,128)(2,1)S(1)} %pad_maximum_fusion.13), channel_id=1, source_target_pairs={{0,16},{2,18},{4,20},{6,22},{8,24},{10,26},{12,28},{14,30},{16,0},... | collective-permute-start | bytes 663560 | tf_op jit(solution)/shard_map/ppermute | solution.py:553
  14.4 22.3 %collective-permute-start = (bf16[48,2304]{1,0:T(8,128)(2,1)S(1)}, bf16[48,2304]{1,0:T(8,128)(2,1)S(1)}, u32[]{:S(2)}, u32[]{:S(2)}) collective-permute-start(bf16[48,2304]{1,0:T(8,128)(2,1)S(1)} %pad_maximum_fusion.13), channel_id=1, source_target_pairs={{0,8},{2,10},{4,12},{6,14},{8,0},{10,2},{12,4},{14,6},{16,24},{18,... | collective-permute-start | bytes 663560 | tf_op jit(solution)/shard_map/ppermute | solution.py:553
  28.3 10.1 %copy-start.13 = (bf16[192,640]{1,0:T(8,128)(2,1)}, bf16[192,640]{1,0:T(8,128)(2,1)S(1)}, u32[]{:S(2)}) copy-start(bf16[192,640]{1,0:T(8,128)(2,1)S(1)} %get-tuple-element.124) | copy-start | bytes 737284
  28.3 11.7 %copy-start = (bf16[2,512,768]{2,1,0:T(8,128)(2,1)S(1)}, bf16[2,512,768]{2,1,0:T(8,128)(2,1)}, u32[]{:S(2)}) copy-start(bf16[2,512,768]{2,1,0:T(8,128)(2,1)} %refs_8_.5) | copy-start | bytes 4718596
  28.3 13.1 %collective-permute-start.16 = (bf16[192,640]{1,0:T(8,128)(2,1)S(1)}, bf16[192,640]{1,0:T(8,128)(2,1)}, u32[]{:S(2)}, u32[]{:S(2)}) collective-permute-start(bf16[192,640]{1,0:T(8,128)(2,1)S(1)} %get-tuple-element.125), channel_id=1, source_target_pairs={{0,2},{2,0},{4,6},{6,4},{8,10},{10,8},{12,14},{14,12},{16,18},{18,... | collective-permute-start | bytes 737288 | tf_op jit(solution)/shard_map/ppermute | solution.py:553
  36.9 13.2 %copy-start.7 = (bf16[192,1152]{1,0:T(8,128)(2,1)}, bf16[192,1152]{1,0:T(8,128)(2,1)S(1)}, u32[]{:S(2)}) copy-start(bf16[192,1152]{1,0:T(8,128)(2,1)S(1)} %get-tuple-element.119) | copy-start | bytes 1327108
  36.9 13.2 %collective-permute-start.3 = (bf16[192,1152]{1,0:T(8,128)(2,1)S(1)}, bf16[192,1152]{1,0:T(8,128)(2,1)}, u32[]{:S(2)}, u32[]{:S(2)}) collective-permute-start(bf16[192,1152]{1,0:T(8,128)(2,1)S(1)} %get-tuple-element.120), channel_id=1, source_target_pairs={{0,2},{2,0},{4,6},{6,4},{8,10},{10,8},{12,14},{14,12},{16,18},{18,... | collective-permute-start | bytes 1327112 | tf_op jit(solution)/shard_map/ppermute | solution.py:553
  38.5 7.9 %collective-permute-start.17 = (bf16[192,640]{1,0:T(8,128)(2,1)S(1)}, bf16[192,640]{1,0:T(8,128)(2,1)}, u32[]{:S(2)}, u32[]{:S(2)}) collective-permute-start(bf16[192,640]{1,0:T(8,128)(2,1)S(1)} %get-tuple-element.124), channel_id=1, source_target_pairs={{0,4},{2,6},{4,0},{6,2},{8,12},{10,14},{12,8},{14,10},{16,20},{18,... | collective-permute-start | bytes 737288 | tf_op jit(solution)/shard_map/ppermute | solution.py:553
  40.9 17.5 %collective-permute-start.11 = (bf16[512,768]{1,0:T(8,128)(2,1)}, bf16[512,768]{1,0:T(8,128)(2,1)S(1)}, u32[]{:S(2)}, u32[]{:S(2)}) collective-permute-start(bf16[512,768]{1,0:T(8,128)(2,1)} %dynamic-slice_bitcast_fusion.1), channel_id=1, source_target_pairs={{0,1},{1,0},{2,3},{3,2},{4,5},{5,4},{6,7},{7,6},{8,9},{9,8},{10,11... | collective-permute-start | bytes 2359304 | tf_op jit(solution)/shard_map/ppermute | solution.py:549
  40.9 15.0 %collective-permute-start.4 = (bf16[192,1152]{1,0:T(8,128)(2,1)S(1)}, bf16[192,1152]{1,0:T(8,128)(2,1)S(1)}, u32[]{:S(2)}, u32[]{:S(2)}) collective-permute-start(bf16[192,1152]{1,0:T(8,128)(2,1)S(1)} %get-tuple-element.119), channel_id=1, source_target_pairs={{0,4},{2,6},{4,0},{6,2},{8,12},{10,14},{12,8},{14,10},{16,20},{18,... | collective-permute-start | bytes 1327112 | tf_op jit(solution)/shard_map/ppermute | solution.py:553
  42.4 16.0 %copy-start.2 = (bf16[384,640]{1,0:T(8,128)(2,1)}, bf16[384,640]{1,0:T(8,128)(2,1)S(1)}, u32[]{:S(2)}) copy-start(bf16[384,640]{1,0:T(8,128)(2,1)S(1)} %pad_maximum_fusion.10.refs_0_) | copy-start | bytes 1474564
  42.4 18.9 %collective-permute-start.20 = (bf16[384,640]{1,0:T(8,128)(2,1)S(1)}, bf16[384,640]{1,0:T(8,128)(2,1)}, u32[]{:S(2)}, u32[]{:S(2)}) collective-permute-start(bf16[384,640]{1,0:T(8,128)(2,1)S(1)} %pad_maximum_fusion.10.refs_0_), channel_id=1, source_target_pairs={{0,1},{1,0},{2,3},{3,2},{4,5},{5,4},{6,7},{7,6},{8,9},{9,8},{10,11... | collective-permute-start | bytes 1474568 | tf_op jit(solution)/shard_map/ppermute | solution.py:549
  46.4 20.0 %collective-permute-start.18 = (bf16[384,640]{1,0:T(8,128)(2,1)S(1)}, bf16[384,640]{1,0:T(8,128)(2,1)}, u32[]{:S(2)}, u32[]{:S(2)}) collective-permute-start(bf16[384,640]{1,0:T(8,128)(2,1)S(1)} %pad_maximum_fusion.10.refs_0_), channel_id=1, source_target_pairs={{0,4},{2,6},{4,0},{6,2},{8,12},{10,14},{12,8},{14,10},{16,20},{18,... | collective-permute-start | bytes 1474568 | tf_op jit(solution)/shard_map/ppermute | solution.py:553
  50.1 11.3 %copy-start.3 = (bf16[384,640]{1,0:T(8,128)(2,1)}, bf16[384,640]{1,0:T(8,128)(2,1)S(1)}, u32[]{:S(2)}) copy-start(bf16[384,640]{1,0:T(8,128)(2,1)S(1)} %pad_maximum_fusion.11.refs_1_) | copy-start | bytes 1474564
  50.1 8.2 %copy-start.8 = (bf16[192,1152]{1,0:T(8,128)(2,1)S(1)}, bf16[192,1152]{1,0:T(8,128)(2,1)}, u32[]{:S(2)}) copy-start(bf16[192,1152]{1,0:T(8,128)(2,1)} %copy-done.7) | copy-start | bytes 1327108
  50.1 16.3 %collective-permute-start.19 = (bf16[384,640]{1,0:T(8,128)(2,1)S(1)}, bf16[384,640]{1,0:T(8,128)(2,1)}, u32[]{:S(2)}, u32[]{:S(2)}) collective-permute-start(bf16[384,640]{1,0:T(8,128)(2,1)S(1)} %pad_maximum_fusion.11.refs_1_), channel_id=1, source_target_pairs={{0,2},{2,0},{4,6},{6,4},{8,10},{10,8},{12,14},{14,12},{16,18},{18,... | collective-permute-start | bytes 1474568 | tf_op jit(solution)/shard_map/ppermute | solution.py:553
  51.8 36.1 %copy-start.4 = (bf16[384,1152]{1,0:T(8,128)(2,1)}, bf16[384,1152]{1,0:T(8,128)(2,1)S(1)}, u32[]{:S(2)}) copy-start(bf16[384,1152]{1,0:T(8,128)(2,1)S(1)} %pad_maximum_fusion.5.refs_0_) | copy-start | bytes 2654212
  55.9 28.4 %collective-permute-start.5 = (bf16[384,1152]{1,0:T(8,128)(2,1)S(1)}, bf16[384,1152]{1,0:T(8,128)(2,1)}, u32[]{:S(2)}, u32[]{:S(2)}) collective-permute-start(bf16[384,1152]{1,0:T(8,128)(2,1)S(1)} %pad_maximum_fusion.5.refs_0_), channel_id=1, source_target_pairs={{0,4},{2,6},{4,0},{6,2},{8,12},{10,14},{12,8},{14,10},{16,20},{18,... | collective-permute-start | bytes 2654216 | tf_op jit(solution)/shard_map/ppermute | solution.py:553
  58.4 31.4 %copy-start.5 = (bf16[384,1152]{1,0:T(8,128)(2,1)}, bf16[384,1152]{1,0:T(8,128)(2,1)S(1)}, u32[]{:S(2)}) copy-start(bf16[384,1152]{1,0:T(8,128)(2,1)S(1)} %pad_maximum_fusion.6.refs_1_) | copy-start | bytes 2654212
  58.5 31.4 %copy-start.1 = (bf16[512,768]{1,0:T(8,128)(2,1)}, bf16[512,768]{1,0:T(8,128)(2,1)S(1)}, u32[]{:S(2)}) copy-start(bf16[512,768]{1,0:T(8,128)(2,1)S(1)} %collective-permute-done.11.refs_9_) | copy-start | bytes 2359300
  58.5 25.8 %collective-permute-start.6 = (bf16[384,1152]{1,0:T(8,128)(2,1)S(1)}, bf16[384,1152]{1,0:T(8,128)(2,1)}, u32[]{:S(2)}, u32[]{:S(2)}) collective-permute-start(bf16[384,1152]{1,0:T(8,128)(2,1)S(1)} %pad_maximum_fusion.6.refs_1_), channel_id=1, source_target_pairs={{0,2},{2,0},{4,6},{6,4},{8,10},{10,8},{12,14},{14,12},{16,18},{18,... | collective-permute-start | bytes 2654216 | tf_op jit(solution)/shard_map/ppermute | solution.py:553
  61.4 8.5 %collective-permute-start.21 = (bf16[384,640]{1,0:T(8,128)(2,1)S(1)}, bf16[384,640]{1,0:T(8,128)(2,1)}, u32[]{:S(2)}, u32[]{:S(2)}) collective-permute-start(bf16[384,640]{1,0:T(8,128)(2,1)S(1)} %pad_maximum_fusion.11.refs_1_), channel_id=1, source_target_pairs={{0,1},{1,0},{2,3},{3,2},{4,5},{5,4},{6,7},{7,6},{8,9},{9,8},{10,11... | collective-permute-start | bytes 1474568 | tf_op jit(solution)/shard_map/ppermute | solution.py:549
  66.4 3.5 %collective-permute-start.22 = (bf16[384,640]{1,0:T(8,128)(2,1)}, bf16[384,640]{1,0:T(8,128)(2,1)S(1)}, u32[]{:S(2)}, u32[]{:S(2)}) collective-permute-start(bf16[384,640]{1,0:T(8,128)(2,1)} %collective-permute-done.18.refs_2_), channel_id=1, source_target_pairs={{0,1},{1,0},{2,3},{3,2},{4,5},{5,4},{6,7},{7,6},{8,9},{9,8},{10,11... | collective-permute-start | bytes 1474568 | tf_op jit(solution)/shard_map/ppermute | solution.py:549
  66.4 19.0 %collective-permute-start.23 = (bf16[384,640]{1,0:T(8,128)(2,1)}, bf16[384,640]{1,0:T(8,128)(2,1)}, u32[]{:S(2)}, u32[]{:S(2)}) collective-permute-start(bf16[384,640]{1,0:T(8,128)(2,1)} %collective-permute-done.19.refs_3_), channel_id=1, source_target_pairs={{0,1},{1,0},{2,3},{3,2},{4,5},{5,4},{6,7},{7,6},{8,9},{9,8},{10,11... | collective-permute-start | bytes 1474568 | tf_op jit(solution)/shard_map/ppermute | solution.py:549
  69.8 54.7 %collective-permute-start.7 = (bf16[384,1152]{1,0:T(8,128)(2,1)S(1)}, bf16[384,1152]{1,0:T(8,128)(2,1)S(1)}, u32[]{:S(2)}, u32[]{:S(2)}) collective-permute-start(bf16[384,1152]{1,0:T(8,128)(2,1)S(1)} %pad_maximum_fusion.5.refs_0_), channel_id=1, source_target_pairs={{0,1},{1,0},{2,3},{3,2},{4,5},{5,4},{6,7},{7,6},{8,9},{9,8},{10,11... | collective-permute-start | bytes 2654216 | tf_op jit(solution)/shard_map/ppermute | solution.py:549
  69.9 20.0 %copy-start.6 = (bf16[384,640]{1,0:T(8,128)(2,1)}, bf16[384,640]{1,0:T(8,128)(2,1)S(1)}, u32[]{:S(2)}) copy-start(bf16[384,640]{1,0:T(8,128)(2,1)S(1)} %collective-permute-done.22.refs_6_) | copy-start | bytes 1474564
  69.9 54.7 %collective-permute-start.8 = (bf16[384,1152]{1,0:T(8,128)(2,1)S(1)}, bf16[384,1152]{1,0:T(8,128)(2,1)S(1)}, u32[]{:S(2)}, u32[]{:S(2)}) collective-permute-start(bf16[384,1152]{1,0:T(8,128)(2,1)S(1)} %pad_maximum_fusion.6.refs_1_), channel_id=1, source_target_pairs={{0,1},{1,0},{2,3},{3,2},{4,5},{5,4},{6,7},{7,6},{8,9},{9,8},{10,11... | collective-permute-start | bytes 2654216 | tf_op jit(solution)/shard_map/ppermute | solution.py:549
  84.3 40.3 %collective-permute-start.9 = (bf16[384,1152]{1,0:T(8,128)(2,1)}, bf16[384,1152]{1,0:T(8,128)(2,1)S(1)}, u32[]{:S(2)}, u32[]{:S(2)}) collective-permute-start(bf16[384,1152]{1,0:T(8,128)(2,1)} %collective-permute-done.5.refs_2_), channel_id=1, source_target_pairs={{0,1},{1,0},{2,3},{3,2},{4,5},{5,4},{6,7},{7,6},{8,9},{9,8},{10,11... | collective-permute-start | bytes 2654216 | tf_op jit(solution)/shard_map/ppermute | solution.py:549
  84.3 40.3 %collective-permute-start.10 = (bf16[384,1152]{1,0:T(8,128)(2,1)}, bf16[384,1152]{1,0:T(8,128)(2,1)S(1)}, u32[]{:S(2)}, u32[]{:S(2)}) collective-permute-start(bf16[384,1152]{1,0:T(8,128)(2,1)} %collective-permute-done.6.refs_3_), channel_id=1, source_target_pairs={{0,1},{1,0},{2,3},{3,2},{4,5},{5,4},{6,7},{7,6},{8,9},{9,8},{10,11... | collective-permute-start | bytes 2654216 | tf_op jit(solution)/shard_map/ppermute | solution.py:549
  85.4 39.1 %collective-permute-start.12 = (bf16[512,768]{1,0:T(8,128)(2,1)}, bf16[512,768]{1,0:T(8,128)(2,1)S(1)}, u32[]{:S(2)}, u32[]{:S(2)}) collective-permute-start(bf16[512,768]{1,0:T(8,128)(2,1)} %dynamic-slice_bitcast_fusion), channel_id=1, source_target_pairs={{0,1},{1,0},{2,3},{3,2},{4,5},{5,4},{6,7},{7,6},{8,9},{9,8},{10,11... | collective-permute-start | bytes 2359304 | tf_op jit(solution)/shard_map/ppermute | solution.py:549
  124.6 1.8 copy-start.16
  124.6 2.0 copy-start.17
  200.9 55.2 %collective-permute-start.29 = (bf16[768,512]{1,0:T(8,128)(2,1)}, bf16[768,512]{1,0:T(8,128)(2,1)S(1)}, u32[]{:S(2)}, u32[]{:S(2)}) collective-permute-start(bf16[768,512]{1,0:T(8,128)(2,1)} %get-tuple-element.54), channel_id=1, source_target_pairs={{0,1},{1,0},{2,3},{3,2},{4,5},{5,4},{6,7},{7,6},{8,9},{9,8},{10,11... | collective-permute-start | bytes 2359304 | tf_op jit(solution)/shard_map/ppermute | solution.py:549
  213.8 43.2 %collective-permute-start.26 = (bf16[768,640]{1,0:T(8,128)(2,1)}, bf16[768,640]{1,0:T(8,128)(2,1)S(1)}, u32[]{:S(2)}, u32[]{:S(2)}) collective-permute-start(bf16[768,640]{1,0:T(8,128)(2,1)} %get-tuple-element.51), channel_id=1, source_target_pairs={{0,1},{1,0},{2,3},{3,2},{4,5},{5,4},{6,7},{7,6},{8,9},{9,8},{10,11... | collective-permute-start | bytes 2949128 | tf_op jit(solution)/shard_map/ppermute | solution.py:549
  240.1 14.3 %copy-start.24 = (bf16[512,768]{1,0:T(8,128)(2,1)S(1)}, bf16[512,768]{1,0:T(8,128)(2,1)}, u32[]{:S(2)}) copy-start(bf16[512,768]{1,0:T(8,128)(2,1)} %get-tuple-element.40) | copy-start | bytes 2359300
  240.1 14.8 %copy-start.19 = (bf16[768,512]{1,0:T(8,128)(2,1)S(1)}, bf16[768,512]{1,0:T(8,128)(2,1)}, u32[]{:S(2)}) copy-start(bf16[768,512]{1,0:T(8,128)(2,1)} %get-tuple-element.52) | copy-start | bytes 2359300
  253.9 2.3 copy-start.23
  253.9 2.5 collective-permute-start.30
  254.4 3.1 collective-permute-start.24
  254.5 23.6 %collective-permute-start.25 = (f32[512,768]{1,0:T(8,128)}, f32[512,768]{1,0:T(8,128)S(1)}, u32[]{:S(2)}, u32[]{:S(2)}) collective-permute-start(f32[512,768]{1,0:T(8,128)} %get-tuple-element.48), channel_id=1, source_target_pairs={{0,1},{1,0},{2,3},{3,2},{4,5},{5,4},{6,7},{7,6},{8,9},{9,8},{10,11... | collective-permute-start | bytes 4718600 | tf_op jit(solution)/shard_map/ppermute | solution.py:549
  254.9 1.7 copy-start.22
  256.1 24.3 %collective-permute-start.36 = (bf16[768,1152]{1,0:T(8,128)(2,1)S(1)}, bf16[768,1152]{1,0:T(8,128)(2,1)S(1)}, u32[]{:S(2)}, u32[]{:S(2)}) collective-permute-start(bf16[768,1152]{1,0:T(8,128)(2,1)S(1)} %copy-done.23), channel_id=1, source_target_pairs={{0,1},{1,0},{2,3},{3,2},{4,5},{5,4},{6,7},{7,6},{8,9},{9,8},{10,11... | collective-permute-start | bytes 5308424 | tf_op jit(solution)/shard_map/ppermute | solution.py:549
  256.6 25.6 %collective-permute-start.39 = (bf16[768,1152]{1,0:T(8,128)(2,1)S(1)}, bf16[768,1152]{1,0:T(8,128)(2,1)S(1)}, u32[]{:S(2)}, u32[]{:S(2)}) collective-permute-start(bf16[768,1152]{1,0:T(8,128)(2,1)S(1)} %copy-done.22), channel_id=1, source_target_pairs={{0,1},{1,0},{2,3},{3,2},{4,5},{5,4},{6,7},{7,6},{8,9},{9,8},{10,11... | collective-permute-start | bytes 5308424 | tf_op jit(solution)/shard_map/ppermute | solution.py:549
  257.0 13.5 %collective-permute-start.31 = (bf16[384,640]{1,0:T(8,128)(2,1)S(1)}, bf16[384,640]{1,0:T(8,128)(2,1)S(1)}, u32[]{:S(2)}, u32[]{:S(2)}) collective-permute-start(bf16[384,640]{1,0:T(8,128)(2,1)S(1)} %add_convert_fusion.2), channel_id=1, source_target_pairs={{0,2},{2,0},{4,6},{6,4},{8,10},{10,8},{12,14},{14,12},{16,18},{18,... | collective-permute-start | bytes 1474568 | tf_op jit(solution)/shard_map/ppermute | solution.py:553
  257.6 13.3 %collective-permute-start.27 = (bf16[384,640]{1,0:T(8,128)(2,1)S(1)}, bf16[384,640]{1,0:T(8,128)(2,1)S(1)}, u32[]{:S(2)}, u32[]{:S(2)}) collective-permute-start(bf16[384,640]{1,0:T(8,128)(2,1)S(1)} %add_convert_fusion.3), channel_id=1, source_target_pairs={{0,4},{2,6},{4,0},{6,2},{8,12},{10,14},{12,8},{14,10},{16,20},{18,... | collective-permute-start | bytes 1474568 | tf_op jit(solution)/shard_map/ppermute | solution.py:553
  259.0 19.1 %copy-start.11 = (f32[512,768]{1,0:T(8,128)S(1)}, f32[512,768]{1,0:T(8,128)}, u32[]{:S(2)}) copy-start(f32[512,768]{1,0:T(8,128)} %get-tuple-element.47) | copy-start | bytes 4718596
  270.6 7.4 %collective-permute-start.32 = (bf16[192,640]{1,0:T(8,128)(2,1)S(1)}, bf16[192,640]{1,0:T(8,128)(2,1)S(1)}, u32[]{:S(2)}, u32[]{:S(2)}) collective-permute-start(bf16[192,640]{1,0:T(8,128)(2,1)S(1)} %add_convert_fusion.6), channel_id=1, source_target_pairs={{0,4},{2,6},{4,0},{6,2},{8,12},{10,14},{12,8},{14,10},{16,20},{18,... | collective-permute-start | bytes 737288 | tf_op jit(solution)/shard_map/ppermute | solution.py:553
  270.9 9.3 %collective-permute-start.28 = (bf16[192,640]{1,0:T(8,128)(2,1)S(1)}, bf16[192,640]{1,0:T(8,128)(2,1)S(1)}, u32[]{:S(2)}, u32[]{:S(2)}) collective-permute-start(bf16[192,640]{1,0:T(8,128)(2,1)S(1)} %add_convert_fusion.7), channel_id=1, source_target_pairs={{0,2},{2,0},{4,6},{6,4},{8,10},{10,8},{12,14},{14,12},{16,18},{18,... | collective-permute-start | bytes 737288 | tf_op jit(solution)/shard_map/ppermute | solution.py:553
  280.3 1.9 copy-start.9
  281.9 20.1 %collective-permute-start.37 = (bf16[384,1152]{1,0:T(8,128)(2,1)S(1)}, bf16[384,1152]{1,0:T(8,128)(2,1)S(1)}, u32[]{:S(2)}, u32[]{:S(2)}) collective-permute-start(bf16[384,1152]{1,0:T(8,128)(2,1)S(1)} %add_convert_fusion.1), channel_id=1, source_target_pairs={{0,4},{2,6},{4,0},{6,2},{8,12},{10,14},{12,8},{14,10},{16,20},{18,... | collective-permute-start | bytes 2654216 | tf_op jit(solution)/shard_map/ppermute | solution.py:553
  282.5 20.8 %collective-permute-start.40 = (bf16[384,1152]{1,0:T(8,128)(2,1)S(1)}, bf16[384,1152]{1,0:T(8,128)(2,1)S(1)}, u32[]{:S(2)}, u32[]{:S(2)}) collective-permute-start(bf16[384,1152]{1,0:T(8,128)(2,1)S(1)} %add_convert_fusion), channel_id=1, source_target_pairs={{0,2},{2,0},{4,6},{6,4},{8,10},{10,8},{12,14},{14,12},{16,18},{18,... | collective-permute-start | bytes 2654216 | tf_op jit(solution)/shard_map/ppermute | solution.py:553
  283.2 33.1 %collective-permute-start.33 = (bf16[48,1280]{1,0:T(8,128)(2,1)S(1)}, bf16[48,1280]{1,0:T(8,128)(2,1)S(1)}, u32[]{:S(2)}, u32[]{:S(2)}) collective-permute-start(bf16[48,1280]{1,0:T(8,128)(2,1)S(1)} %get-tuple-element.121), channel_id=1, source_target_pairs={{0,8},{2,10},{4,12},{6,14},{8,0},{10,2},{12,4},{14,6},{16,24},{18,... | collective-permute-start | bytes 368648 | tf_op jit(solution)/shard_map/ppermute | solution.py:553
  283.3 34.6 %collective-permute-start.35 = (bf16[48,1280]{1,0:T(8,128)(2,1)S(1)}, bf16[48,1280]{1,0:T(8,128)(2,1)S(1)}, u32[]{:S(2)}, u32[]{:S(2)}) collective-permute-start(bf16[48,1280]{1,0:T(8,128)(2,1)S(1)} %get-tuple-element.122), channel_id=1, source_target_pairs={{0,24},{2,26},{4,28},{6,30},{8,16},{10,18},{12,20},{14,22},{16,8},... | collective-permute-start | bytes 368648 | tf_op jit(solution)/shard_map/ppermute | solution.py:553
  286.5 31.4 %collective-permute-start.34 = (bf16[48,1280]{1,0:T(8,128)(2,1)S(1)}, bf16[48,1280]{1,0:T(8,128)(2,1)S(1)}, u32[]{:S(2)}, u32[]{:S(2)}) collective-permute-start(bf16[48,1280]{1,0:T(8,128)(2,1)S(1)} %get-tuple-element.123), channel_id=1, source_target_pairs={{0,16},{2,18},{4,20},{6,22},{8,24},{10,26},{12,28},{14,30},{16,0},... | collective-permute-start | bytes 368648 | tf_op jit(solution)/shard_map/ppermute | solution.py:553
  302.2 9.9 %collective-permute-start.38 = (bf16[192,1152]{1,0:T(8,128)(2,1)S(1)}, bf16[192,1152]{1,0:T(8,128)(2,1)S(1)}, u32[]{:S(2)}, u32[]{:S(2)}) collective-permute-start(bf16[192,1152]{1,0:T(8,128)(2,1)S(1)} %add_convert_fusion.5), channel_id=1, source_target_pairs={{0,2},{2,0},{4,6},{6,4},{8,10},{10,8},{12,14},{14,12},{16,18},{18,... | collective-permute-start | bytes 1327112 | tf_op jit(solution)/shard_map/ppermute | solution.py:553
  303.4 9.8 %collective-permute-start.41 = (bf16[192,1152]{1,0:T(8,128)(2,1)S(1)}, bf16[192,1152]{1,0:T(8,128)(2,1)S(1)}, u32[]{:S(2)}, u32[]{:S(2)}) collective-permute-start(bf16[192,1152]{1,0:T(8,128)(2,1)S(1)} %add_convert_fusion.4), channel_id=1, source_target_pairs={{0,4},{2,6},{4,0},{6,2},{8,12},{10,14},{12,8},{14,10},{16,20},{18,... | collective-permute-start | bytes 1327112 | tf_op jit(solution)/shard_map/ppermute | solution.py:553
  314.4 8.9 %collective-permute-start.42 = (bf16[48,2304]{1,0:T(8,128)(2,1)}, bf16[48,2304]{1,0:T(8,128)(2,1)S(1)}, u32[]{:S(2)}, u32[]{:S(2)}) collective-permute-start(bf16[48,2304]{1,0:T(8,128)(2,1)} %get-tuple-element.116), channel_id=1, source_target_pairs={{0,8},{2,10},{4,12},{6,14},{8,0},{10,2},{12,4},{14,6},{16,24},{18,... | collective-permute-start | bytes 663560 | tf_op jit(solution)/shard_map/ppermute | solution.py:553
  314.4 12.2 %collective-permute-start.44 = (bf16[48,2304]{1,0:T(8,128)(2,1)}, bf16[48,2304]{1,0:T(8,128)(2,1)S(1)}, u32[]{:S(2)}, u32[]{:S(2)}) collective-permute-start(bf16[48,2304]{1,0:T(8,128)(2,1)} %get-tuple-element.117), channel_id=1, source_target_pairs={{0,24},{2,26},{4,28},{6,30},{8,16},{10,18},{12,20},{14,22},{16,8},... | collective-permute-start | bytes 663560 | tf_op jit(solution)/shard_map/ppermute | solution.py:553
  316.2 17.9 %collective-permute-start.43 = (bf16[48,2304]{1,0:T(8,128)(2,1)S(1)}, bf16[48,2304]{1,0:T(8,128)(2,1)S(1)}, u32[]{:S(2)}, u32[]{:S(2)}) collective-permute-start(bf16[48,2304]{1,0:T(8,128)(2,1)S(1)} %get-tuple-element.118), channel_id=1, source_target_pairs={{0,16},{2,18},{4,20},{6,22},{8,24},{10,26},{12,28},{14,30},{16,0},... | collective-permute-start | bytes 663560 | tf_op jit(solution)/shard_map/ppermute | solution.py:553
  (6 other events, 7.6 us)

commit v2 on v1

--- a/solution.py
+++ b/solution.py
@@ -68,7 +68,11 @@
         live = new
 
 
-def call(kernel, name, grid, in_specs, out_specs, out_shape, scratch=(), prefetch=1):
+def after(x, *deps):
+    return lax.optimization_barrier((x, deps))[0]
+
+
+def call(kernel, name, us, grid, in_specs, out_specs, out_shape, scratch=(), prefetch=1):
     return pl.pallas_call(
         kernel,
         grid_spec=pltpu.PrefetchScalarGridSpec(
@@ -80,6 +84,7 @@
         ),
         out_shape=out_shape,
         compiler_params=pltpu.CompilerParams(vmem_limit_bytes=VMEM),
+        cost_estimate=pl.CostEstimate(flops=int(us * 1.15e9), transcendentals=0, bytes_accessed=int(us * 1e6)),
         name=name,
     )
 
@@ -167,6 +172,7 @@
     return call(
         functools.partial(qkv_kernel, layout=layout, rows=rows, width=width, half=half),
         "qkv",
+        12,
         (s // TB,),
         [ANY] * len(layout) + [held, received, table, table],
         [
@@ -244,6 +250,7 @@
     return call(
         attend_kernel,
         "attend",
+        20,
         (2, s // QB),
         [
             pl.BlockSpec((s, LANES), lambda r, i, g: (0, 0)),
@@ -321,33 +328,37 @@
                 dq_ref[at, cols] = rotate(dq, cos_ref[at, :], sin_ref[at, :], -1).astype(BF)
 
 
-def attend_back_call(ranges, col, row, qkv, do, o, lse, cos, sin):
+def attend_back_call(r, ranges, col, row, qkv, do, o, lse, cos, sin):
     _, s, w3 = qkv.shape
     width = w3 // 3
-    whole = pl.BlockSpec((None, s, width), lambda r, c, g: (r, 0, 0))
-    table = pl.BlockSpec((s, LANES), lambda r, c, g: (0, 0))
+    whole = pl.BlockSpec((None, s, width), lambda _, c, g: (r, 0, 0))
+    table = pl.BlockSpec((s, LANES), lambda _, c, g: (0, 0))
 
     def block(n):
-        return pl.BlockSpec((None, QB, width), lambda r, c, g: (r, c, n))
+        return pl.BlockSpec((None, QB, width), lambda _, c, g: (r, c, n))
 
     return call(
         attend_back_kernel,
         "attend_back",
-        (2, s // QB),
+        18,
+        (1, s // QB),
         [
-            pl.BlockSpec((QB, LANES), lambda r, c, g: (c, 0)),
-            pl.BlockSpec((8, s), lambda r, c, g: (0, 0)),
+            pl.BlockSpec((QB, LANES), lambda _, c, g: (c, 0)),
+            pl.BlockSpec((8, s), lambda _, c, g: (0, 0)),
             whole,
             block(1),
             block(2),
             whole,
             whole,
-            pl.BlockSpec((None, 8, s), lambda r, c, g: (r, 0, 0)),
+            pl.BlockSpec((None, 8, s), lambda _, c, g: (r, 0, 0)),
             table,
             table,
         ],
-        [whole, pl.BlockSpec((None, QB, 2 * width), lambda r, c, g: (r, c, 0))],
-        [jax.ShapeDtypeStruct((2, s, width), BF), jax.ShapeDtypeStruct((2, s, 2 * width), BF)],
+        [
+            pl.BlockSpec((s, width), lambda _, c, g: (0, 0)),
+            pl.BlockSpec((QB, 2 * width), lambda _, c, g: (c, 0)),
+        ],
+        [jax.ShapeDtypeStruct((s, width), BF), jax.ShapeDtypeStruct((s, 2 * width), BF)],
         [
             pltpu.VMEM((width, s), BF),
             pltpu.VMEM((width, s), BF),
@@ -426,6 +437,7 @@
     return call(
         functools.partial(mlp_kernel, layout=layout, rows=rows, width=width, units=units, half=half),
         "mlp",
+        32,
         (s // TB,),
         [ANY] * len(layout) + [held, received, held, received, pair(width), row],
         [own, other, block, pair(width), block, block, block, pair(2 * units), pair(units), row],
@@ -459,7 +471,7 @@
             store_rows(info, value, out_ref, slice(start - base, stop - base), order, rows)
 
 
-def weight_grad_call(name, info, rows, orders, operands, products, split, total):
+def weight_grad_call(name, us, info, rows, orders, operands, products, split, total):
     specs, arrays = [], []
     for array, lead in operands:
         arrays.append(array)
@@ -473,6 +485,7 @@
     return call(
         functools.partial(weight_grad_kernel, products=products, orders=orders, rows=rows),
         name,
+        us,
         (1,),
         specs,
         [pl.BlockSpec(shape, lambda g, i: (0, 0)) for shape in shapes],
@@ -483,7 +496,7 @@
 
 def input_kernel(info, *refs, layout, rows, width, half, order):
     n = len(layout)
-    (x_ref, xr_ref, dq_ref, dkv_ref, dr_ref, gain_ref, gg_ref,
+    (x_ref, xr_ref, dq0_ref, dkv0_ref, dq1_ref, dkv1_ref, dr_ref, gain_ref, gg_ref,
      own_ref, other_ref, gcol_ref, w_ref, acc_ref, col_ref, sems) = refs[n:]
     own = own_block(info, half)
 
@@ -497,8 +510,9 @@
     x = jnp.where(own, x_ref[...], xr_ref[...]).astype(F32)
     xhat, inverse = norm(x)
     dh = 0.0
-    for r in range(2):
-        dh = dh + nt(dq_ref[r], w_ref[r, :, :width]) + nt(dkv_ref[r], w_ref[r, :, width : 3 * width])
+    for r, dq_ref, dkv_ref in ((0, dq0_ref, dkv0_ref), (1, dq1_ref, dkv1_ref)):
+        dh = dh + nt(dq_ref[...], w_ref[r, :, :width])
+        dh = dh + nt(dkv_ref[...], w_ref[r, :, width : 3 * width])
     acc_ref[0:1, :] += jnp.sum(dh * xhat, axis=0, keepdims=True)
     grad = dr_ref[...] + norm_back(dh, xhat, inverse, gain)
 
@@ -516,20 +530,18 @@
         store_rows(info, col_ref, gcol_ref, slice(0, LANES), order, rows)
 
 
-def input_call(info, pieces, layout, rows, width, x, xr, dq, dkv, dr, gains, gg, order):
-    d, s = x.shape[2], dq.shape[1]
+def input_call(info, pieces, layout, rows, width, x, xr, draw, dr, gains, gg, order):
+    d, s = x.shape[2], dr.shape[0]
     half = s // TB // 2
     held, received, block, own, other = token_specs(d, half)
-
-    def pair(w):
-        return pl.BlockSpec((2, TB, w), lambda b, i: (0, b, 0))
-
+    dq, dkv = [pl.BlockSpec((TB, w), lambda b, i: (b, 0)) for w in (width, 2 * width)]
     row = pl.BlockSpec((8, d), lambda b, i: (0, 0))
     return call(
         functools.partial(input_kernel, layout=layout, rows=rows, width=width, half=half, order=order),
         "input_back",
+        13,
         (s // TB,),
-        [ANY] * len(layout) + [held, received, pair(width), pair(2 * width), block, row, row],
+        [ANY] * len(layout) + [held, received, dq, dkv, dq, dkv, block, row, row],
         [own, other, pl.BlockSpec((d, LANES), lambda b, i: (0, 0))],
         [
             jax.ShapeDtypeStruct((s // 2, d), F32),
@@ -542,7 +554,7 @@
             pltpu.VMEM((d, LANES), F32),
             pltpu.SemaphoreType.DMA((copies_of(layout),)),
         ],
-    )(info, *pieces, x, xr, dq, dkv, dr, gains, gg)
+    )(info, *pieces, x, xr, *draw, dr, gains, gg)
 
 
 def swap(x):
@@ -553,45 +565,67 @@
     return lax.ppermute(x, "dp", [(i, i ^ k) for i in range(16)])
 
 
-def gather(slab, split, cube):
-    if not cube:
-        whole = lax.all_gather(slab, "dp", axis=0, tiled=True)
-        return [whole, swap(whole)], [(0, 0, None), (1, 0, None)]
-    block = jnp.concatenate([slab] + [peer(slab, k) for k in (4, 8, 12)], 0)
-    a, b = block[:, :split], block[:, split:]
-    a = jnp.concatenate([a, peer(a, 1)], 0)
-    b = jnp.concatenate([b, peer(b, 2)], 0)
-    own = [a, b, peer(a, 2), peer(b, 1)]
-    where = [
-        (0, ORDER_A[:8]),
-        (split, ORDER_B[:8]),
-        (0, ORDER_A[8:]),
-        (split, ORDER_B[8:]),
-    ]
-    layout = [(r, col, order) for r in range(2) for col, order in where]
-    return own + [swap(p) for p in own], layout
+def under(x, run, *sends):
+    x, arrays = after((x, [a for _, a in sends]))
+    got = [f(a) for (f, _), a in zip(sends, arrays)]
+    return after((run(x), got))
+
+
+def to(k):
+    return lambda x: peer(x, k)
 
 
 def add(*terms):
     return functools.reduce(jnp.add, [t.astype(F32) for t in terms])
 
 
-def scatter(a, b, cube):
-    if not cube:
-        both = jnp.concatenate([add(*a), add(*b)], 1)
-        return lax.psum_scatter(both, "dp", scatter_dimension=0, tiled=True)
-    n = a[0].shape[0] // 2
-    ra = peer(add(*(t[n:] for t in a)).astype(BF), 2)
-    rb = peer(add(*(t[n:] for t in b)).astype(BF), 1)
-    a, b = [t[:n] for t in a] + [ra], [t[:n] for t in b] + [rb]
-    n = n // 2
-    ra = peer(add(*(t[n:] for t in a)).astype(BF), 1)
-    rb = peer(add(*(t[n:] for t in b)).astype(BF), 2)
-    both = jnp.concatenate([add(*(t[:n] for t in a), ra[:n]), add(*(t[:n] for t in b), rb[:n])], 1)
-    n = n // 4
-    send = both.astype(BF)
-    got = [peer(send[i * n : (i + 1) * n], 4 * i) for i in (1, 2, 3)]
-    return add(both[:n], *got)
+class Gather:
+    def __init__(self, split):
+        self.split = split
+
+    def first(self, slab):
+        return [(to(k), slab) for k in (4, 8, 12)]
+
+    def near(self, slab, got):
+        block = jnp.concatenate([slab, *got], 0)
+        self.ab = block[:, : self.split], block[:, self.split :]
+        return [(to(k), x) for k, x in zip((1, 2), self.ab)]
+
+    def far(self, got):
+        self.ab = [jnp.concatenate(x, 0) for x in zip(self.ab, got)]
+        return [(to(k), x) for k, x in zip((2, 1), self.ab)]
+
+    def pieces(self, got, theirs, got_theirs):
+        where = [(0, ORDER_A[:8]), (self.split, ORDER_B[:8]), (0, ORDER_A[8:]), (self.split, ORDER_B[8:])]
+        layout = [(r, col, order) for r in range(2) for col, order in where]
+        return [*self.ab, *got, *theirs, *got_theirs], layout
+
+
+def half_sends(terms, ks):
+    n = terms[0][0].shape[0] // 2
+    keep = [[t[:n] for t in ts] for ts in terms]
+    return keep, [(to(k), add(*(t[n:] for t in ts)).astype(BF)) for k, ts in zip(ks, terms)]
+
+
+def joined(keep, got):
+    return [ts + [g] for ts, g in zip(keep, got)]
+
+
+def last_sends(terms):
+    both = jnp.concatenate([add(*ts) for ts in terms], 1)
+    n = both.shape[0] // 4
+    send = both[n:].astype(BF)
+    return both[:n], [(to(4 * i), send[(i - 1) * n : i * n]) for i in (1, 2, 3)]
+
+
+def gather_plain(slab):
+    whole = lax.all_gather(slab, "dp", axis=0, tiled=True)
+    return [whole, swap(whole)], [(0, 0, None), (1, 0, None)]
+
+
+def scatter_plain(a, b):
+    both = jnp.concatenate([add(*a), add(*b)], 1)
+    return lax.psum_scatter(both, "dp", scatter_dimension=0, tiled=True)
 
 
 def local(
@@ -606,14 +640,14 @@
     units = up_to(units_here)
     s = segment_ids.shape[1]
 
-    def other_half(x):
-        return swap(lax.dynamic_index_in_dim(x, 1 - t, 0, False))
-
     def placed(own, got):
         first = t == 0
         return jnp.stack([jnp.where(first, own, got), jnp.where(first, got, own)])
 
-    x_recv = other_half(hidden_in)
+    def other(x):
+        return lax.dynamic_index_in_dim(x, 1 - t, 0, False)
+
+    x_recv = swap(other(hidden_in))
     gain_cols = jnp.stack([attn_gain, mlp_gain], 1)
     gain_cols = jnp.pad(gain_cols, ((0, 0), (0, LANES - 2)))
     slab1 = jnp.concatenate([qkv_weight[0], qkv_weight[1], qkv_weight[2], gain_cols], 1)
@@ -626,10 +660,6 @@
     )
     total1, total2 = slab1.shape[1], slab2.shape[1]
     split1, split2 = total1 // 2 // LANES * LANES, total2 // 2 // LANES * LANES
-    w1, layout1 = gather(slab1, split1, cube)
-    w2, layout2 = gather(slab2, split2, cube)
-    dy_recv = other_half(cotangent)
-
     seg = lax.dynamic_index_in_dim(segment_ids, t, 0, False)
     index = jnp.arange(s, dtype=jnp.int32)
     start = jnp.sum((seg[None, :] < seg[:, None]).astype(jnp.int32), axis=1)
@@ -648,50 +678,103 @@
     high = jnp.max(jnp.where(meet, block, -1), axis=1)
     ranges = jnp.stack([low * QB, high - low + 1], 1).astype(jnp.int32)
 
-    qkv, h1, gains = qkv_call(info, w1, layout1, rows, width, hidden_in, x_recv, cos, sin)
-    o, lse = attend_call(ranges, col, row, qkv)
+    def project(w1):
+        return qkv_call(info, w1, layout1, rows, width, hidden_in, x_recv, cos, sin)
+
+    def attend(qkv):
+        return attend_call(ranges, col, row, qkv)
+
+    if cube:
+        g1, g2 = Gather(split1), Gather(split2)
+        got = [f(x) for f, x in g1.first(slab1)]
+        sends = g1.near(slab1, got)
+        slab2, near = after((slab2, [x for _, x in sends]))
+        g1.ab = near
+        got = [f(x) for (f, _), x in zip(sends, near)]
+        got2 = [f(x) for f, x in g2.first(slab2)]
+        sends = g1.far(got)
+        theirs = [swap(x) for _, x in sends]
+        got = [f(x) for f, x in sends]
+        w1, layout1 = g1.pieces(got, theirs, [swap(x) for x in got])
+        (qkv, h1, gains), (*got, dy_recv) = under(
+            w1, project, *g2.near(slab2, got2), (swap, other(cotangent))
+        )
+        far = g2.far(got)
+        (o, lse), got = under(qkv, attend, *far, *((swap, x) for _, x in far))
+        w2, layout2 = g2.pieces(got[:2], got[2:], [swap(x) for x in got[:2]])
+    else:
+        w1, layout1 = gather_plain(slab1)
+        w2, layout2 = gather_plain(slab2)
+        dy_recv = swap(other(cotangent))
+        qkv, h1, gains = project(w1)
+        o, lse = attend(qkv)
     out_own, out_other, dr, do, h2, dy, da, dgu, m, gg = mlp_call(
         info, w2, layout2, rows, width, units, hidden_in, x_recv, cotangent, dy_recv, o, gains
     )
-    layer_out = placed(out_own, swap(out_other))
-
     orders = (ORDER_A, ORDER_B) if cube else (None, None)
 
     def grads2(r):
-        return weight_grad_call(
-            "mlp_weight_grad", info, rows, orders,
+        return lambda o: weight_grad_call(
+            "mlp_weight_grad", 10, info, rows, orders,
             [(da, None), (h2, None), (dy, None), (o, r), (dgu, r), (m, r)],
             [(0, 3, 0), (1, 4, width), (2, 5, width + 2 * units)], split2, total2,
         )
 
-    theirs = [swap(g) for g in grads2(1)]
-    mine = grads2(0)
-    sum2 = scatter((mine[0], theirs[0]), (mine[1], theirs[1]), cube)
-
-    dq, dkv = attend_back_call(ranges, col, row, qkv, do, o, lse, cos, sin)
-
-    def grads1(r):
+    def grads1(draw):
         return weight_grad_call(
-            "qkv_weight_grad", info, rows, orders,
-            [(h1, None), (dq, r), (dkv, r)],
+            "qkv_weight_grad", 6, info, rows, orders,
+            [(h1, None), (draw[0], None), (draw[1], None)],
             [(0, 1, 0), (0, 2, width)], split1, total1 - LANES,
         )
 
-    theirs = [swap(g) for g in grads1(1)]
-    mine = grads1(0)
-    in_own, in_other, gcol = input_call(
-        info, w1, layout1, rows, width, hidden_in, x_recv, dq, dkv, dr, gains, gg, orders[1]
-    )
-    input_grad = placed(in_own, swap(in_other))
-    gcol_got = swap(gcol)
-    sum1 = scatter(
-        (mine[0], theirs[0]),
-        (
-            jnp.concatenate([mine[1], gcol], 1),
-            jnp.concatenate([theirs[1], gcol_got], 1),
-        ),
-        cube,
-    )
+    def back(r):
+        return lambda do: attend_back_call(r, ranges, col, row, qkv, do, o, lse, cos, sin)
+
+    def input_back(dr):
+        return input_call(
+            info, w1, layout1, rows, width, hidden_in, x_recv, (*draw0, *draw1), dr, gains, gg, orders[1]
+        )
+
+    sent = grads2(1)(o)
+    mine, (*theirs, out_recv) = under(o, grads2(0), *((swap, g) for g in sent), (swap, out_other))
+    layer_out = placed(out_own, out_recv)
+    sums2 = [[a, b] for a, b in zip(mine, theirs)]
+    if cube:
+        keep, sends = half_sends(sums2, (2, 1))
+        draw1, got = under(do, back(1), *sends)
+        keep, sends = half_sends(joined(keep, got), (1, 2))
+        do, sends2 = after((do, [x for _, x in sends]))
+        sent = grads1(after(draw1, sends2))
+        draw0, got = under(
+            after(do, sent), back(0), *((f, x) for (f, _), x in zip(sends, sends2)), *((swap, g) for g in sent)
+        )
+        keep2, sends2 = last_sends(joined(keep, got[:2]))
+        draw0, last = after((draw0, [x for _, x in sends2]))
+        mine = grads1(draw0)
+        keep, sends = half_sends([[a, b] for a, b in zip(mine, got[2:])], (2, 1))
+        (in_own, in_other, gcol), got = under(
+            dr, input_back, *((f, x) for (f, _), x in zip(sends2, last)), *sends
+        )
+        sum2 = add(keep2, *got[:3])
+        n = d // 2
+        gcols = gcol, swap(gcol)
+        gain_sum = add(*(g[:n] for g in gcols), peer(add(*(g[n:] for g in gcols)).astype(BF), 1))
+        keep = joined(keep, got[3:])
+        keep, sends = half_sends([keep[0], [jnp.concatenate([add(*keep[1]), gain_sum], 1)]], (1, 2))
+        got = [f(x) for f, x in sends]
+        in_recv = swap(in_other)
+        input_grad = placed(in_own, in_recv)
+        keep, sends = last_sends(joined(keep, got))
+        sum1 = add(keep, *(f(x) for f, x in sends))
+    else:
+        sum2 = scatter_plain(*sums2)
+        draw1, draw0 = back(1)(do), back(0)(do)
+        theirs = [swap(g) for g in grads1(draw1)]
+        mine = grads1(draw0)
+        in_own, in_other, gcol = input_back(dr)
+        input_grad = placed(in_own, swap(in_other))
+        b = [jnp.concatenate([g, c], 1) for g, c in zip((mine[1], theirs[1]), (gcol, swap(gcol)))]
+        sum1 = scatter_plain((mine[0], theirs[0]), b)
     qkv_grad = sum1[:, : 3 * width].reshape(rows, 3, width).transpose(1, 0, 2)
     c = width
     proj_grad = sum2[:, :c].T

time: 342 us -> 299 us (0.87)
  waiting for transfers between devices: 98.9 us -> 50.1 us
  other arithmetic: 17.1 us -> 24.5 us
    ppermute x28 -> x29, waiting for transfers between devices: 98.8 us -> 44.5 us  [peer(): return lax.ppermute(x, 'dp', [(i, i ^ k) for i in range(16)])]
    ppermute x28 -> x29, starting transfers between devices: 36.9 us -> 51.9 us  [peer(): return lax.ppermute(x, 'dp', [(i, i ^ k) for i in range(16)])]
    ppermute x17, starting transfers between devices: 16.3 us -> 3.69 us  [swap(): return lax.ppermute(x, 'tensor', [(0, 1), (1, 0)])]
    convert_element_type x10 -> x8, other arithmetic: 1.39 us -> 8.33 us  [the longest x7 8.3 us: half_sends(): add(*(t[n:] for t in ts)).astype(BF)]
    ppermute x17, waiting for transfers between devices: 0.04 us -> 5.54 us  [swap(): return lax.ppermute(x, 'tensor', [(0, 1), (1, 0)])]
    add x6 -> x8, other arithmetic: 0.83 us -> 4.3 us  [add(): return functools.reduce(jnp.add, [t.astype(F32) for t in terms])]
    pallas_call x2 -> x3, Pallas kernels: 56.8 us -> 54.6 us  [the longest x2 36 us: attend_back_call(): call(attend_back_kernel, 'attend_back', 18, (1, s // QB), [pl.BlockSpec((...]
  transfers between devices with their start and end apart: 45 -> 46, of which waited for: 15 -> 17; matrix products, arithmetic and copies ran while one was open for 8% -> 7% of each run, Pallas kernels for 22% -> 31%
where the time goes in v2:
time: 299 us; the launch traced here: 293 us
  Pallas kernels  146 us (49%)
  starting transfers between devices  55.6 us (19%)
  waiting for transfers between devices  50.1 us (17%)
  other arithmetic  24.5 us (8%)
  local copies, waits for them, and re-layouts  15.3 us (5%)
    ppermute x29, starting transfers between devices, peer(): return lax.ppermute(x, 'dp', [(i, i ^ k) for i in range(16)])  51.9 us
    ppermute x29, waiting for transfers between devices, peer(): return lax.ppermute(x, 'dp', [(i, i ^ k) for i in range(16)])  44.5 us
    pallas_call x2, Pallas kernels, attend_back_call(): call(attend_back_kernel, 'attend_back', 18, (1, s // QB), [pl.BlockSpec((...  36 us
    pallas_call x1, Pallas kernels, mlp_call(): call(functools.partial(mlp_kernel, layout=layout, rows=rows, width=width,...  32.5 us
    pallas_call x4, Pallas kernels, weight_grad_call(): call(functools.partial(weight_grad_kernel, products=products, orders=orde...  32.5 us
    pallas_call x1, Pallas kernels, attend_call(): call(attend_kernel, 'attend', 20, (2, s // QB), [pl.BlockSpec((s, LANES),...  18.6 us
    pallas_call x1, Pallas kernels, input_call(): call(functools.partial(input_kernel, layout=layout, rows=rows, width=widt...  13.8 us
    pallas_call x1, Pallas kernels, qkv_call(): call(functools.partial(qkv_kernel, layout=layout, rows=rows, width=width,...  12.4 us
  transfers between devices with their start and end apart: 46, of which 17 were waited for; matrix products, arithmetic and copies ran while one was open for 7% of the time, Pallas kernels for 31%

profile of v2, /device:TPU:0, one launch (start us, length us, event | category | flops | bytes accessed | tf_op | source)
XLA Modules:
  0.0 293.2 jit_solution(8179247331506192659)
XLA Ops:
  2.4 5.1 %collective-permute-start.2 = (bf16[48,1280]{1,0:T(8,128)(2,1)S(1)}, bf16[48,1280]{1,0:T(8,128)(2,1)S(1)}, u32[]{:S(2)}, u32[]{:S(2)}) collective-permute-start(bf16[48,1280]{1,0:T(8,128)(2,1)S(1)} %pad_maximum_fusion.11), channel_id=1, source_target_pairs={{0,24},{2,26},{4,28},{6,30},{8,16},{10,18},{12,20},{14,22},{16,8},... | collective-permute-start | bytes 368648 | tf_op jit(solution)/shard_map/ppermute | solution.py:565
  8.2 1.2 dynamic-slice_bitcast_fusion
  12.0 1.9 fusion.21
  13.9 1.3 pad_maximum_fusion.6.refs_10_.cos_ref
  16.5 1.3 pad_maximum_fusion.7.refs_11_.sin_ref
  18.0 3.6 %collective-permute-start.5 = (bf16[48,2304]{1,0:T(8,128)(2,1)S(1)}, bf16[48,2304]{1,0:T(8,128)(2,1)S(1)}, u32[]{:S(2)}, u32[]{:S(2)}) collective-permute-start(bf16[48,2304]{1,0:T(8,128)(2,1)S(1)} %fusion.19), channel_id=1, source_target_pairs={{0,24},{2,26},{4,28},{6,30},{8,16},{10,18},{12,20},{14,22},{16,8},... | collective-permute-start | bytes 663560 | tf_op jit(solution)/shard_map/ppermute | solution.py:565
  21.7 0.8 collective-permute-start.3
  22.5 1.6 collective-permute-start.6
  24.1 12.5 %collective-permute-done.3 = bf16[48,2304]{1,0:T(8,128)(2,1)S(1)} collective-permute-done((bf16[48,2304]{1,0:T(8,128)(2,1)S(1)}, bf16[48,2304]{1,0:T(8,128)(2,1)S(1)}, u32[]{:S(2)}, u32[]{:S(2)}) %collective-permute-start.3) | collective-permute-done | bytes 221216 | tf_op jit(solution)/shard_map/ppermute | solution.py:565
  36.6 1.5 collective-permute-start.7
  38.1 6.0 %collective-permute-done.7 = bf16[192,640]{1,0:T(8,128)(2,1)S(1)} collective-permute-done((bf16[192,640]{1,0:T(8,128)(2,1)S(1)}, bf16[192,640]{1,0:T(8,128)(2,1)S(1)}, u32[]{:S(2)}, u32[]{:S(2)}) %collective-permute-start.7) | collective-permute-done | bytes 245792 | tf_op jit(solution)/shard_map/ppermute | solution.py:565
  44.2 1.6 collective-permute-start.9
  45.8 1.6 collective-permute-start.8
  48.0 8.2 %collective-permute-done.9.refs_3_ = bf16[384,640]{1,0:T(8,128)(2,1)S(1)} collective-permute-done((bf16[384,640]{1,0:T(8,128)(2,1)S(1)}, bf16[384,640]{1,0:T(8,128)(2,1)S(1)}, u32[]{:S(2)}, u32[]{:S(2)}) %collective-permute-start.9) | collective-permute-done | bytes 491552 | tf_op jit(solution)/shard_map/ppermute | solution.py:565
  56.2 1.3 collective-permute-done.8.refs_2_
  58.1 1.3 collective-permute-done.12.refs_6_
  59.4 1.0 collective-permute-start.15
  60.4 1.5 collective-permute-start.16
  61.9 12.4 %qkv.1 = (bf16[2,1024,1152]{2,1,0:T(8,128)(2,1)}, bf16[1024,768]{1,0:T(8,128)(2,1)}, f32[8,768]{1,0:T(8,128)}) custom-call(s32[2]{0:T(128)} %pad_add_fusion.1.info, bf16[384,640]{1,0:T(8,128)(2,1)} %copy-done.14, bf16[384,640]{1,0:T(8,128)(2,1)} %copy-done.15, bf16[384,640]{1,0:T(8,128)(2,1)} %copy-done.28, bf16[384,640]{1,0:T(8,128)(2,1)} %copy-done.27, ...), custom_call_target="tpu_custom_call" | custom-call | flops 13799999488 | bytes 12000000 | tf_op jit(solution)/shard_map/qkv/pallas_call | solution.py:172
  75.8 1.1 collective-permute-start.19
  78.0 1.0 broadcast_in_dim.41.col_ref
  79.0 18.6 %attend.1 = (bf16[2,1024,384]{2,1,0:T(8,128)(2,1)}, f32[2,8,1024]{2,1,0:T(8,128)}) custom-call(s32[4,2]{1,0:T(4,128)} %pad_add_fusion.ranges, s32[1024,128]{1,0:T(8,128)} %broadcast_in_dim.41.col_ref, s32[8,1024]{1,0:T(8,128)} %broadcast_in_dim.42.row_ref, bf16[2,1024,1152]{2,1,0:T(8,128)(2,1)} %get-tuple-element.141.q_ref.k_ref.v_ref, ...), custom_call_target="tpu_custom_call" | custom-call | flops 23000000512 | bytes 20000000 | tf_op jit(solution)/shard_map/attend/pallas_call | solution.py:250
  98.3 1.9 collective-permute-done.22.refs_6_
  100.2 1.3 collective-permute-done.23.refs_7_
  101.5 0.9 copy-done.25
  102.4 32.5 %mlp.1 = (bf16[512,768]{1,0:T(8,128)(2,1)}, bf16[512,768]{1,0:T(8,128)(2,1)}, f32[1024,768]{1,0:T(8,128)}, bf16[2,1024,384]{2,1,0:T(8,128)(2,1)}, bf16[1024,768]...) custom-call(s32[2]{0:T(128)} %pad_add_fusion.1.info, ...), custom_call_target="tpu_custom_call" | custom-call | flops 36800000000 | bytes 32000000 | tf_op jit(solution)/shard_map/mlp/pallas_call | solution.py:437
  135.0 10.1 %mlp_weight_grad.2 = (bf16[768,1152]{1,0:T(8,128)(2,1)}, bf16[768,1152]{1,0:T(8,128)(2,1)}) custom-call(s32[2]{0:T(128)} %pad_add_fusion.1.info, bf16[1024,768]{1,0:T(8,128)(2,1)} %get-tuple-element.156.refs_0_, bf16[1024,768]{1,0:T(8,128)(2,1)} %get-tuple-element.157.refs_1_, bf16[1024,768]{1,0:T(8,128)(2,1)} %get-tuple-element.158.refs_2_, ...), custom_call_target="tpu_custom_call" | custom-call | flops 11500000256 | bytes 10000000 | tf_op jit(solution)/shard_map/mlp_weight_grad/pallas_call | solution.py:485
  145.7 10.1 %mlp_weight_grad.3 = (bf16[768,1152]{1,0:T(8,128)(2,1)}, bf16[768,1152]{1,0:T(8,128)(2,1)}) custom-call(s32[2]{0:T(128)} %pad_add_fusion.1.info, bf16[1024,768]{1,0:T(8,128)(2,1)} %get-tuple-element.156.refs_0_, bf16[1024,768]{1,0:T(8,128)(2,1)} %get-tuple-element.157.refs_1_, bf16[1024,768]{1,0:T(8,128)(2,1)} %get-tuple-element.158.refs_2_, ...), custom_call_target="tpu_custom_call" | custom-call | flops 11500000256 | bytes 10000000 | tf_op jit(solution)/shard_map/mlp_weight_grad/pallas_call | solution.py:485
  155.8 2.5 add_convert_fusion.1
  158.3 1.1 add_convert_fusion
  159.4 3.5 %collective-permute-start.27 = (bf16[384,1152]{1,0:T(8,128)(2,1)}, bf16[384,1152]{1,0:T(8,128)(2,1)}, u32[]{:S(2)}, u32[]{:S(2)}) collective-permute-start(bf16[384,1152]{1,0:T(8,128)(2,1)} %add_convert_fusion.1), channel_id=1, source_target_pairs={{0,4},{2,6},{4,0},{6,2},{8,12},{10,14},{12,8},{14,10},{16,20},{18,... | collective-permute-start | bytes 2654216 | tf_op jit(solution)/shard_map/ppermute | solution.py:565
  162.9 3.9 %collective-permute-start.28 = (bf16[384,1152]{1,0:T(8,128)(2,1)}, bf16[384,1152]{1,0:T(8,128)(2,1)}, u32[]{:S(2)}, u32[]{:S(2)}) collective-permute-start(bf16[384,1152]{1,0:T(8,128)(2,1)} %add_convert_fusion), channel_id=1, source_target_pairs={{0,2},{2,0},{4,6},{6,4},{8,10},{10,8},{12,14},{14,12},{16,18},{18,... | collective-permute-start | bytes 2654216 | tf_op jit(solution)/shard_map/ppermute | solution.py:565
  166.8 18.1 %attend_back.2 = (bf16[1024,384]{1,0:T(8,128)(2,1)}, bf16[1024,768]{1,0:T(8,128)(2,1)}) custom-call(s32[4,2]{1,0:T(4,128)} %pad_add_fusion.ranges, s32[1024,128]{1,0:T(8,128)} %broadcast_in_dim.41.col_ref, s32[8,1024]{1,0:T(8,128)} %broadcast_in_dim.42.row_ref, bf16[2,1024,1152]{2,1,0:T(8,128)(2,1)} %get-tuple-element.141.q_ref.k_ref.v_ref, ...), custom_call_target="tpu_custom_call" | custom-call | flops 20700000256 | bytes 18000000 | tf_op jit(solution)/shard_map/attend_back/pallas_call | solution.py:340
  185.0 1.3 pad_maximum_fusion.2
  186.3 1.0 collective-permute-done.28
  187.3 1.2 add_convert_fusion.4
  188.5 1.2 add_convert_fusion.3
  189.7 6.1 %qkv_weight_grad.2 = (bf16[768,640]{1,0:T(8,128)(2,1)}, bf16[768,512]{1,0:T(8,128)(2,1)}) custom-call(s32[2]{0:T(128)} %pad_add_fusion.1.info, bf16[1024,768]{1,0:T(8,128)(2,1)} %get-tuple-element.185.refs_0_, bf16[1024,384]{1,0:T(8,128)(2,1)} %get-tuple-element.190.refs_1_.refs_12_, bf16[1024,768]{1,0:T(8,128)(2,1)} %get-tuple-element.191.refs_2_.refs_13_), custom_call_target="tpu_custom_call" | custom-call | flops 6899999744 | bytes 6000000 | tf_op jit(solution)/shard_map/qkv_weight_grad/pallas_call | solution.py:485
  195.8 5.9 %collective-permute-start.29 = (bf16[192,1152]{1,0:T(8,128)(2,1)S(1)}, bf16[192,1152]{1,0:T(8,128)(2,1)}, u32[]{:S(2)}, u32[]{:S(2)}) collective-permute-start(bf16[192,1152]{1,0:T(8,128)(2,1)S(1)} %add_convert_fusion.4), channel_id=1, source_target_pairs={{0,2},{2,0},{4,6},{6,4},{8,10},{10,8},{12,14},{14,12},{16,18},{18,... | collective-permute-start | bytes 1327112 | tf_op jit(solution)/shard_map/ppermute | solution.py:565
  202.1 18.0 %attend_back.3 = (bf16[1024,384]{1,0:T(8,128)(2,1)}, bf16[1024,768]{1,0:T(8,128)(2,1)}) custom-call(s32[4,2]{1,0:T(4,128)} %pad_add_fusion.ranges, s32[1024,128]{1,0:T(8,128)} %broadcast_in_dim.41.col_ref, s32[8,1024]{1,0:T(8,128)} %broadcast_in_dim.42.row_ref, bf16[2,1024,1152]{2,1,0:T(8,128)(2,1)} %get-tuple-element.141.q_ref.k_ref.v_ref, ...), custom_call_target="tpu_custom_call" | custom-call | flops 20700000256 | bytes 18000000 | tf_op jit(solution)/shard_map/attend_back/pallas_call | solution.py:340
  220.2 0.9 copy-done.8
  221.0 1.5 convert_add_fusion
  222.5 1.4 convert_add_fusion.1
  224.1 6.2 %qkv_weight_grad.3 = (bf16[768,640]{1,0:T(8,128)(2,1)}, bf16[768,512]{1,0:T(8,128)(2,1)}) custom-call(s32[2]{0:T(128)} %pad_add_fusion.1.info, bf16[1024,768]{1,0:T(8,128)(2,1)} %get-tuple-element.185.refs_0_, bf16[1024,384]{1,0:T(8,128)(2,1)} %get-tuple-element.206.refs_1_.refs_10_, bf16[1024,768]{1,0:T(8,128)(2,1)} %get-tuple-element.207.refs_2_.refs_11_), custom_call_target="tpu_custom_call" | custom-call | flops 6899999744 | bytes 6000000 | tf_op jit(solution)/shard_map/qkv_weight_grad/pallas_call | solution.py:485
  230.3 1.1 add_convert_fusion.5
  231.4 1.1 add_convert_fusion.2
  232.5 4.9 %collective-permute-start.33 = (bf16[48,2304]{1,0:T(8,128)(2,1)S(1)}, bf16[48,2304]{1,0:T(8,128)(2,1)S(1)}, u32[]{:S(2)}, u32[]{:S(2)}) collective-permute-start(bf16[48,2304]{1,0:T(8,128)(2,1)S(1)} %get-tuple-element.221), channel_id=1, source_target_pairs={{0,8},{2,10},{4,12},{6,14},{8,0},{10,2},{12,4},{14,6},{16,24},{18,... | collective-permute-start | bytes 663560 | tf_op jit(solution)/shard_map/ppermute | solution.py:565
  237.4 2.4 collective-permute-start.35
  239.9 3.1 %collective-permute-start.37 = (bf16[384,512]{1,0:T(8,128)(2,1)S(1)}, bf16[384,512]{1,0:T(8,128)(2,1)S(1)}, u32[]{:S(2)}, u32[]{:S(2)}) collective-permute-start(bf16[384,512]{1,0:T(8,128)(2,1)S(1)} %add_convert_fusion.5), channel_id=1, source_target_pairs={{0,2},{2,0},{4,6},{6,4},{8,10},{10,8},{12,14},{14,12},{16,18},{18,... | collective-permute-start | bytes 1179656 | tf_op jit(solution)/shard_map/ppermute | solution.py:565
  243.0 13.8 %input_back.1 = (f32[512,768]{1,0:T(8,128)}, f32[512,768]{1,0:T(8,128)}, bf16[768,128]{1,0:T(8,128)(2,1)}) custom-call(s32[2]{0:T(128)} %pad_add_fusion.1.info, bf16[384,640]{1,0:T(8,128)(2,1)} %copy-done.14, bf16[384,640]{1,0:T(8,128)(2,1)} %copy-done.15, bf16[384,640]{1,0:T(8,128)(2,1)} %copy-done.28, bf16[384,640]{1,0:T(8,128)(2,1)} %copy-done.27, ...), custom_call_target="tpu_custom_call" | custom-call | flops 14949999616 | bytes 13000000 | tf_op jit(solution)/shard_map/input_back/pallas_call | solution.py:539
  260.9 1.5 collective-permute-start.39
  262.4 2.9 collective-permute-done.41
  265.4 1.6 collective-permute-start.42
  267.0 3.0 %collective-permute-done.39 = bf16[192,640]{1,0:T(8,128)(2,1)S(1)} collective-permute-done((bf16[192,640]{1,0:T(8,128)(2,1)S(1)}, bf16[192,640]{1,0:T(8,128)(2,1)S(1)}, u32[]{:S(2)}, u32[]{:S(2)}) %collective-permute-start.39) | collective-permute-done | bytes 245792 | tf_op jit(solution)/shard_map/ppermute | solution.py:565
  270.0 1.1 convert_add_fusion.3
  271.1 1.2 collective-permute-done.42
  272.5 2.5 collective-permute-start.43
  275.4 1.1 collective-permute-start.44
  277.9 2.5 collective-permute-done.43
  280.4 1.8 collective-permute-done.45
  282.2 3.8 %collective-permute-done.44 = bf16[48,1280]{1,0:T(8,128)(2,1)S(1)} collective-permute-done((bf16[48,1280]{1,0:T(8,128)(2,1)S(1)}, bf16[48,1280]{1,0:T(8,128)(2,1)S(1)}, u32[]{:S(2)}, u32[]{:S(2)}) %collective-permute-start.44) | collective-permute-done | bytes 122912 | tf_op jit(solution)/shard_map/ppermute | solution.py:565
  287.5 1.0 reshape.66
  289.2 1.5 slice_reduce_fusion
  290.9 1.9 pad_maximum_fusion
  (175 shorter events, 20.7 us)
Async XLA Ops:
  0.6 9.4 %copy-start.19 = (s32[2,1024]{1,0:T(2,128)S(1)}, s32[2,1024]{1,0:T(2,128)}, u32[]{:S(2)}) copy-start(s32[2,1024]{1,0:T(2,128)} %param.10) | copy-start | bytes 24580
  0.6 11.2 %copy-start.16 = (bf16[2,48,576]{2,1,0:T(8,128)(2,1)S(1)}, bf16[2,48,576]{2,1,0:T(8,128)(2,1)}, u32[]{:S(2)}) copy-start(bf16[2,48,576]{2,1,0:T(8,128)(2,1)} %param.13) | copy-start | bytes 331780
  0.7 11.2 %copy-start.12 = (bf16[2,512,768]{2,1,0:T(8,128)(2,1)S(1)}, bf16[2,512,768]{2,1,0:T(8,128)(2,1)}, u32[]{:S(2)}) copy-start(bf16[2,512,768]{2,1,0:T(8,128)(2,1)} %refs_10_.1) | copy-start | bytes 4718596
  2.4 15.3 %collective-permute-start.2 = (bf16[48,1280]{1,0:T(8,128)(2,1)S(1)}, bf16[48,1280]{1,0:T(8,128)(2,1)S(1)}, u32[]{:S(2)}, u32[]{:S(2)}) collective-permute-start(bf16[48,1280]{1,0:T(8,128)(2,1)S(1)} %pad_maximum_fusion.11), channel_id=1, source_target_pairs={{0,24},{2,26},{4,28},{6,30},{8,16},{10,18},{12,20},{14,22},{16,8},... | collective-permute-start | bytes 368648 | tf_op jit(solution)/shard_map/ppermute | solution.py:565
  7.6 10.4 %collective-permute-start.1 = (bf16[48,1280]{1,0:T(8,128)(2,1)S(1)}, bf16[48,1280]{1,0:T(8,128)(2,1)S(1)}, u32[]{:S(2)}, u32[]{:S(2)}) collective-permute-start(bf16[48,1280]{1,0:T(8,128)(2,1)S(1)} %pad_maximum_fusion.11), channel_id=1, source_target_pairs={{0,16},{2,18},{4,20},{6,22},{8,24},{10,26},{12,28},{14,30},{16,0},... | collective-permute-start | bytes 368648 | tf_op jit(solution)/shard_map/ppermute | solution.py:565
  7.6 10.4 %collective-permute-start = (bf16[48,1280]{1,0:T(8,128)(2,1)S(1)}, bf16[48,1280]{1,0:T(8,128)(2,1)S(1)}, u32[]{:S(2)}, u32[]{:S(2)}) collective-permute-start(bf16[48,1280]{1,0:T(8,128)(2,1)S(1)} %pad_maximum_fusion.11), channel_id=1, source_target_pairs={{0,8},{2,10},{4,12},{6,14},{8,0},{10,2},{12,4},{14,6},{16,24},{18,... | collective-permute-start | bytes 368648 | tf_op jit(solution)/shard_map/ppermute | solution.py:565
  9.4 52.5 %collective-permute-start.14 = (bf16[512,768]{1,0:T(8,128)(2,1)S(1)}, bf16[512,768]{1,0:T(8,128)(2,1)}, u32[]{:S(2)}, u32[]{:S(2)}) collective-permute-start(bf16[512,768]{1,0:T(8,128)(2,1)S(1)} %dynamic-slice_bitcast_fusion), channel_id=1, source_target_pairs={{0,1},{1,0},{2,3},{3,2},{4,5},{5,4},{6,7},{7,6},{8,9},{9,8},{10,11... | collective-permute-start | bytes 2359304 | tf_op jit(solution)/shard_map/ppermute | solution.py:561
  11.9 4.5 %copy-start.17 = (bf16[576,48]{0,1:T(8,128)(2,1)S(1)}, bf16[576,48]{0,1:T(8,128)(2,1)}, u32[]{:S(2)}) copy-start(bf16[576,48]{0,1:T(8,128)(2,1)} %param.14) | copy-start | bytes 165892
  11.9 4.5 %copy-start.18 = (bf16[384,48]{0,1:T(8,128)(2,1)S(1)}, bf16[384,48]{0,1:T(8,128)(2,1)}, u32[]{:S(2)}) copy-start(bf16[384,48]{0,1:T(8,128)(2,1)} %param.12) | copy-start | bytes 110596
  18.0 29.4 %collective-permute-start.5 = (bf16[48,2304]{1,0:T(8,128)(2,1)S(1)}, bf16[48,2304]{1,0:T(8,128)(2,1)S(1)}, u32[]{:S(2)}, u32[]{:S(2)}) collective-permute-start(bf16[48,2304]{1,0:T(8,128)(2,1)S(1)} %fusion.19), channel_id=1, source_target_pairs={{0,24},{2,26},{4,28},{6,30},{8,16},{10,18},{12,20},{14,22},{16,8},... | collective-permute-start | bytes 663560 | tf_op jit(solution)/shard_map/ppermute | solution.py:565
  21.7 25.7 %collective-permute-start.4 = (bf16[48,2304]{1,0:T(8,128)(2,1)S(1)}, bf16[48,2304]{1,0:T(8,128)(2,1)S(1)}, u32[]{:S(2)}, u32[]{:S(2)}) collective-permute-start(bf16[48,2304]{1,0:T(8,128)(2,1)S(1)} %fusion.19), channel_id=1, source_target_pairs={{0,16},{2,18},{4,20},{6,22},{8,24},{10,26},{12,28},{14,30},{16,0},... | collective-permute-start | bytes 663560 | tf_op jit(solution)/shard_map/ppermute | solution.py:565
  21.7 14.9 %collective-permute-start.3 = (bf16[48,2304]{1,0:T(8,128)(2,1)S(1)}, bf16[48,2304]{1,0:T(8,128)(2,1)S(1)}, u32[]{:S(2)}, u32[]{:S(2)}) collective-permute-start(bf16[48,2304]{1,0:T(8,128)(2,1)S(1)} %fusion.19), channel_id=1, source_target_pairs={{0,8},{2,10},{4,12},{6,14},{8,0},{10,2},{12,4},{14,6},{16,24},{18,... | collective-permute-start | bytes 663560 | tf_op jit(solution)/shard_map/ppermute | solution.py:565
  22.5 23.2 %collective-permute-start.6 = (bf16[192,640]{1,0:T(8,128)(2,1)S(1)}, bf16[192,640]{1,0:T(8,128)(2,1)S(1)}, u32[]{:S(2)}, u32[]{:S(2)}) collective-permute-start(bf16[192,640]{1,0:T(8,128)(2,1)S(1)} %get-tuple-element.122), channel_id=1, source_target_pairs={{0,2},{2,0},{4,6},{6,4},{8,10},{10,8},{12,14},{14,12},{16,18},{18,... | collective-permute-start | bytes 737288 | tf_op jit(solution)/shard_map/ppermute | solution.py:565
  36.6 7.6 %collective-permute-start.7 = (bf16[192,640]{1,0:T(8,128)(2,1)S(1)}, bf16[192,640]{1,0:T(8,128)(2,1)S(1)}, u32[]{:S(2)}, u32[]{:S(2)}) collective-permute-start(bf16[192,640]{1,0:T(8,128)(2,1)S(1)} %get-tuple-element.123), channel_id=1, source_target_pairs={{0,4},{2,6},{4,0},{6,2},{8,12},{10,14},{12,8},{14,10},{16,20},{18,... | collective-permute-start | bytes 737288 | tf_op jit(solution)/shard_map/ppermute | solution.py:565
  44.2 17.7 %copy-start.15 = (bf16[384,640]{1,0:T(8,128)(2,1)}, bf16[384,640]{1,0:T(8,128)(2,1)S(1)}, u32[]{:S(2)}) copy-start(bf16[384,640]{1,0:T(8,128)(2,1)S(1)} %constant_dynamic-update-slice_fusion.6.refs_1_) | copy-start | bytes 1474564
  44.2 12.0 %collective-permute-start.9 = (bf16[384,640]{1,0:T(8,128)(2,1)S(1)}, bf16[384,640]{1,0:T(8,128)(2,1)S(1)}, u32[]{:S(2)}, u32[]{:S(2)}) collective-permute-start(bf16[384,640]{1,0:T(8,128)(2,1)S(1)} %constant_dynamic-update-slice_fusion.6.refs_1_), channel_id=1, source_target_pairs={{0,2},{2,0},{4,6},{6,4},{8,10},{10,8},{12,14},{14,12},{16,18},{18,... | collective-permute-start | bytes 1474568 | tf_op jit(solution)/shard_map/ppermute | solution.py:565
  45.8 16.1 %copy-start.14 = (bf16[384,640]{1,0:T(8,128)(2,1)}, bf16[384,640]{1,0:T(8,128)(2,1)S(1)}, u32[]{:S(2)}) copy-start(bf16[384,640]{1,0:T(8,128)(2,1)S(1)} %constant_dynamic-update-slice_fusion.4.refs_0_) | copy-start | bytes 1474564
  45.8 11.7 %collective-permute-start.8 = (bf16[384,640]{1,0:T(8,128)(2,1)S(1)}, bf16[384,640]{1,0:T(8,128)(2,1)S(1)}, u32[]{:S(2)}, u32[]{:S(2)}) collective-permute-start(bf16[384,640]{1,0:T(8,128)(2,1)S(1)} %constant_dynamic-update-slice_fusion.4.refs_0_), channel_id=1, source_target_pairs={{0,4},{2,6},{4,0},{6,2},{8,12},{10,14},{12,8},{14,10},{16,20},{18,... | collective-permute-start | bytes 1474568 | tf_op jit(solution)/shard_map/ppermute | solution.py:565
  47.4 10.2 %collective-permute-start.11 = (bf16[384,640]{1,0:T(8,128)(2,1)S(1)}, bf16[384,640]{1,0:T(8,128)(2,1)S(1)}, u32[]{:S(2)}, u32[]{:S(2)}) collective-permute-start(bf16[384,640]{1,0:T(8,128)(2,1)S(1)} %constant_dynamic-update-slice_fusion.6.refs_1_), channel_id=1, source_target_pairs={{0,1},{1,0},{2,3},{3,2},{4,5},{5,4},{6,7},{7,6},{8,9},{9,8},{10,11... | collective-permute-start | bytes 1474568 | tf_op jit(solution)/shard_map/ppermute | solution.py:561
  47.5 10.1 %collective-permute-start.10 = (bf16[384,640]{1,0:T(8,128)(2,1)S(1)}, bf16[384,640]{1,0:T(8,128)(2,1)S(1)}, u32[]{:S(2)}, u32[]{:S(2)}) collective-permute-start(bf16[384,640]{1,0:T(8,128)(2,1)S(1)} %constant_dynamic-update-slice_fusion.4.refs_0_), channel_id=1, source_target_pairs={{0,1},{1,0},{2,3},{3,2},{4,5},{5,4},{6,7},{7,6},{8,9},{9,8},{10,11... | collective-permute-start | bytes 1474568 | tf_op jit(solution)/shard_map/ppermute | solution.py:561
  56.2 5.7 %copy-start.27 = (bf16[384,640]{1,0:T(8,128)(2,1)}, bf16[384,640]{1,0:T(8,128)(2,1)S(1)}, u32[]{:S(2)}) copy-start(bf16[384,640]{1,0:T(8,128)(2,1)S(1)} %collective-permute-done.9.refs_3_) | copy-start | bytes 1474564
  56.2 1.9 collective-permute-start.13
  57.5 4.4 %copy-start.28 = (bf16[384,640]{1,0:T(8,128)(2,1)}, bf16[384,640]{1,0:T(8,128)(2,1)S(1)}, u32[]{:S(2)}) copy-start(bf16[384,640]{1,0:T(8,128)(2,1)S(1)} %collective-permute-done.8.refs_2_) | copy-start | bytes 1474564
  57.5 1.9 collective-permute-start.12
  57.6 4.3 %copy-start.29 = (bf16[384,640]{1,0:T(8,128)(2,1)}, bf16[384,640]{1,0:T(8,128)(2,1)S(1)}, u32[]{:S(2)}) copy-start(bf16[384,640]{1,0:T(8,128)(2,1)S(1)} %collective-permute-done.11.refs_5_) | copy-start | bytes 1474564
  59.4 15.0 %collective-permute-start.15 = (bf16[192,1152]{1,0:T(8,128)(2,1)S(1)}, bf16[192,1152]{1,0:T(8,128)(2,1)S(1)}, u32[]{:S(2)}, u32[]{:S(2)}) collective-permute-start(bf16[192,1152]{1,0:T(8,128)(2,1)S(1)} %get-tuple-element.135), channel_id=1, source_target_pairs={{0,2},{2,0},{4,6},{6,4},{8,10},{10,8},{12,14},{14,12},{16,18},{18,... | collective-permute-start | bytes 1327112 | tf_op jit(solution)/shard_map/ppermute | solution.py:565
  60.4 14.0 %collective-permute-start.16 = (bf16[192,1152]{1,0:T(8,128)(2,1)S(1)}, bf16[192,1152]{1,0:T(8,128)(2,1)S(1)}, u32[]{:S(2)}, u32[]{:S(2)}) collective-permute-start(bf16[192,1152]{1,0:T(8,128)(2,1)S(1)} %get-tuple-element.136), channel_id=1, source_target_pairs={{0,4},{2,6},{4,0},{6,2},{8,12},{10,14},{12,8},{14,10},{16,20},{18,... | collective-permute-start | bytes 1327112 | tf_op jit(solution)/shard_map/ppermute | solution.py:565
  61.9 12.5 %collective-permute-start.17 = (bf16[512,768]{1,0:T(8,128)(2,1)S(1)}, bf16[512,768]{1,0:T(8,128)(2,1)S(1)}, u32[]{:S(2)}, u32[]{:S(2)}) collective-permute-start(bf16[512,768]{1,0:T(8,128)(2,1)S(1)} %dynamic-slice_bitcast_fusion.1), channel_id=1, source_target_pairs={{0,1},{1,0},{2,3},{3,2},{4,5},{5,4},{6,7},{7,6},{8,9},{9,8},{10,11... | collective-permute-start | bytes 2359304 | tf_op jit(solution)/shard_map/ppermute | solution.py:561
  75.3 22.3 %copy-start.6 = (bf16[384,1152]{1,0:T(8,128)(2,1)}, bf16[384,1152]{1,0:T(8,128)(2,1)S(1)}, u32[]{:S(2)}) copy-start(bf16[384,1152]{1,0:T(8,128)(2,1)S(1)} %get-tuple-element.146.refs_0_) | copy-start | bytes 2654212
  75.3 22.3 %copy-start.7 = (bf16[384,1152]{1,0:T(8,128)(2,1)}, bf16[384,1152]{1,0:T(8,128)(2,1)S(1)}, u32[]{:S(2)}) copy-start(bf16[384,1152]{1,0:T(8,128)(2,1)S(1)} %get-tuple-element.147.refs_1_) | copy-start | bytes 2654212
  75.3 22.3 %collective-permute-start.18 = (bf16[384,1152]{1,0:T(8,128)(2,1)S(1)}, bf16[384,1152]{1,0:T(8,128)(2,1)S(1)}, u32[]{:S(2)}, u32[]{:S(2)}) collective-permute-start(bf16[384,1152]{1,0:T(8,128)(2,1)S(1)} %get-tuple-element.146.refs_0_), channel_id=1, source_target_pairs={{0,4},{2,6},{4,0},{6,2},{8,12},{10,14},{12,8},{14,10},{16,20},{18,... | collective-permute-start | bytes 2654216 | tf_op jit(solution)/shard_map/ppermute | solution.py:565
  75.8 21.8 %collective-permute-start.19 = (bf16[384,1152]{1,0:T(8,128)(2,1)S(1)}, bf16[384,1152]{1,0:T(8,128)(2,1)S(1)}, u32[]{:S(2)}, u32[]{:S(2)}) collective-permute-start(bf16[384,1152]{1,0:T(8,128)(2,1)S(1)} %get-tuple-element.147.refs_1_), channel_id=1, source_target_pairs={{0,2},{2,0},{4,6},{6,4},{8,10},{10,8},{12,14},{14,12},{16,18},{18,... | collective-permute-start | bytes 2654216 | tf_op jit(solution)/shard_map/ppermute | solution.py:565
  76.9 20.8 %collective-permute-start.20 = (bf16[384,1152]{1,0:T(8,128)(2,1)S(1)}, bf16[384,1152]{1,0:T(8,128)(2,1)S(1)}, u32[]{:S(2)}, u32[]{:S(2)}) collective-permute-start(bf16[384,1152]{1,0:T(8,128)(2,1)S(1)} %get-tuple-element.146.refs_0_), channel_id=1, source_target_pairs={{0,1},{1,0},{2,3},{3,2},{4,5},{5,4},{6,7},{7,6},{8,9},{9,8},{10,11... | collective-permute-start | bytes 2654216 | tf_op jit(solution)/shard_map/ppermute | solution.py:561
  76.9 20.8 %collective-permute-start.21 = (bf16[384,1152]{1,0:T(8,128)(2,1)S(1)}, bf16[384,1152]{1,0:T(8,128)(2,1)S(1)}, u32[]{:S(2)}, u32[]{:S(2)}) collective-permute-start(bf16[384,1152]{1,0:T(8,128)(2,1)S(1)} %get-tuple-element.147.refs_1_), channel_id=1, source_target_pairs={{0,1},{1,0},{2,3},{3,2},{4,5},{5,4},{6,7},{7,6},{8,9},{9,8},{10,11... | collective-permute-start | bytes 2654216 | tf_op jit(solution)/shard_map/ppermute | solution.py:561
  97.6 3.8 %copy-start.20 = (bf16[384,1152]{1,0:T(8,128)(2,1)}, bf16[384,1152]{1,0:T(8,128)(2,1)S(1)}, u32[]{:S(2)}) copy-start(bf16[384,1152]{1,0:T(8,128)(2,1)S(1)} %collective-permute-done.18.refs_2_) | copy-start | bytes 2654212
  97.7 2.5 collective-permute-start.22
  97.8 3.7 %collective-permute-start.23 = (bf16[384,1152]{1,0:T(8,128)(2,1)S(1)}, bf16[384,1152]{1,0:T(8,128)(2,1)S(1)}, u32[]{:S(2)}, u32[]{:S(2)}) collective-permute-start(bf16[384,1152]{1,0:T(8,128)(2,1)S(1)} %collective-permute-done.19.refs_3_), channel_id=1, source_target_pairs={{0,1},{1,0},{2,3},{3,2},{4,5},{5,4},{6,7},{7,6},{8,9},{9,8},{10,11... | collective-permute-start | bytes 2654216 | tf_op jit(solution)/shard_map/ppermute | solution.py:561
  145.1 10.7 %collective-permute-start.24 = (bf16[768,1152]{1,0:T(8,128)(2,1)}, bf16[768,1152]{1,0:T(8,128)(2,1)S(1)}, u32[]{:S(2)}, u32[]{:S(2)}) collective-permute-start(bf16[768,1152]{1,0:T(8,128)(2,1)} %get-tuple-element.167), channel_id=1, source_target_pairs={{0,1},{1,0},{2,3},{3,2},{4,5},{5,4},{6,7},{7,6},{8,9},{9,8},{10,11... | collective-permute-start | bytes 5308424 | tf_op jit(solution)/shard_map/ppermute | solution.py:561
  145.2 10.6 %collective-permute-start.25 = (bf16[768,1152]{1,0:T(8,128)(2,1)}, bf16[768,1152]{1,0:T(8,128)(2,1)S(1)}, u32[]{:S(2)}, u32[]{:S(2)}) collective-permute-start(bf16[768,1152]{1,0:T(8,128)(2,1)} %get-tuple-element.168), channel_id=1, source_target_pairs={{0,1},{1,0},{2,3},{3,2},{4,5},{5,4},{6,7},{7,6},{8,9},{9,8},{10,11... | collective-permute-start | bytes 5308424 | tf_op jit(solution)/shard_map/ppermute | solution.py:561
  145.6 10.2 %collective-permute-start.26 = (bf16[512,768]{1,0:T(8,128)(2,1)}, bf16[512,768]{1,0:T(8,128)(2,1)S(1)}, u32[]{:S(2)}, u32[]{:S(2)}) collective-permute-start(bf16[512,768]{1,0:T(8,128)(2,1)} %get-tuple-element.169), channel_id=1, source_target_pairs={{0,1},{1,0},{2,3},{3,2},{4,5},{5,4},{6,7},{7,6},{8,9},{9,8},{10,11... | collective-permute-start | bytes 2359304 | tf_op jit(solution)/shard_map/ppermute | solution.py:561
  159.4 25.5 %copy-start.11 = (bf16[512,768]{1,0:T(8,128)(2,1)S(1)}, bf16[512,768]{1,0:T(8,128)(2,1)}, u32[]{:S(2)}) copy-start(bf16[512,768]{1,0:T(8,128)(2,1)} %get-tuple-element.155) | copy-start | bytes 2359300
  159.4 26.9 %collective-permute-start.27 = (bf16[384,1152]{1,0:T(8,128)(2,1)}, bf16[384,1152]{1,0:T(8,128)(2,1)}, u32[]{:S(2)}, u32[]{:S(2)}) collective-permute-start(bf16[384,1152]{1,0:T(8,128)(2,1)} %add_convert_fusion.1), channel_id=1, source_target_pairs={{0,4},{2,6},{4,0},{6,2},{8,12},{10,14},{12,8},{14,10},{16,20},{18,... | collective-permute-start | bytes 2654216 | tf_op jit(solution)/shard_map/ppermute | solution.py:565
  162.9 24.4 %collective-permute-start.28 = (bf16[384,1152]{1,0:T(8,128)(2,1)}, bf16[384,1152]{1,0:T(8,128)(2,1)}, u32[]{:S(2)}, u32[]{:S(2)}) collective-permute-start(bf16[384,1152]{1,0:T(8,128)(2,1)} %add_convert_fusion), channel_id=1, source_target_pairs={{0,2},{2,0},{4,6},{6,4},{8,10},{10,8},{12,14},{14,12},{16,18},{18,... | collective-permute-start | bytes 2654216 | tf_op jit(solution)/shard_map/ppermute | solution.py:565
  195.8 24.3 %collective-permute-start.29 = (bf16[192,1152]{1,0:T(8,128)(2,1)S(1)}, bf16[192,1152]{1,0:T(8,128)(2,1)}, u32[]{:S(2)}, u32[]{:S(2)}) collective-permute-start(bf16[192,1152]{1,0:T(8,128)(2,1)S(1)} %add_convert_fusion.4), channel_id=1, source_target_pairs={{0,2},{2,0},{4,6},{6,4},{8,10},{10,8},{12,14},{14,12},{16,18},{18,... | collective-permute-start | bytes 1327112 | tf_op jit(solution)/shard_map/ppermute | solution.py:565
  201.6 18.5 %collective-permute-start.30 = (bf16[192,1152]{1,0:T(8,128)(2,1)S(1)}, bf16[192,1152]{1,0:T(8,128)(2,1)}, u32[]{:S(2)}, u32[]{:S(2)}) collective-permute-start(bf16[192,1152]{1,0:T(8,128)(2,1)S(1)} %add_convert_fusion.3), channel_id=1, source_target_pairs={{0,4},{2,6},{4,0},{6,2},{8,12},{10,14},{12,8},{14,10},{16,20},{18,... | collective-permute-start | bytes 1327112 | tf_op jit(solution)/shard_map/ppermute | solution.py:565
  201.6 18.5 %collective-permute-start.32 = (bf16[768,512]{1,0:T(8,128)(2,1)}, bf16[768,512]{1,0:T(8,128)(2,1)S(1)}, u32[]{:S(2)}, u32[]{:S(2)}) collective-permute-start(bf16[768,512]{1,0:T(8,128)(2,1)} %get-tuple-element.201), channel_id=1, source_target_pairs={{0,1},{1,0},{2,3},{3,2},{4,5},{5,4},{6,7},{7,6},{8,9},{9,8},{10,11... | collective-permute-start | bytes 2359304 | tf_op jit(solution)/shard_map/ppermute | solution.py:561
  201.6 18.5 %collective-permute-start.31 = (bf16[768,640]{1,0:T(8,128)(2,1)}, bf16[768,640]{1,0:T(8,128)(2,1)S(1)}, u32[]{:S(2)}, u32[]{:S(2)}) collective-permute-start(bf16[768,640]{1,0:T(8,128)(2,1)} %get-tuple-element.200), channel_id=1, source_target_pairs={{0,1},{1,0},{2,3},{3,2},{4,5},{5,4},{6,7},{7,6},{8,9},{9,8},{10,11... | collective-permute-start | bytes 2949128 | tf_op jit(solution)/shard_map/ppermute | solution.py:561
  220.2 38.5 %copy-start.4 = (bf16[768,640]{1,0:T(8,128)(2,1)}, bf16[768,640]{1,0:T(8,128)(2,1)S(1)}, u32[]{:S(2)}) copy-start(bf16[768,640]{1,0:T(8,128)(2,1)S(1)} %collective-permute-done.31) | copy-start | bytes 2949124
  224.0 6.2 %copy-start.9 = (bf16[768,512]{1,0:T(8,128)(2,1)S(1)}, bf16[768,512]{1,0:T(8,128)(2,1)}, u32[]{:S(2)}) copy-start(bf16[768,512]{1,0:T(8,128)(2,1)} %copy-done.8) | copy-start | bytes 2359300
  232.5 24.3 %collective-permute-start.33 = (bf16[48,2304]{1,0:T(8,128)(2,1)S(1)}, bf16[48,2304]{1,0:T(8,128)(2,1)S(1)}, u32[]{:S(2)}, u32[]{:S(2)}) collective-permute-start(bf16[48,2304]{1,0:T(8,128)(2,1)S(1)} %get-tuple-element.221), channel_id=1, source_target_pairs={{0,8},{2,10},{4,12},{6,14},{8,0},{10,2},{12,4},{14,6},{16,24},{18,... | collective-permute-start | bytes 663560 | tf_op jit(solution)/shard_map/ppermute | solution.py:565
  237.4 19.4 %collective-permute-start.34 = (bf16[48,2304]{1,0:T(8,128)(2,1)S(1)}, bf16[48,2304]{1,0:T(8,128)(2,1)S(1)}, u32[]{:S(2)}, u32[]{:S(2)}) collective-permute-start(bf16[48,2304]{1,0:T(8,128)(2,1)S(1)} %get-tuple-element.222), channel_id=1, source_target_pairs={{0,16},{2,18},{4,20},{6,22},{8,24},{10,26},{12,28},{14,30},{16,0},... | collective-permute-start | bytes 663560 | tf_op jit(solution)/shard_map/ppermute | solution.py:565
  237.4 19.4 %collective-permute-start.35 = (bf16[48,2304]{1,0:T(8,128)(2,1)S(1)}, bf16[48,2304]{1,0:T(8,128)(2,1)S(1)}, u32[]{:S(2)}, u32[]{:S(2)}) collective-permute-start(bf16[48,2304]{1,0:T(8,128)(2,1)S(1)} %get-tuple-element.223), channel_id=1, source_target_pairs={{0,24},{2,26},{4,28},{6,30},{8,16},{10,18},{12,20},{14,22},{16,8},... | collective-permute-start | bytes 663560 | tf_op jit(solution)/shard_map/ppermute | solution.py:565
  239.9 17.0 %collective-permute-start.37 = (bf16[384,512]{1,0:T(8,128)(2,1)S(1)}, bf16[384,512]{1,0:T(8,128)(2,1)S(1)}, u32[]{:S(2)}, u32[]{:S(2)}) collective-permute-start(bf16[384,512]{1,0:T(8,128)(2,1)S(1)} %add_convert_fusion.5), channel_id=1, source_target_pairs={{0,2},{2,0},{4,6},{6,4},{8,10},{10,8},{12,14},{14,12},{16,18},{18,... | collective-permute-start | bytes 1179656 | tf_op jit(solution)/shard_map/ppermute | solution.py:565
  243.0 13.8 %collective-permute-start.36 = (bf16[384,640]{1,0:T(8,128)(2,1)S(1)}, bf16[384,640]{1,0:T(8,128)(2,1)S(1)}, u32[]{:S(2)}, u32[]{:S(2)}) collective-permute-start(bf16[384,640]{1,0:T(8,128)(2,1)S(1)} %add_convert_fusion.2), channel_id=1, source_target_pairs={{0,4},{2,6},{4,0},{6,2},{8,12},{10,14},{12,8},{14,10},{16,20},{18,... | collective-permute-start | bytes 1474568 | tf_op jit(solution)/shard_map/ppermute | solution.py:565
  243.0 13.8 %copy-start.10 = (bf16[768,512]{1,0:T(8,128)(2,1)S(1)}, bf16[768,512]{1,0:T(8,128)(2,1)}, u32[]{:S(2)}) copy-start(bf16[768,512]{1,0:T(8,128)(2,1)} %get-tuple-element.214) | copy-start | bytes 2359300
  257.7 1.9 collective-permute-start.40
  259.6 5.7 %collective-permute-start.41 = (bf16[384,128]{1,0:T(8,128)(2,1)S(1)}, bf16[384,128]{1,0:T(8,128)(2,1)S(1)}, u32[]{:S(2)}, u32[]{:S(2)}) collective-permute-start(bf16[384,128]{1,0:T(8,128)(2,1)S(1)} %add_convert_fusion.7), channel_id=1, source_target_pairs={{0,2},{2,0},{4,6},{6,4},{8,10},{10,8},{12,14},{14,12},{16,18},{18,... | collective-permute-start | bytes 294920 | tf_op jit(solution)/shard_map/ppermute | solution.py:565
  260.9 9.1 %collective-permute-start.39 = (bf16[192,640]{1,0:T(8,128)(2,1)S(1)}, bf16[192,640]{1,0:T(8,128)(2,1)S(1)}, u32[]{:S(2)}, u32[]{:S(2)}) collective-permute-start(bf16[192,640]{1,0:T(8,128)(2,1)S(1)} %add_convert_fusion.6), channel_id=1, source_target_pairs={{0,2},{2,0},{4,6},{6,4},{8,10},{10,8},{12,14},{14,12},{16,18},{18,... | collective-permute-start | bytes 737288 | tf_op jit(solution)/shard_map/ppermute | solution.py:565
  262.4 28.3 %collective-permute-start.38 = (f32[512,768]{1,0:T(8,128)}, f32[512,768]{1,0:T(8,128)S(1)}, u32[]{:S(2)}, u32[]{:S(2)}) collective-permute-start(f32[512,768]{1,0:T(8,128)} %get-tuple-element.227), channel_id=1, source_target_pairs={{0,1},{1,0},{2,3},{3,2},{4,5},{5,4},{6,7},{7,6},{8,9},{9,8},{10,11... | collective-permute-start | bytes 4718600 | tf_op jit(solution)/shard_map/ppermute | solution.py:561
  265.4 6.9 %collective-permute-start.42 = (bf16[192,640]{1,0:T(8,128)(2,1)S(1)}, bf16[192,640]{1,0:T(8,128)(2,1)S(1)}, u32[]{:S(2)}, u32[]{:S(2)}) collective-permute-start(bf16[192,640]{1,0:T(8,128)(2,1)S(1)} %fusion.4), channel_id=1, source_target_pairs={{0,4},{2,6},{4,0},{6,2},{8,12},{10,14},{12,8},{14,10},{16,20},{18,... | collective-permute-start | bytes 737288 | tf_op jit(solution)/shard_map/ppermute | solution.py:565
  272.5 7.9 %collective-permute-start.43 = (bf16[48,1280]{1,0:T(8,128)(2,1)S(1)}, bf16[48,1280]{1,0:T(8,128)(2,1)S(1)}, u32[]{:S(2)}, u32[]{:S(2)}) collective-permute-start(bf16[48,1280]{1,0:T(8,128)(2,1)S(1)} %get-tuple-element.291), channel_id=1, source_target_pairs={{0,8},{2,10},{4,12},{6,14},{8,0},{10,2},{12,4},{14,6},{16,24},{18,... | collective-permute-start | bytes 368648 | tf_op jit(solution)/shard_map/ppermute | solution.py:565
  275.0 7.2 %collective-permute-start.45 = (bf16[48,1280]{1,0:T(8,128)(2,1)S(1)}, bf16[48,1280]{1,0:T(8,128)(2,1)S(1)}, u32[]{:S(2)}, u32[]{:S(2)}) collective-permute-start(bf16[48,1280]{1,0:T(8,128)(2,1)S(1)} %get-tuple-element.292), channel_id=1, source_target_pairs={{0,24},{2,26},{4,28},{6,30},{8,16},{10,18},{12,20},{14,22},{16,8},... | collective-permute-start | bytes 368648 | tf_op jit(solution)/shard_map/ppermute | solution.py:565
  275.4 10.6 %collective-permute-start.44 = (bf16[48,1280]{1,0:T(8,128)(2,1)S(1)}, bf16[48,1280]{1,0:T(8,128)(2,1)S(1)}, u32[]{:S(2)}, u32[]{:S(2)}) collective-permute-start(bf16[48,1280]{1,0:T(8,128)(2,1)S(1)} %get-tuple-element.293), channel_id=1, source_target_pairs={{0,16},{2,18},{4,20},{6,22},{8,24},{10,26},{12,28},{14,30},{16,0},... | collective-permute-start | bytes 368648 | tf_op jit(solution)/shard_map/ppermute | solution.py:565
  277.2 13.6 %copy-start.2 = (f32[512,768]{1,0:T(8,128)S(1)}, f32[512,768]{1,0:T(8,128)}, u32[]{:S(2)}) copy-start(f32[512,768]{1,0:T(8,128)} %get-tuple-element.226) | copy-start | bytes 4718596
  (15 other events, 29.6 us)

commit v3 on v2

v3 whole, which is shorter than its diff:
```python
import functools

import jax
import jax.numpy as jnp
from jax import lax
from jax.experimental import pallas as pl
from jax.experimental.pallas import tpu as pltpu
from jax.sharding import PartitionSpec as P

HEAD_DIM = 64
LANES = 128
QB = 256
TB = 256
THETA = 160000.0
EPS = 1e-05
BF = jnp.bfloat16
F32 = jnp.float32

ORDER_A = (0, 4, 8, 12, 1, 5, 9, 13, 2, 6, 10, 14, 3, 7, 11, 15)
ORDER_B = (0, 4, 8, 12, 2, 6, 10, 14, 1, 5, 9, 13, 3, 7, 11, 15)


def nn(a, b):
    return lax.dot_general(a, b, (((1,), (0,)), ((), ())), preferred_element_type=F32)


def nt(a, b):
    return lax.dot_general(a, b, (((1,), (1,)), ((), ())), preferred_element_type=F32)


def tn(a, b):
    return lax.dot_general(a, b, (((0,), (0,)), ((), ())), preferred_element_type=F32)


def up_to(n):
    return -(-n // LANES) * LANES


def rotate(u, cos, sin, sign):
    lane = lax.broadcasted_iota(jnp.int32, u.shape, 1)
    half = HEAD_DIM // 2
    partner = jnp.where(
        (lane % HEAD_DIM) < half, pltpu.roll(u, LANES - half, 1), pltpu.roll(u, half, 1)
    )
    return u * cos + partner * sin if sign > 0 else u * cos - partner * sin


def norm(x):
    center = x - jnp.mean(x, axis=-1, keepdims=True)
    inverse = lax.rsqrt(jnp.mean(center * center, axis=-1, keepdims=True) + EPS)
    return center * inverse, inverse


def norm_back(grad, xhat, inverse, gain):
    z = grad * gain
    inner = z - jnp.mean(z, axis=-1, keepdims=True) - xhat * jnp.mean(z * xhat, axis=-1, keepdims=True)
    return inverse * inner


def staged(count, stages):
    live = [None] * len(stages)
    for step in range(count + len(stages) - 1):
        new = [None] * len(stages)
        for s, stage in enumerate(stages):
            if 0 <= step - s < count:
                new[s] = stage(step - s, live[s - 1] if s else None)
        live = new


def after(x, *deps):
    return lax.optimization_barrier((x, deps))[0]


def call(kernel, name, us, vmem, operands, out_shape, scratch=()):
    spaces = [space for _, space in operands]
    return pl.pallas_call(
        kernel,
        in_specs=[pl.BlockSpec(memory_space=space) for space in spaces],
        out_specs=[pl.BlockSpec(memory_space=pltpu.VMEM)] * len(out_shape),
        scratch_shapes=list(scratch),
        out_shape=[jax.ShapeDtypeStruct(shape, dtype) for shape, dtype in out_shape],
        compiler_params=pltpu.CompilerParams(vmem_limit_bytes=vmem << 20),
        cost_estimate=pl.CostEstimate(flops=int(us * 1.15e9), transcendentals=0, bytes_accessed=int(us * 1e6)),
        name=name,
    )(*[array for array, _ in operands])


def vector(*arrays):
    return [(a, pltpu.VMEM) for a in arrays]


def stored(*arrays):
    return [(a, pltpu.HBM) for a in arrays]


def scalar(*arrays):
    return [(a, pltpu.SMEM) for a in arrays]


def load_weights(info, pieces, layout, rows, dest, sems):
    copies = []
    for ref, (r, col, order) in zip(pieces, layout, strict=True):
        cols = pl.ds(col, ref.shape[1])
        if order is None:
            copies.append((ref, dest.at[r, :, cols]))
            continue
        for i, k in enumerate(order):
            row = pl.multiple_of((info[1] ^ k) * rows, rows)
            copies.append((ref.at[pl.ds(i * rows, rows), :], dest.at[r, pl.ds(row, rows), cols]))
    copies = [pltpu.make_async_copy(a, b, sems.at[i]) for i, (a, b) in enumerate(copies)]
    for c in copies:
        c.start()
    for c in copies:
        c.wait()


def copies_of(layout):
    return sum(1 if order is None else len(order) for _, _, order in layout)


def store_rows(info, value_ref, out_ref, cols, order, rows):
    if order is None:
        out_ref[:, cols] = value_ref[...].astype(BF)
        return
    for i, k in enumerate(order):
        row = pl.multiple_of((info[1] ^ k) * rows, rows)
        out_ref[i * rows : (i + 1) * rows, cols] = value_ref[pl.ds(row, rows), :].astype(BF)


def token_blocks(info, half, run):
    for part in range(2):
        first = (info[0] if part == 0 else 1 - info[0]) * half

        @pl.loop(0, half // TB)
        def _(b, part=part, first=first):
            here = pl.multiple_of(b * TB, TB)
            run(part == 0, pl.ds(here, TB), pl.ds(pl.multiple_of(first + here, TB), TB))


def qkv_kernel(info, *refs, layout, rows, width):
    n = len(layout)
    pieces, (x_ref, recv_ref, cos_ref, sin_ref, qkv_ref, h_ref, gain_ref, w_ref, sems) = refs[:n], refs[n:]
    load_weights(info, pieces, layout, rows, w_ref, sems)
    gain_ref[...] = w_ref[0, :, 3 * width :].astype(F32).T[:8]

    def run(held, here, at):
        x = (x_ref[info[0], here, :] if held else recv_ref[here, :]).astype(F32)
        xhat, _ = norm(x)
        h = (xhat * gain_ref[0:1, :]).astype(BF)
        h_ref[at, :] = h
        cos, sin = cos_ref[at, :], sin_ref[at, :]
        for r in range(2):
            raw = nn(h, w_ref[r, :, : 3 * width])
            for b in range(2 * width // LANES):
                cols = slice(b * LANES, (b + 1) * LANES)
                u = rotate(raw[:, cols], cos, sin, 1)
                if b < width // LANES:
                    u = u * HEAD_DIM**-0.5
                qkv_ref[r, at, cols] = u.astype(BF)
            qkv_ref[r, at, 2 * width :] = raw[:, 2 * width :].astype(BF)

    token_blocks(info, recv_ref.shape[0], run)


def qkv_call(info, pieces, layout, rows, width, x, recv, cos, sin):
    d, s = x.shape[2], cos.shape[0]
    return call(
        functools.partial(qkv_kernel, layout=layout, rows=rows, width=width),
        "qkv",
        12,
        16,
        scalar(info) + stored(*pieces) + vector(x, recv, cos, sin),
        [((2, s, 3 * width), BF), ((s, d), BF), ((8, d), F32)],
        [pltpu.VMEM((2, d, 3 * width + LANES), BF), pltpu.SemaphoreType.DMA((copies_of(layout),))],
    )


def same_segment(col, row):
    parts = [
        jnp.where(col == row[:, i * LANES : (i + 1) * LANES], 0.0, -1e30).astype(F32)
        for i in range(row.shape[1] // LANES)
    ]
    return jnp.concatenate(parts, 1)


def by_range(ranges, i, blocks, run):
    for n in range(1, blocks + 1):

        @pl.when(ranges[i, 1] == n)
        def _(n=n):
            run(n, pl.ds(pl.multiple_of(ranges[i, 0], QB) if n < blocks else 0, n * QB))


def head(h):
    return slice(h * HEAD_DIM, (h + 1) * HEAD_DIM)


def attend_kernel(ranges, col_ref, row_ref, qkv_ref, o_ref, lse_ref, vt_ref):
    s, width = o_ref.shape[1:]
    heads, blocks = width // HEAD_DIM, s // QB

    @pl.loop(0, 2 * blocks)
    def _(step):
        r, i = step // blocks, step % blocks
        at = pl.ds(pl.multiple_of(i * QB, QB), QB)

        @pl.when(i == 0)
        def _():
            vt_ref[...] = qkv_ref[r, :, 2 * width :].T

        def run(n, keys):
            bias = same_segment(col_ref[keys, :], row_ref[0:1, at])
            outs, sums = [None] * heads, [None] * heads

            def scores(h, _):
                q = qkv_ref[r, at, head(h)].T
                x = nn(qkv_ref[r, keys, width + h * HEAD_DIM : width + (h + 1) * HEAD_DIM], q) + bias
                return x, jnp.max(x, axis=0, keepdims=True)

            def expo(h, a):
                e = jnp.exp(a[0] - a[1])
                return e.astype(BF), jnp.sum(e, axis=0, keepdims=True), a[1]

            def out(h, a):
                outs[h] = nn(vt_ref[head(h), keys], a[0]) * (1.0 / a[1])
                sums[h] = a[2] + jnp.log(a[1])

            staged(heads, [scores, expo, out])
            o_ref[r, at, :] = jnp.concatenate(outs, axis=0).T.astype(BF)
            for h in range(heads):
                lse_ref[r, h : h + 1, at] = sums[h]

        by_range(ranges, i, blocks, run)


def attend_call(ranges, col, row, qkv):
    _, s, w3 = qkv.shape
    width = w3 // 3
    return call(
        attend_kernel,
        "attend",
        20,
        20,
        scalar(ranges) + vector(col, row, qkv),
        [((2, s, width), BF), ((2, 8, s), F32)],
        [pltpu.VMEM((width, s), BF)],
    )


def attend_back_kernel(
    ranges, col_ref, row_ref, qkv_ref, do_ref, o_ref, lse_ref, cos_ref, sin_ref,
    dq_ref, dkv_ref, qt_ref, dot_ref, dqt_ref, delta_ref, *, r,
):
    s, width = dq_ref.shape
    heads, blocks = width // HEAD_DIM, s // QB
    qt_ref[...] = qkv_ref[r, :, :width].T
    dqt_ref[...] = jnp.zeros_like(dqt_ref)
    for i in range(blocks):
        at = slice(i * QB, (i + 1) * QB)
        dot = do_ref[at, :].astype(F32).T
        dot_ref[:, at] = dot.astype(BF)
        both = dot * o_ref[r, at, :].astype(F32).T
        for h in range(heads):
            delta_ref[h : h + 1, at] = jnp.sum(both[head(h)], axis=0, keepdims=True)

    @pl.loop(0, blocks)
    def _(c):
        here = pl.ds(pl.multiple_of(c * QB, QB), QB)

        def run(n, queries):
            bias = same_segment(col_ref[here, :], row_ref[0:1, queries])
            dks, dvs = [None] * heads, [None] * heads

            def part(h, c):
                return qkv_ref[r, here, c * width + h * HEAD_DIM : c * width + (h + 1) * HEAD_DIM]

            def products(h, _):
                return (
                    nn(part(h, 1), qt_ref[head(h), queries]) + bias,
                    nn(part(h, 2), dot_ref[head(h), queries]),
                )

            def scores(h, a):
                p = jnp.exp(a[0] - lse_ref[r, h : h + 1, queries])
                return p.astype(BF), (p * (a[1] - delta_ref[h : h + 1, queries])).astype(BF)

            def grads(h, a):
                dvs[h] = nt(dot_ref[head(h), queries], a[0])
                dks[h] = nt(qt_ref[head(h), queries], a[1])
                dqt_ref[head(h), queries] += nn(part(h, 1).T, a[1])

            staged(heads, [products, scores, grads])
            cos, sin = cos_ref[here, :], sin_ref[here, :]
            for b in range(width // LANES):
                dk = jnp.concatenate(dks[2 * b : 2 * b + 2], 0).T
                dv = jnp.concatenate(dvs[2 * b : 2 * b + 2], 0).T
                dkv_ref[here, b * LANES : (b + 1) * LANES] = rotate(dk, cos, sin, -1).astype(BF)
                dkv_ref[here, width + b * LANES : width + (b + 1) * LANES] = dv.astype(BF)

        by_range(ranges, c, blocks, run)

    for i in range(blocks):
        at = slice(i * QB, (i + 1) * QB)
        for b in range(width // LANES):
            cols = slice(b * LANES, (b + 1) * LANES)
            dq = dqt_ref[cols, at].T * HEAD_DIM**-0.5
            dq_ref[at, cols] = rotate(dq, cos_ref[at, :], sin_ref[at, :], -1).astype(BF)


def attend_back_call(r, ranges, col, row, qkv, do, o, lse, cos, sin):
    _, s, w3 = qkv.shape
    width = w3 // 3
    return call(
        functools.partial(attend_back_kernel, r=r),
        "attend_back",
        18,
        24,
        scalar(ranges) + vector(col, row, qkv, do, o, lse, cos, sin),
        [((s, width), BF), ((s, 2 * width), BF)],
        [
            pltpu.VMEM((width, s), BF),
            pltpu.VMEM((width, s), BF),
            pltpu.VMEM((width, s), F32),
            pltpu.VMEM((8, s), F32),
        ],
    )


def mlp_kernel(info, *refs, layout, rows, width, units):
    n = len(layout)
    (x_ref, xr_ref, dy_ref, dyr_ref, o_ref, gain_ref,
     own_ref, other_ref, dr_ref, do0_ref, do1_ref, h_ref, dyo_ref, da_ref,
     dgu0_ref, dgu1_ref, m0_ref, m1_ref, gg_ref,
     w_ref, sems) = refs[n:]
    load_weights(info, refs[:n], layout, rows, w_ref, sems)
    gg_ref[...] = jnp.zeros_like(gg_ref)
    c0, c1, c2, c3 = width, width + units, width + 2 * units, width + 3 * units
    gain = gain_ref[1:2, :]

    def run(held, here, at):
        x = (x_ref[info[0], here, :] if held else xr_ref[here, :]).astype(F32)
        dyb = dy_ref[info[0], here, :] if held else dyr_ref[here, :]
        dyo_ref[at, :] = dyb
        r1 = x + nt(o_ref[0, at, :], w_ref[0, :, :c0]) + nt(o_ref[1, at, :], w_ref[1, :, :c0])
        xhat, inverse = norm(r1)
        h = (xhat * gain).astype(BF)
        h_ref[at, :] = h
        outs, dhs = [], []

        def products(r, _):
            return nn(h, w_ref[r, :, c0:c1]), nn(h, w_ref[r, :, c1:c2]), nn(dyb, w_ref[r, :, c2:c3])

        def units_of(r, a):
            gate, up, dm = a
            phi = 0.5 + 0.5 * lax.erf(gate * 0.7071067811865476)
            density = jnp.exp(-0.5 * gate * gate) * 0.3989422804014327
            gelu = gate * phi
            m = (gelu * up).astype(BF)
            dgate = (dm * up * (phi + gate * density)).astype(BF)
            dup = (dm * gelu).astype(BF)
            (m0_ref, m1_ref)[r][at, :] = m
            dgu_ref = (dgu0_ref, dgu1_ref)[r]
            dgu_ref[at, :units] = dgate
            dgu_ref[at, units:] = dup
            return m, dgate, dup

        def sums(r, a):
            outs.append(nt(a[0], w_ref[r, :, c2:c3]))
            dhs.append(nt(a[1], w_ref[r, :, c0:c1]) + nt(a[2], w_ref[r, :, c1:c2]))

        staged(2, [products, units_of, sums])
        out = (r1 + (outs[0] + outs[1])).astype(BF)
        (own_ref if held else other_ref)[here, :] = out
        dh = dhs[0] + dhs[1]
        gg_ref[0:1, :] += jnp.sum(dh * xhat, axis=0, keepdims=True)
        dr = dyb.astype(F32) + norm_back(dh, xhat, inverse, gain)
        dr_ref[at, :] = dr
        da = dr.astype(BF)
        da_ref[at, :] = da
        for r in range(2):
            (do0_ref, do1_ref)[r][at, :] = nn(da, w_ref[r, :, :c0]).astype(BF)

    token_blocks(info, xr_ref.shape[0], run)


def mlp_call(info, pieces, layout, rows, width, units, x, xr, dy, dyr, o, gains):
    d, s = x.shape[2], o.shape[1]
    return call(
        functools.partial(mlp_kernel, layout=layout, rows=rows, width=width, units=units),
        "mlp",
        30,
        24,
        scalar(info) + stored(*pieces) + vector(x, xr, dy, dyr, o, gains),
        [
            ((s // 2, d), BF),
            ((s // 2, d), BF),
            ((s, d), F32),
            ((s, width), BF),
            ((s, width), BF),
            ((s, d), BF),
            ((s, d), BF),
            ((s, d), BF),
            ((s, 2 * units), BF),
            ((s, 2 * units), BF),
            ((s, units), BF),
            ((s, units), BF),
            ((8, d), F32),
        ],
        [pltpu.VMEM((2, d, width + 3 * units), BF), pltpu.SemaphoreType.DMA((copies_of(layout),))],
    )


def weight_grad_kernel(info, *refs, leads, products, orders, rows):
    n = len(leads)
    outs, g_ref = refs[n : n + 2], refs[n + 2]
    for a, b, col in products:
        left, right = refs[a], refs[b]
        for out_ref, order, base in zip(outs, orders, (0, outs[0].shape[1])):
            start, stop = max(col, base), min(col + right.shape[-1], base + out_ref.shape[1])
            if start >= stop:
                continue
            cols = slice(start - col, stop - col)
            value = g_ref.at[:, pl.ds(0, stop - start)]
            value[...] = tn(left[...], right[:, cols] if leads[b] is None else right[leads[b], :, cols]).astype(BF)
            store_rows(info, value, out_ref, slice(start - base, stop - base), order, rows)


def weight_grad_call(name, us, info, rows, orders, operands, products, split, total):
    arrays = [a for a, _ in operands]
    d = arrays[0].shape[-1]
    widest = max(a.shape[-1] for a in arrays)
    leads = [lead for _, lead in operands]
    return call(
        functools.partial(weight_grad_kernel, leads=leads, products=products, orders=orders, rows=rows),
        name,
        us,
        16,
        scalar(info) + vector(*arrays),
        [((d, split), BF), ((d, total - split), BF)],
        [pltpu.VMEM((d, widest), BF)],
    )


def input_kernel(info, *refs, layout, rows, width, order):
    n = len(layout)
    (x_ref, xr_ref, dq0_ref, dkv0_ref, dq1_ref, dkv1_ref, dr_ref, gain_ref, gg_ref,
     own_ref, other_ref, gcol_ref, w_ref, acc_ref, col_ref, sems) = refs[n:]
    load_weights(info, refs[:n], layout, rows, w_ref, sems)
    acc_ref[...] = jnp.zeros_like(acc_ref)
    acc_ref[1:2, :] = gg_ref[0:1, :]
    gain = gain_ref[0:1, :]

    def run(held, here, at):
        x = (x_ref[info[0], here, :] if held else xr_ref[here, :]).astype(F32)
        xhat, inverse = norm(x)
        dh = nt(dq0_ref[at, :], w_ref[0, :, :width]) + nt(dq1_ref[at, :], w_ref[1, :, :width])
        dh = dh + nt(dkv0_ref[at, :], w_ref[0, :, width : 3 * width])
        dh = dh + nt(dkv1_ref[at, :], w_ref[1, :, width : 3 * width])
        acc_ref[0:1, :] += jnp.sum(dh * xhat, axis=0, keepdims=True)
        (own_ref if held else other_ref)[here, :] = dr_ref[at, :] + norm_back(dh, xhat, inverse, gain)

    token_blocks(info, xr_ref.shape[0], run)
    col_ref[...] = acc_ref[...].T
    store_rows(info, col_ref, gcol_ref, slice(0, LANES), order, rows)


def input_call(info, pieces, layout, rows, width, x, xr, draw, dr, gains, gg, order):
    d, s = x.shape[2], dr.shape[0]
    return call(
        functools.partial(input_kernel, layout=layout, rows=rows, width=width, order=order),
        "input_back",
        10,
        16,
        scalar(info) + stored(*pieces) + vector(x, xr, *draw, dr, gains, gg),
        [((s // 2, d), F32), ((s // 2, d), F32), ((d, LANES), BF)],
        [
            pltpu.VMEM((2, d, 3 * width + LANES), BF),
            pltpu.VMEM((LANES, d), F32),
            pltpu.VMEM((d, LANES), F32),
            pltpu.SemaphoreType.DMA((copies_of(layout),)),
        ],
    )


def swap(x):
    return lax.ppermute(x, "tensor", [(0, 1), (1, 0)])


def peer(x, k):
    return lax.ppermute(x, "dp", [(i, i ^ k) for i in range(16)])


def under(x, run, *sends):
    x, arrays = after((x, [a for _, a in sends]))
    got = [f(a) for (f, _), a in zip(sends, arrays)]
    return after((run(x), got))


def to(k):
    return lambda x: peer(x, k)


def add(*terms):
    return functools.reduce(jnp.add, [t.astype(F32) for t in terms])


class Gather:
    def __init__(self, split):
        self.split = split

    def near(self, block):
        self.ab = block[:, : self.split], block[:, self.split :]
        return [(to(k), x) for k, x in zip((1, 2), self.ab)]

    def far(self, got):
        self.ab = [jnp.concatenate(x, 0) for x in zip(self.ab, got)]
        return [(to(k), x) for k, x in zip((2, 1), self.ab)]

    def pieces(self, got, theirs, got_theirs):
        orders = (0, ORDER_A), (self.split, ORDER_B)
        where = [(col, order[8 * i : 8 * i + 8]) for i in range(2) for col, order in orders]
        layout = [(r, *w) for r in range(2) for w in where]
        return [*self.ab, *got, *theirs, *got_theirs], layout


def half_sends(terms, ks):
    n = terms[0][0].shape[0] // 2
    keep = [[t[:n] for t in ts] for ts in terms]
    return keep, [(to(k), add(*(t[n:] for t in ts)).astype(BF)) for k, ts in zip(ks, terms)]


def joined(keep, got):
    return [ts + [g] for ts, g in zip(keep, got)]


def last_sends(terms):
    both = jnp.concatenate([add(*ts) for ts in terms], 1)
    n = both.shape[0] // 4
    send = both[n:].astype(BF)
    return both[:n], [(to(4 * i), send[(i - 1) * n : i * n]) for i in (1, 2, 3)]


def gather_plain(slab):
    whole = lax.all_gather(slab, "dp", axis=0, tiled=True)
    return [whole, swap(whole)], [(0, 0, None), (1, 0, None)]


def scatter_plain(a, b):
    both = jnp.concatenate([add(*a), add(*b)], 1)
    return lax.psum_scatter(both, "dp", scatter_dimension=0, tiled=True)


def local(
    hidden_in, segment_ids, qkv_weight, out_weight, mlp_weight, down_weight, attn_gain, mlp_gain,
    cotangent, *, cube,
):
    t, me = lax.axis_index("tensor"), lax.axis_index("dp")
    info = jnp.stack([t, me]).astype(jnp.int32)
    rows, width = qkv_weight.shape[1:]
    d = hidden_in.shape[2]
    units_here = mlp_weight.shape[2]
    units = up_to(units_here)
    s = segment_ids.shape[1]

    def placed(own, got):
        first = t == 0
        return jnp.stack([jnp.where(first, own, got), jnp.where(first, got, own)])

    def other(x):
        return lax.dynamic_index_in_dim(x, 1 - t, 0, False)

    x_recv = swap(other(hidden_in))
    gain_cols = jnp.stack([attn_gain, mlp_gain], 1)
    gain_cols = jnp.pad(gain_cols, ((0, 0), (0, LANES - 2)))
    slab1 = jnp.concatenate([qkv_weight[0], qkv_weight[1], qkv_weight[2], gain_cols], 1)

    def wide(w):
        return jnp.pad(w, ((0, 0), (0, units - units_here)))

    def second_slab(out_weight, mlp_weight, down_weight):
        return jnp.concatenate(
            [out_weight.T, wide(mlp_weight[0]), wide(mlp_weight[1]), wide(down_weight.T)], 1
        )

    weights2 = out_weight, mlp_weight, down_weight
    total1, total2 = slab1.shape[1], width + 3 * units
    split1, split2 = total1 // 2 // LANES * LANES, total2 // 2 // LANES * LANES
    seg = lax.dynamic_index_in_dim(segment_ids, t, 0, False)
    index = jnp.arange(s, dtype=jnp.int32)
    start = jnp.sum((seg[None, :] < seg[:, None]).astype(jnp.int32), axis=1)
    freqs = THETA ** (-2.0 * jnp.arange(HEAD_DIM // 2, dtype=F32) / HEAD_DIM)
    angles = (index - start).astype(F32)[:, None] * freqs[None, :]
    cos, sin = jnp.cos(angles), jnp.sin(angles)
    cos = jnp.concatenate([cos, cos, cos, cos], 1)
    sin = jnp.concatenate([-sin, sin, -sin, sin], 1)
    col = jnp.broadcast_to(seg[:, None], (s, LANES))
    row = jnp.broadcast_to(seg[None, :], (8, s))
    ends = seg.reshape(s // QB, QB)
    first, last = ends[:, 0], ends[:, -1]
    meet = (first[:, None] <= last[None, :]) & (first[None, :] <= last[:, None])
    block = jnp.arange(s // QB, dtype=jnp.int32)[None, :]
    low = jnp.min(jnp.where(meet, block, s), axis=1)
    high = jnp.max(jnp.where(meet, block, -1), axis=1)
    ranges = jnp.stack([low * QB, high - low + 1], 1).astype(jnp.int32)

    def project(w1):
        return qkv_call(info, w1, layout1, rows, width, hidden_in, x_recv, cos, sin)

    def attend(qkv):
        return attend_call(ranges, col, row, qkv)

    if cube:
        g1 = Gather(split1)
        g2 = Gather(split2)
        sends = g1.near(jnp.concatenate([slab1] + [peer(slab1, k) for k in (4, 8, 12)], 0))
        (weights2, x_recv), g1.ab = after(((weights2, x_recv), [x for _, x in sends]))
        got = [f(x) for (f, _), x in zip(sends, g1.ab)]
        slab2 = second_slab(*weights2)
        block2 = jnp.concatenate([slab2] + [peer(slab2, k) for k in (4, 8, 12)], 0)
        sends = g1.far(got)
        got = [f(x) for f, x in sends]
        got, g1.ab = after((got, g1.ab))
        w1, layout1 = g1.pieces(got, [swap(x) for x in g1.ab], [swap(x) for x in got])
        (qkv, h1, gains), (*got, dy_recv) = under(
            w1, project, *g2.near(block2), (swap, other(cotangent))
        )
        far = g2.far(got)
        (o, lse), got = under(qkv, attend, *far, *((swap, x) for _, x in far))
        w2, layout2 = g2.pieces(got[:2], got[2:], [swap(x) for x in got[:2]])
    else:
        w1, layout1 = gather_plain(slab1)
        w2, layout2 = gather_plain(second_slab(*weights2))
        dy_recv = swap(other(cotangent))
        qkv, h1, gains = project(w1)
        o, lse = attend(qkv)
    out_own, out_other, dr, do0, do1, h2, dy, da, dgu0, dgu1, m0, m1, gg = mlp_call(
        info, w2, layout2, rows, width, units, hidden_in, x_recv, cotangent, dy_recv, o, gains
    )
    orders = (ORDER_A, ORDER_B) if cube else (None, None)

    def grads2(r):
        return lambda o: weight_grad_call(
            "mlp_weight_grad", 10, info, rows, orders,
            [(da, None), (h2, None), (dy, None), (o, r), ((dgu0, dgu1)[r], None), ((m0, m1)[r], None)],
            [(0, 3, 0), (1, 4, width), (2, 5, width + 2 * units)], split2, total2,
        )

    def grads1(draw):
        return weight_grad_call(
            "qkv_weight_grad", 6, info, rows, orders,
            [(h1, None), (draw[0], None), (draw[1], None)],
            [(0, 1, 0), (0, 2, width)], split1, total1 - LANES,
        )

    def back(r):
        return lambda do: attend_back_call(r, ranges, col, row, qkv, do, o, lse, cos, sin)

    def input_back(dr):
        return input_call(
            info, w1, layout1, rows, width, hidden_in, x_recv, (*draw0, *draw1), dr, gains, gg, orders[1]
        )

    sent = grads2(1)(o)
    mine, (*theirs, out_recv) = under(o, grads2(0), *((swap, g) for g in sent), (swap, out_other))
    layer_out = placed(out_own, out_recv)
    sums2 = [[a, b] for a, b in zip(mine, theirs)]
    if cube:
        keep, sends = half_sends(sums2, (2, 1))
        draw1, got = under(do1, back(1), *sends)
        keep, sends = half_sends(joined(keep, got), (1, 2))
        do0, sends2 = after((do0, [x for _, x in sends]))
        sent = grads1(after(draw1, sends2))
        draw0, got = under(
            after(do0, sent), back(0), *((f, x) for (f, _), x in zip(sends, sends2)), *((swap, g) for g in sent)
        )
        keep2, sends2 = last_sends(joined(keep, got[:2]))
        draw0, last = after((draw0, [x for _, x in sends2]))
        mine = grads1(draw0)
        keep, sends = half_sends([[a, b] for a, b in zip(mine, got[2:])], (2, 1))
        (in_own, in_other, gcol), got = under(
            dr, input_back, *((f, x) for (f, _), x in zip(sends2, last)), *sends
        )
        sum2 = add(keep2, *got[:3])
        keep, sends = half_sends(joined(keep, got[3:]), (1, 2))

        def gain_sums(gcol):
            both = add(gcol, swap(gcol))
            for k in (1, 2):
                n = both.shape[0] // 2
                both = add(both[:n], peer(both[n:].astype(BF), k))
            return both

        gain_sum, (*got, in_recv) = under(gcol, gain_sums, *sends, (swap, in_other))
        keep = joined(keep, got)
        keep, sends = last_sends([keep[0], [jnp.concatenate([add(*keep[1]), gain_sum], 1)]])
        input_grad, got = under(in_recv, lambda got: placed(in_own, got), *sends)
        sum1 = add(keep, *got)
    else:
        sum2 = scatter_plain(*sums2)
        draw1, draw0 = back(1)(do1), back(0)(do0)
        theirs = [swap(g) for g in grads1(draw1)]
        mine = grads1(draw0)
        in_own, in_other, gcol = input_back(dr)
        input_grad = placed(in_own, swap(in_other))
        b = [jnp.concatenate([g, c], 1) for g, c in zip((mine[1], theirs[1]), (gcol, swap(gcol)))]
        sum1 = scatter_plain((mine[0], theirs[0]), b)
    qkv_grad = sum1[:, : 3 * width].reshape(rows, 3, width).transpose(1, 0, 2)
    c = width
    proj_grad = sum2[:, :c].T
    mlp_grad = jnp.stack([sum2[:, c : c + units_here], sum2[:, c + units : c + units + units_here]])
    down_grad = sum2[:, c + 2 * units : c + 2 * units + units_here].T
    return (
        layer_out,
        input_grad,
        qkv_grad,
        proj_grad,
        mlp_grad,
        down_grad,
        sum1[:, 3 * width],
        sum1[:, 3 * width + 1],
    )


def solution(mesh):
    rows = P(None, ("dp", "tensor"), None)
    in_specs = (
        rows,
        P(None, "dp"),
        P(None, "dp", "tensor"),
        P("tensor", "dp"),
        P(None, "dp", "tensor"),
        P("tensor", "dp"),
        P("dp"),
        P("dp"),
        rows,
    )
    out_specs = (
        rows,
        rows,
        P(None, "dp", "tensor"),
        P("tensor", "dp"),
        P(None, "dp", "tensor"),
        P("tensor", "dp"),
        P("dp"),
        P("dp"),
    )
    cube = mesh.shape["dp"] == 16
    return jax.shard_map(
        functools.partial(local, cube=cube), mesh=mesh, in_specs=in_specs, out_specs=out_specs, check_vma=False
    )
```

time: 299 us -> 253 us (0.85)
  Pallas kernels: 146 us -> 113 us
  waiting for transfers between devices: 50.1 us -> 40.9 us
  local copies, waits for them, and re-layouts: 15.3 us -> 21.3 us
  other arithmetic: 24.5 us -> 18.7 us
    pallas_call x10, Pallas kernels: 146 us -> 113 us  [call(): pl.pallas_call(kernel, in_specs=[pl.BlockSpec(memory_space=space) for spa...]
    ppermute x29 -> x30, waiting for transfers between devices: 44.5 us -> 34.6 us  [peer(): return lax.ppermute(x, 'dp', [(i, i ^ k) for i in range(16)])]
    unnamed x72 -> x99, local copies, waits for them, and re-layouts: 5.15 us -> 14.1 us
    ppermute x29 -> x30, starting transfers between devices: 51.9 us -> 50 us  [peer(): return lax.ppermute(x, 'dp', [(i, i ^ k) for i in range(16)])]
    convert_element_type x7 -> x8, other arithmetic: 8.3 us -> 6.43 us  [half_sends(): add(*(t[n:] for t in ts)).astype(BF)]
  transfers between devices with their start and end apart: 46 -> 47, of which waited for: 17 -> 21; matrix products, arithmetic and copies ran while one was open for 7% -> 6% of each run, Pallas kernels for 31% -> 29%
where the time goes in v3:
time: 253 us; the launch traced here: 250 us
  Pallas kernels  113 us (45%)
  starting transfers between devices  54.2 us (21%)
  waiting for transfers between devices  40.9 us (16%)
  local copies, waits for them, and re-layouts  21.3 us (8%)
  other arithmetic  18.7 us (7%)
    pallas_call x10, Pallas kernels, call(): pl.pallas_call(kernel, in_specs=[pl.BlockSpec(memory_space=space) for spa...  113 us
    ppermute x30, starting transfers between devices, peer(): return lax.ppermute(x, 'dp', [(i, i ^ k) for i in range(16)])  50 us
    ppermute x30, waiting for transfers between devices, peer(): return lax.ppermute(x, 'dp', [(i, i ^ k) for i in range(16)])  34.6 us
    unnamed x99, local copies, waits for them, and re-layouts  14.1 us
    convert_element_type x8, other arithmetic, half_sends(): add(*(t[n:] for t in ts)).astype(BF)  6.43 us
    ppermute x17, waiting for transfers between devices, swap(): return lax.ppermute(x, 'tensor', [(0, 1), (1, 0)])  6.29 us
  transfers between devices with their start and end apart: 47, of which 21 were waited for; matrix products, arithmetic and copies ran while one was open for 6% of the time, Pallas kernels for 29%

profile of v3, /device:TPU:0, one launch (start us, length us, event | category | flops | bytes accessed | tf_op | source)
XLA Modules:
  0.0 249.9 jit_solution(4619817006691199851)
XLA Ops:
  1.4 0.8 slice_bitcast_fusion.8
  2.3 5.1 %collective-permute-start.3 = (bf16[48,1280]{1,0:T(8,128)(2,1)S(1)}, bf16[48,1280]{1,0:T(8,128)(2,1)S(1)}, u32[]{:S(2)}, u32[]{:S(2)}) collective-permute-start(bf16[48,1280]{1,0:T(8,128)(2,1)S(1)} %pad_maximum_fusion.12), channel_id=1, source_target_pairs={{0,24},{2,26},{4,28},{6,30},{8,16},{10,18},{12,20},{14,22},{16,8},... | collective-permute-start | bytes 368648 | tf_op jit(solution)/shard_map/ppermute | solution.py:490
  8.1 2.1 dynamic-slice_bitcast_fusion.1
  12.6 1.9 fusion.7
  15.2 2.6 %collective-permute-done.2 = bf16[48,1280]{1,0:T(8,128)(2,1)S(1)} collective-permute-done((bf16[48,1280]{1,0:T(8,128)(2,1)S(1)}, bf16[48,1280]{1,0:T(8,128)(2,1)S(1)}, u32[]{:S(2)}, u32[]{:S(2)}) %collective-permute-start.2) | collective-permute-done | bytes 122912 | tf_op jit(solution)/shard_map/ppermute | solution.py:490
  18.0 1.6 collective-permute-start.9
  19.6 2.5 %collective-permute-start.6 = (bf16[48,2304]{1,0:T(8,128)(2,1)S(1)}, bf16[48,2304]{1,0:T(8,128)(2,1)S(1)}, u32[]{:S(2)}, u32[]{:S(2)}) collective-permute-start(bf16[48,2304]{1,0:T(8,128)(2,1)S(1)} %pad_maximum_fusion.11), channel_id=1, source_target_pairs={{0,24},{2,26},{4,28},{6,30},{8,16},{10,18},{12,20},{14,22},{16,8},... | collective-permute-start | bytes 663560 | tf_op jit(solution)/shard_map/ppermute | solution.py:490
  22.2 1.9 collective-permute-start.4
  24.1 1.5 collective-permute-start.7
  25.7 1.0 collective-permute-start.10
  26.7 6.3 %collective-permute-done.7 = bf16[192,640]{1,0:T(8,128)(2,1)S(1)} collective-permute-done((bf16[192,640]{1,0:T(8,128)(2,1)S(1)}, bf16[192,640]{1,0:T(8,128)(2,1)S(1)}, u32[]{:S(2)}, u32[]{:S(2)}) %collective-permute-start.7) | collective-permute-done | bytes 245792 | tf_op jit(solution)/shard_map/ppermute | solution.py:490
  34.1 5.8 %collective-permute-done.5 = bf16[48,2304]{1,0:T(8,128)(2,1)S(1)} collective-permute-done((bf16[48,2304]{1,0:T(8,128)(2,1)S(1)}, bf16[48,2304]{1,0:T(8,128)(2,1)S(1)}, u32[]{:S(2)}, u32[]{:S(2)}) %collective-permute-start.5) | collective-permute-done | bytes 221216 | tf_op jit(solution)/shard_map/ppermute | solution.py:490
  40.5 1.4 collective-permute-done.8.refs_2_
  43.0 0.8 collective-permute-done.11.refs_4_
  45.2 0.7 collective-permute-done.14.refs_7_
  45.9 1.5 collective-permute-start.15
  47.9 8.5 %qkv.1 = (bf16[2,1024,1152]{2,1,0:T(8,128)(2,1)S(1)}, bf16[1024,768]{1,0:T(8,128)(2,1)S(1)}, f32[8,768]{1,0:T(8,128)S(1)}) custom-call(s32[2]{0:T(128)S(1)} %pad_add_fusion.1.info, bf16[384,640]{1,0:T(8,128)(2,1)S(1)} %constant_dynamic-update-slice_fusion.refs_0_, bf16[384,640]{1,0:T(8,128)(2,1)S(1)} %constant_dynamic-update-slice_fusion.2.refs_1_, ...), custom_call_target="tpu_custom_call" | custom-call | flops 13799999488 | bytes 12000000 | tf_op jit(solution)/shard_map/qkv/pallas_call | solution.py:76
  56.4 1.7 collective-permute-done.15
  58.1 1.2 collective-permute-done.16
  61.3 18.1 %attend.1 = (bf16[2,1024,384]{2,1,0:T(8,128)(2,1)S(1)}, f32[2,8,1024]{2,1,0:T(8,128)S(1)}) custom-call(s32[4,2]{1,0:T(4,128)S(1)} %pad_add_fusion.ranges, s32[1024,128]{1,0:T(8,128)S(1)} %broadcast_in_dim.41.col_ref, s32[8,1024]{1,0:T(8,128)S(1)} %broadcast_in_dim.42.row_ref, bf16[2,1024,1152]{2,1,0:T(8,128)(2,1)S(1)} %get-tuple-element.174.qkv_ref), custom_call_target="tpu_custom_call" | custom-call | flops 23000000512 | bytes 20000000 | tf_op jit(solution)/shard_map/attend/pallas_call | solution.py:76
  79.4 2.2 copy-done.25
  82.2 1.9 collective-permute-done.22.refs_6_
  84.1 1.3 collective-permute-done.23.refs_7_
  85.4 27.4 %mlp.1 = (bf16[512,768]{1,0:T(8,128)(2,1)S(1)}, bf16[512,768]{1,0:T(8,128)(2,1)S(1)}, f32[1024,768]{1,0:T(8,128)}, bf16[1024,384]{1,0:T(8,128)(2,1)S(1)}, bf16[1...) custom-call(s32[2]{0:T(128)S(1)} %pad_add_fusion.1.info, ...), custom_call_target="tpu_custom_call" | custom-call | flops 34500001792 | bytes 30000000 | tf_op jit(solution)/shard_map/mlp/pallas_call | solution.py:76
  112.8 6.3 %mlp_weight_grad.2 = (bf16[768,1152]{1,0:T(8,128)(2,1)}, bf16[768,1152]{1,0:T(8,128)(2,1)}) custom-call(s32[2]{0:T(128)S(1)} %pad_add_fusion.1.info, bf16[1024,768]{1,0:T(8,128)(2,1)S(1)} %get-tuple-element.189.refs_0_, bf16[1024,768]{1,0:T(8,128)(2,1)S(1)} %get-tuple-element.190.refs_1_, bf16[1024,768]{1,0:T(8,128)(2,1)S(1)} %get-tuple-element.191.refs_2_, ...), custom_call_target="tpu_custom_call" | custom-call | flops 11500000256 | bytes 10000000 | tf_op jit(solution)/shard_map/mlp_weight_grad/pallas_call | solution.py:76
  119.9 1.7 copy-done.24
  121.7 1.4 copy-done.28
  123.1 1.4 copy-done.31
  124.5 1.4 copy-done.33
  125.9 1.4 copy-done.35
  127.3 1.3 copy-done.37
  128.6 5.1 %mlp_weight_grad.3 = (bf16[768,1152]{1,0:T(8,128)(2,1)S(1)}, bf16[768,1152]{1,0:T(8,128)(2,1)S(1)}) custom-call(s32[2]{0:T(128)S(1)} %pad_add_fusion.1.info, bf16[1024,768]{1,0:T(8,128)(2,1)S(1)} %copy-done.35, bf16[1024,768]{1,0:T(8,128)(2,1)S(1)} %copy-done.31, bf16[1024,768]{1,0:T(8,128)(2,1)S(1)} %copy-done.33, bf16[2,1024,384]{2,1,0:T(8,128)(2,1)S(1)} %copy-done.28, ...), custom_call_target="tpu_custom_call" | custom-call | flops 11500000256 | bytes 10000000 | tf_op jit(solution)/shard_map/mlp_weight_grad/pallas_call | solution.py:76
  133.8 1.4 add_convert_fusion.1
  135.2 1.6 add_convert_fusion
  136.8 6.2 %collective-permute-start.27 = (bf16[384,1152]{1,0:T(8,128)(2,1)S(1)}, bf16[384,1152]{1,0:T(8,128)(2,1)S(1)}, u32[]{:S(2)}, u32[]{:S(2)}) collective-permute-start(bf16[384,1152]{1,0:T(8,128)(2,1)S(1)} %add_convert_fusion.1), channel_id=1, source_target_pairs={{0,4},{2,6},{4,0},{6,2},{8,12},{10,14},{12,8},{14,10},{16,20},{18,... | collective-permute-start | bytes 2654216 | tf_op jit(solution)/shard_map/ppermute | solution.py:490
  143.0 2.3 copy-done.26
  145.3 16.4 %attend_back.2 = (bf16[1024,384]{1,0:T(8,128)(2,1)S(1)}, bf16[1024,768]{1,0:T(8,128)(2,1)S(1)}) custom-call(s32[4,2]{1,0:T(4,128)S(1)} %pad_add_fusion.ranges, s32[1024,128]{1,0:T(8,128)S(1)} %broadcast_in_dim.41.col_ref, s32[8,1024]{1,0:T(8,128)S(1)} %broadcast_in_dim.42.row_ref, bf16[2,1024,1152]{2,1,0:T(8,128)(2,1)S(1)} %copy-done.26, ...), custom_call_target="tpu_custom_call" | custom-call | flops 20700000256 | bytes 18000000 | tf_op jit(solution)/shard_map/attend_back/pallas_call | solution.py:76
  161.9 1.3 pad_maximum_fusion.2
  163.2 1.5 collective-permute-done.28
  164.6 1.4 add_convert_fusion.4
  166.0 1.7 add_convert_fusion.3
  167.7 2.9 %qkv_weight_grad.2 = (bf16[768,640]{1,0:T(8,128)(2,1)S(1)}, bf16[768,512]{1,0:T(8,128)(2,1)S(1)}) custom-call(s32[2]{0:T(128)S(1)} %pad_add_fusion.1.info, bf16[1024,768]{1,0:T(8,128)(2,1)S(1)} %copy-done.22, bf16[1024,384]{1,0:T(8,128)(2,1)S(1)} %get-tuple-element.226.refs_1_.refs_12_, bf16[1024,768]{1,0:T(8,128)(2,1)S(1)} %get-tuple-element.227.refs_2_.refs_13_), custom_call_target="tpu_custom_call" | custom-call | flops 6899999744 | bytes 6000000 | tf_op jit(solution)/shard_map/qkv_weight_grad/pallas_call | solution.py:76
  171.3 2.1 collective-permute-start.30
  174.0 16.7 %attend_back.3 = (bf16[1024,384]{1,0:T(8,128)(2,1)S(1)}, bf16[1024,768]{1,0:T(8,128)(2,1)S(1)}) custom-call(s32[4,2]{1,0:T(4,128)S(1)} %pad_add_fusion.ranges, s32[1024,128]{1,0:T(8,128)S(1)} %broadcast_in_dim.41.col_ref, s32[8,1024]{1,0:T(8,128)S(1)} %broadcast_in_dim.42.row_ref, bf16[2,1024,1152]{2,1,0:T(8,128)(2,1)S(1)} %bitcast.43, ...), custom_call_target="tpu_custom_call" | custom-call | flops 20700000256 | bytes 18000000 | tf_op jit(solution)/shard_map/attend_back/pallas_call | solution.py:76
  190.7 1.3 convert_add_fusion
  192.0 1.3 convert_add_fusion.1
  193.5 2.9 %qkv_weight_grad.3 = (bf16[768,640]{1,0:T(8,128)(2,1)S(1)}, bf16[768,512]{1,0:T(8,128)(2,1)S(1)}) custom-call(s32[2]{0:T(128)S(1)} %pad_add_fusion.1.info, bf16[1024,768]{1,0:T(8,128)(2,1)S(1)} %copy-done.22, bf16[1024,384]{1,0:T(8,128)(2,1)S(1)} %get-tuple-element.242.refs_1_.refs_10_, bf16[1024,768]{1,0:T(8,128)(2,1)S(1)} %get-tuple-element.243.refs_2_.refs_11_), custom_call_target="tpu_custom_call" | custom-call | flops 6899999744 | bytes 6000000 | tf_op jit(solution)/shard_map/qkv_weight_grad/pallas_call | solution.py:76
  196.8 4.5 %collective-permute-start.34 = (bf16[48,2304]{1,0:T(8,128)(2,1)S(1)}, bf16[48,2304]{1,0:T(8,128)(2,1)S(1)}, u32[]{:S(2)}, u32[]{:S(2)}) collective-permute-start(bf16[48,2304]{1,0:T(8,128)(2,1)S(1)} %get-tuple-element.258), channel_id=1, source_target_pairs={{0,16},{2,18},{4,20},{6,22},{8,24},{10,26},{12,28},{14,30},{16,0},... | collective-permute-start | bytes 663560 | tf_op jit(solution)/shard_map/ppermute | solution.py:490
  201.3 1.8 collective-permute-start.37
  203.2 2.2 collective-permute-start.36
  205.4 8.3 %input_back.1 = (f32[512,768]{1,0:T(8,128)S(1)}, f32[512,768]{1,0:T(8,128)S(1)}, bf16[768,128]{1,0:T(8,128)(2,1)S(1)}) custom-call(s32[2]{0:T(128)S(1)} %pad_add_fusion.1.info, bf16[384,640]{1,0:T(8,128)(2,1)S(1)} %constant_dynamic-update-slice_fusion.refs_0_, bf16[384,640]{1,0:T(8,128)(2,1)S(1)} %constant_dynamic-update-slice_fusion.2.refs_1_, ...), custom_call_target="tpu_custom_call" | custom-call | flops 11500000256 | bytes 10000000 | tf_op jit(solution)/shard_map/input_back/pallas_call | solution.py:76
  214.0 3.0 %collective-permute-done.36 = bf16[384,640]{1,0:T(8,128)(2,1)S(1)} collective-permute-done((bf16[384,640]{1,0:T(8,128)(2,1)S(1)}, bf16[384,640]{1,0:T(8,128)(2,1)S(1)}, u32[]{:S(2)}, u32[]{:S(2)}) %collective-permute-start.36) | collective-permute-done | bytes 491552 | tf_op jit(solution)/shard_map/ppermute | solution.py:490
  217.2 0.8 collective-permute-start.38
  219.1 1.2 collective-permute-start.39
  220.9 2.6 %collective-permute-start.42 = (bf16[192,512]{1,0:T(8,128)(2,1)S(1)}, bf16[192,512]{1,0:T(8,128)(2,1)S(1)}, u32[]{:S(2)}, u32[]{:S(2)}) collective-permute-start(bf16[192,512]{1,0:T(8,128)(2,1)S(1)} %add_convert_fusion.7), channel_id=1, source_target_pairs={{0,4},{2,6},{4,0},{6,2},{8,12},{10,14},{12,8},{14,10},{16,20},{18,... | collective-permute-start | bytes 589832 | tf_op jit(solution)/shard_map/ppermute | solution.py:490
  224.2 2.3 collective-permute-start.40
  226.6 0.7 pad_maximum_fusion.10
  227.3 2.2 collective-permute-done.40
  229.5 1.4 collective-permute-done.41
  231.4 5.3 %collective-permute-start.44 = (bf16[48,1280]{1,0:T(8,128)(2,1)S(1)}, bf16[48,1280]{1,0:T(8,128)(2,1)S(1)}, u32[]{:S(2)}, u32[]{:S(2)}) collective-permute-start(bf16[48,1280]{1,0:T(8,128)(2,1)S(1)} %get-tuple-element.276), channel_id=1, source_target_pairs={{0,8},{2,10},{4,12},{6,14},{8,0},{10,2},{12,4},{14,6},{16,24},{18,... | collective-permute-start | bytes 368648 | tf_op jit(solution)/shard_map/ppermute | solution.py:490
  236.7 0.8 collective-permute-start.45
  237.5 1.6 collective-permute-start.46
  239.3 2.0 pad_maximum_fusion
  241.3 6.5 %collective-permute-done.45 = bf16[48,1280]{1,0:T(8,128)(2,1)S(1)} collective-permute-done((bf16[48,1280]{1,0:T(8,128)(2,1)S(1)}, bf16[48,1280]{1,0:T(8,128)(2,1)S(1)}, u32[]{:S(2)}, u32[]{:S(2)}) %collective-permute-start.45) | collective-permute-done | bytes 122912 | tf_op jit(solution)/shard_map/ppermute | solution.py:490
  (211 shorter events, 19.7 us)
Async XLA Ops:
  2.3 12.3 %copy-start = (bf16[2,512,768]{2,1,0:T(8,128)(2,1)S(1)}, bf16[2,512,768]{2,1,0:T(8,128)(2,1)}, u32[]{:S(2)}) copy-start(bf16[2,512,768]{2,1,0:T(8,128)(2,1)} %refs_10_.1) | copy-start | bytes 4718596
  2.3 12.8 %collective-permute-start.3 = (bf16[48,1280]{1,0:T(8,128)(2,1)S(1)}, bf16[48,1280]{1,0:T(8,128)(2,1)S(1)}, u32[]{:S(2)}, u32[]{:S(2)}) collective-permute-start(bf16[48,1280]{1,0:T(8,128)(2,1)S(1)} %pad_maximum_fusion.12), channel_id=1, source_target_pairs={{0,24},{2,26},{4,28},{6,30},{8,16},{10,18},{12,20},{14,22},{16,8},... | collective-permute-start | bytes 368648 | tf_op jit(solution)/shard_map/ppermute | solution.py:490
  7.4 10.4 %collective-permute-start.2 = (bf16[48,1280]{1,0:T(8,128)(2,1)S(1)}, bf16[48,1280]{1,0:T(8,128)(2,1)S(1)}, u32[]{:S(2)}, u32[]{:S(2)}) collective-permute-start(bf16[48,1280]{1,0:T(8,128)(2,1)S(1)} %pad_maximum_fusion.12), channel_id=1, source_target_pairs={{0,16},{2,18},{4,20},{6,22},{8,24},{10,26},{12,28},{14,30},{16,0},... | collective-permute-start | bytes 368648 | tf_op jit(solution)/shard_map/ppermute | solution.py:490
  7.4 10.4 %collective-permute-start.1 = (bf16[48,1280]{1,0:T(8,128)(2,1)S(1)}, bf16[48,1280]{1,0:T(8,128)(2,1)S(1)}, u32[]{:S(2)}, u32[]{:S(2)}) collective-permute-start(bf16[48,1280]{1,0:T(8,128)(2,1)S(1)} %pad_maximum_fusion.12), channel_id=1, source_target_pairs={{0,8},{2,10},{4,12},{6,14},{8,0},{10,2},{12,4},{14,6},{16,24},{18,... | collective-permute-start | bytes 368648 | tf_op jit(solution)/shard_map/ppermute | solution.py:490
  10.1 7.8 %collective-permute-start = (bf16[512,768]{1,0:T(8,128)(2,1)}, bf16[512,768]{1,0:T(8,128)(2,1)S(1)}, u32[]{:S(2)}, u32[]{:S(2)}) collective-permute-start(bf16[512,768]{1,0:T(8,128)(2,1)} %dynamic-slice_bitcast_fusion.1), channel_id=1, source_target_pairs={{0,1},{1,0},{2,3},{3,2},{4,5},{5,4},{6,7},{7,6},{8,9},{9,8},{10,11... | collective-permute-start | bytes 2359304 | tf_op jit(solution)/shard_map/ppermute | solution.py:486
  18.0 7.6 %collective-permute-start.9 = (bf16[192,640]{1,0:T(8,128)(2,1)S(1)}, bf16[192,640]{1,0:T(8,128)(2,1)S(1)}, u32[]{:S(2)}, u32[]{:S(2)}) collective-permute-start(bf16[192,640]{1,0:T(8,128)(2,1)S(1)} %get-tuple-element.151), channel_id=1, source_target_pairs={{0,4},{2,6},{4,0},{6,2},{8,12},{10,14},{12,8},{14,10},{16,20},{18,... | collective-permute-start | bytes 737288 | tf_op jit(solution)/shard_map/ppermute | solution.py:490
  19.6 14.5 %collective-permute-start.6 = (bf16[48,2304]{1,0:T(8,128)(2,1)S(1)}, bf16[48,2304]{1,0:T(8,128)(2,1)S(1)}, u32[]{:S(2)}, u32[]{:S(2)}) collective-permute-start(bf16[48,2304]{1,0:T(8,128)(2,1)S(1)} %pad_maximum_fusion.11), channel_id=1, source_target_pairs={{0,24},{2,26},{4,28},{6,30},{8,16},{10,18},{12,20},{14,22},{16,8},... | collective-permute-start | bytes 663560 | tf_op jit(solution)/shard_map/ppermute | solution.py:490
  22.2 17.7 %collective-permute-start.5 = (bf16[48,2304]{1,0:T(8,128)(2,1)S(1)}, bf16[48,2304]{1,0:T(8,128)(2,1)S(1)}, u32[]{:S(2)}, u32[]{:S(2)}) collective-permute-start(bf16[48,2304]{1,0:T(8,128)(2,1)S(1)} %pad_maximum_fusion.11), channel_id=1, source_target_pairs={{0,16},{2,18},{4,20},{6,22},{8,24},{10,26},{12,28},{14,30},{16,0},... | collective-permute-start | bytes 663560 | tf_op jit(solution)/shard_map/ppermute | solution.py:490
  22.2 17.7 %collective-permute-start.4 = (bf16[48,2304]{1,0:T(8,128)(2,1)S(1)}, bf16[48,2304]{1,0:T(8,128)(2,1)S(1)}, u32[]{:S(2)}, u32[]{:S(2)}) collective-permute-start(bf16[48,2304]{1,0:T(8,128)(2,1)S(1)} %pad_maximum_fusion.11), channel_id=1, source_target_pairs={{0,8},{2,10},{4,12},{6,14},{8,0},{10,2},{12,4},{14,6},{16,24},{18,... | collective-permute-start | bytes 663560 | tf_op jit(solution)/shard_map/ppermute | solution.py:490
  24.1 8.9 %collective-permute-start.7 = (bf16[192,640]{1,0:T(8,128)(2,1)S(1)}, bf16[192,640]{1,0:T(8,128)(2,1)S(1)}, u32[]{:S(2)}, u32[]{:S(2)}) collective-permute-start(bf16[192,640]{1,0:T(8,128)(2,1)S(1)} %get-tuple-element.150), channel_id=1, source_target_pairs={{0,2},{2,0},{4,6},{6,4},{8,10},{10,8},{12,14},{14,12},{16,18},{18,... | collective-permute-start | bytes 737288 | tf_op jit(solution)/shard_map/ppermute | solution.py:490
  25.7 14.8 %collective-permute-start.10 = (bf16[384,640]{1,0:T(8,128)(2,1)S(1)}, bf16[384,640]{1,0:T(8,128)(2,1)S(1)}, u32[]{:S(2)}, u32[]{:S(2)}) collective-permute-start(bf16[384,640]{1,0:T(8,128)(2,1)S(1)} %constant_dynamic-update-slice_fusion.2.refs_1_), channel_id=1, source_target_pairs={{0,2},{2,0},{4,6},{6,4},{8,10},{10,8},{12,14},{14,12},{16,18},{18,... | collective-permute-start | bytes 1474568 | tf_op jit(solution)/shard_map/ppermute | solution.py:490
  33.0 8.9 %collective-permute-start.8 = (bf16[384,640]{1,0:T(8,128)(2,1)S(1)}, bf16[384,640]{1,0:T(8,128)(2,1)S(1)}, u32[]{:S(2)}, u32[]{:S(2)}) collective-permute-start(bf16[384,640]{1,0:T(8,128)(2,1)S(1)} %constant_dynamic-update-slice_fusion.refs_0_), channel_id=1, source_target_pairs={{0,4},{2,6},{4,0},{6,2},{8,12},{10,14},{12,8},{14,10},{16,20},{18,... | collective-permute-start | bytes 1474568 | tf_op jit(solution)/shard_map/ppermute | solution.py:490
  34.1 13.8 %copy-start.2 = (bf16[2,512,768]{2,1,0:T(8,128)(2,1)S(1)}, bf16[2,512,768]{2,1,0:T(8,128)(2,1)}, u32[]{:S(2)}) copy-start(bf16[2,512,768]{2,1,0:T(8,128)(2,1)} %refs_8_.5) | copy-start | bytes 4718596
  34.1 13.8 %copy-start.5 = (bf16[512,768]{1,0:T(8,128)(2,1)S(1)}, bf16[512,768]{1,0:T(8,128)(2,1)}, u32[]{:S(2)}) copy-start(bf16[512,768]{1,0:T(8,128)(2,1)} %copy-done.4) | copy-start | bytes 2359300
  40.5 15.9 %copy-start.8 = (bf16[384,640]{1,0:T(8,128)(2,1)}, bf16[384,640]{1,0:T(8,128)(2,1)S(1)}, u32[]{:S(2)}) copy-start(bf16[384,640]{1,0:T(8,128)(2,1)S(1)} %collective-permute-done.10.refs_3_) | copy-start | bytes 1474564
  41.9 14.5 %copy-start.10 = (bf16[384,640]{1,0:T(8,128)(2,1)}, bf16[384,640]{1,0:T(8,128)(2,1)S(1)}, u32[]{:S(2)}) copy-start(bf16[384,640]{1,0:T(8,128)(2,1)S(1)} %collective-permute-done.8.refs_2_) | copy-start | bytes 1474564
  41.9 1.9 collective-permute-start.11
  41.9 2.6 %collective-permute-start.12 = (bf16[384,640]{1,0:T(8,128)(2,1)S(1)}, bf16[384,640]{1,0:T(8,128)(2,1)S(1)}, u32[]{:S(2)}, u32[]{:S(2)}) collective-permute-start(bf16[384,640]{1,0:T(8,128)(2,1)S(1)} %constant_dynamic-update-slice_fusion.2.refs_1_), channel_id=1, source_target_pairs={{0,1},{1,0},{2,3},{3,2},{4,5},{5,4},{6,7},{7,6},{8,9},{9,8},{10,11... | collective-permute-start | bytes 1474568 | tf_op jit(solution)/shard_map/ppermute | solution.py:486
  42.4 2.8 %collective-permute-start.13 = (bf16[384,640]{1,0:T(8,128)(2,1)S(1)}, bf16[384,640]{1,0:T(8,128)(2,1)S(1)}, u32[]{:S(2)}, u32[]{:S(2)}) collective-permute-start(bf16[384,640]{1,0:T(8,128)(2,1)S(1)} %collective-permute-done.8.refs_2_), channel_id=1, source_target_pairs={{0,1},{1,0},{2,3},{3,2},{4,5},{5,4},{6,7},{7,6},{8,9},{9,8},{10,11... | collective-permute-start | bytes 1474568 | tf_op jit(solution)/shard_map/ppermute | solution.py:486
  42.4 3.5 %collective-permute-start.14 = (bf16[384,640]{1,0:T(8,128)(2,1)S(1)}, bf16[384,640]{1,0:T(8,128)(2,1)S(1)}, u32[]{:S(2)}, u32[]{:S(2)}) collective-permute-start(bf16[384,640]{1,0:T(8,128)(2,1)S(1)} %collective-permute-done.10.refs_3_), channel_id=1, source_target_pairs={{0,1},{1,0},{2,3},{3,2},{4,5},{5,4},{6,7},{7,6},{8,9},{9,8},{10,11... | collective-permute-start | bytes 1474568 | tf_op jit(solution)/shard_map/ppermute | solution.py:486
  43.8 12.6 %copy-start.12 = (bf16[384,640]{1,0:T(8,128)(2,1)}, bf16[384,640]{1,0:T(8,128)(2,1)S(1)}, u32[]{:S(2)}) copy-start(bf16[384,640]{1,0:T(8,128)(2,1)S(1)} %collective-permute-done.11.refs_4_) | copy-start | bytes 1474564
  44.5 11.9 %copy-start.14 = (bf16[384,640]{1,0:T(8,128)(2,1)}, bf16[384,640]{1,0:T(8,128)(2,1)S(1)}, u32[]{:S(2)}) copy-start(bf16[384,640]{1,0:T(8,128)(2,1)S(1)} %collective-permute-done.12.refs_5_) | copy-start | bytes 1474564
  45.2 11.2 %copy-start.16 = (bf16[384,640]{1,0:T(8,128)(2,1)}, bf16[384,640]{1,0:T(8,128)(2,1)S(1)}, u32[]{:S(2)}) copy-start(bf16[384,640]{1,0:T(8,128)(2,1)S(1)} %collective-permute-done.13.refs_6_) | copy-start | bytes 1474564
  45.9 12.2 %collective-permute-start.15 = (bf16[192,1152]{1,0:T(8,128)(2,1)S(1)}, bf16[192,1152]{1,0:T(8,128)(2,1)S(1)}, u32[]{:S(2)}, u32[]{:S(2)}) collective-permute-start(bf16[192,1152]{1,0:T(8,128)(2,1)S(1)} %get-tuple-element.168), channel_id=1, source_target_pairs={{0,2},{2,0},{4,6},{6,4},{8,10},{10,8},{12,14},{14,12},{16,18},{18,... | collective-permute-start | bytes 1327112 | tf_op jit(solution)/shard_map/ppermute | solution.py:490
  47.4 11.9 %collective-permute-start.16 = (bf16[192,1152]{1,0:T(8,128)(2,1)S(1)}, bf16[192,1152]{1,0:T(8,128)(2,1)S(1)}, u32[]{:S(2)}, u32[]{:S(2)}) collective-permute-start(bf16[192,1152]{1,0:T(8,128)(2,1)S(1)} %get-tuple-element.169), channel_id=1, source_target_pairs={{0,4},{2,6},{4,0},{6,2},{8,12},{10,14},{12,8},{14,10},{16,20},{18,... | collective-permute-start | bytes 1327112 | tf_op jit(solution)/shard_map/ppermute | solution.py:490
  47.9 11.4 %collective-permute-start.17 = (bf16[512,768]{1,0:T(8,128)(2,1)S(1)}, bf16[512,768]{1,0:T(8,128)(2,1)S(1)}, u32[]{:S(2)}, u32[]{:S(2)}) collective-permute-start(bf16[512,768]{1,0:T(8,128)(2,1)S(1)} %dynamic-slice_bitcast_fusion), channel_id=1, source_target_pairs={{0,1},{1,0},{2,3},{3,2},{4,5},{5,4},{6,7},{7,6},{8,9},{9,8},{10,11... | collective-permute-start | bytes 2359304 | tf_op jit(solution)/shard_map/ppermute | solution.py:486
  59.5 22.1 %collective-permute-start.18 = (bf16[384,1152]{1,0:T(8,128)(2,1)S(1)}, bf16[384,1152]{1,0:T(8,128)(2,1)S(1)}, u32[]{:S(2)}, u32[]{:S(2)}) collective-permute-start(bf16[384,1152]{1,0:T(8,128)(2,1)S(1)} %get-tuple-element.179.refs_0_), channel_id=1, source_target_pairs={{0,4},{2,6},{4,0},{6,2},{8,12},{10,14},{12,8},{14,10},{16,20},{18,... | collective-permute-start | bytes 2654216 | tf_op jit(solution)/shard_map/ppermute | solution.py:490
  60.0 21.6 %collective-permute-start.19 = (bf16[384,1152]{1,0:T(8,128)(2,1)S(1)}, bf16[384,1152]{1,0:T(8,128)(2,1)S(1)}, u32[]{:S(2)}, u32[]{:S(2)}) collective-permute-start(bf16[384,1152]{1,0:T(8,128)(2,1)S(1)} %get-tuple-element.180.refs_1_), channel_id=1, source_target_pairs={{0,2},{2,0},{4,6},{6,4},{8,10},{10,8},{12,14},{14,12},{16,18},{18,... | collective-permute-start | bytes 2654216 | tf_op jit(solution)/shard_map/ppermute | solution.py:490
  60.6 21.0 %collective-permute-start.20 = (bf16[384,1152]{1,0:T(8,128)(2,1)S(1)}, bf16[384,1152]{1,0:T(8,128)(2,1)S(1)}, u32[]{:S(2)}, u32[]{:S(2)}) collective-permute-start(bf16[384,1152]{1,0:T(8,128)(2,1)S(1)} %get-tuple-element.179.refs_0_), channel_id=1, source_target_pairs={{0,1},{1,0},{2,3},{3,2},{4,5},{5,4},{6,7},{7,6},{8,9},{9,8},{10,11... | collective-permute-start | bytes 2654216 | tf_op jit(solution)/shard_map/ppermute | solution.py:486
  60.6 21.1 %collective-permute-start.21 = (bf16[384,1152]{1,0:T(8,128)(2,1)S(1)}, bf16[384,1152]{1,0:T(8,128)(2,1)S(1)}, u32[]{:S(2)}, u32[]{:S(2)}) collective-permute-start(bf16[384,1152]{1,0:T(8,128)(2,1)S(1)} %get-tuple-element.180.refs_1_), channel_id=1, source_target_pairs={{0,1},{1,0},{2,3},{3,2},{4,5},{5,4},{6,7},{7,6},{8,9},{9,8},{10,11... | collective-permute-start | bytes 2654216 | tf_op jit(solution)/shard_map/ppermute | solution.py:486
  61.3 24.1 %copy-start.1 = (bf16[2,512,768]{2,1,0:T(8,128)(2,1)S(1)}, bf16[2,512,768]{2,1,0:T(8,128)(2,1)}, u32[]{:S(2)}) copy-start(bf16[2,512,768]{2,1,0:T(8,128)(2,1)} %refs_10_.1) | copy-start | bytes 4718596
  81.6 31.2 %copy-start.27 = (bf16[2,1024,384]{2,1,0:T(8,128)(2,1)}, bf16[2,1024,384]{2,1,0:T(8,128)(2,1)S(1)}, u32[]{:S(2)}) copy-start(bf16[2,1024,384]{2,1,0:T(8,128)(2,1)S(1)} %get-tuple-element.197.refs_12_.refs_3_.o_ref) | copy-start | bytes 4718596
  81.6 2.5 collective-permute-start.22
  81.7 3.7 %collective-permute-start.23 = (bf16[384,1152]{1,0:T(8,128)(2,1)S(1)}, bf16[384,1152]{1,0:T(8,128)(2,1)S(1)}, u32[]{:S(2)}, u32[]{:S(2)}) collective-permute-start(bf16[384,1152]{1,0:T(8,128)(2,1)S(1)} %collective-permute-done.19.refs_3_), channel_id=1, source_target_pairs={{0,1},{1,0},{2,3},{3,2},{4,5},{5,4},{6,7},{7,6},{8,9},{9,8},{10,11... | collective-permute-start | bytes 2654216 | tf_op jit(solution)/shard_map/ppermute | solution.py:486
  119.2 14.5 %collective-permute-start.24 = (bf16[768,1152]{1,0:T(8,128)(2,1)}, bf16[768,1152]{1,0:T(8,128)(2,1)}, u32[]{:S(2)}, u32[]{:S(2)}) collective-permute-start(bf16[768,1152]{1,0:T(8,128)(2,1)} %get-tuple-element.202), channel_id=1, source_target_pairs={{0,1},{1,0},{2,3},{3,2},{4,5},{5,4},{6,7},{7,6},{8,9},{9,8},{10,11... | collective-permute-start | bytes 5308424 | tf_op jit(solution)/shard_map/ppermute | solution.py:486
  119.4 14.3 %collective-permute-start.25 = (bf16[768,1152]{1,0:T(8,128)(2,1)}, bf16[768,1152]{1,0:T(8,128)(2,1)}, u32[]{:S(2)}, u32[]{:S(2)}) collective-permute-start(bf16[768,1152]{1,0:T(8,128)(2,1)} %get-tuple-element.203), channel_id=1, source_target_pairs={{0,1},{1,0},{2,3},{3,2},{4,5},{5,4},{6,7},{7,6},{8,9},{9,8},{10,11... | collective-permute-start | bytes 5308424 | tf_op jit(solution)/shard_map/ppermute | solution.py:486
  119.8 13.9 %collective-permute-start.26 = (bf16[512,768]{1,0:T(8,128)(2,1)}, bf16[512,768]{1,0:T(8,128)(2,1)S(1)}, u32[]{:S(2)}, u32[]{:S(2)}) collective-permute-start(bf16[512,768]{1,0:T(8,128)(2,1)} %copy-done.7), channel_id=1, source_target_pairs={{0,1},{1,0},{2,3},{3,2},{4,5},{5,4},{6,7},{7,6},{8,9},{9,8},{10,11... | collective-permute-start | bytes 2359304 | tf_op jit(solution)/shard_map/ppermute | solution.py:486
  136.8 26.4 %collective-permute-start.27 = (bf16[384,1152]{1,0:T(8,128)(2,1)S(1)}, bf16[384,1152]{1,0:T(8,128)(2,1)S(1)}, u32[]{:S(2)}, u32[]{:S(2)}) collective-permute-start(bf16[384,1152]{1,0:T(8,128)(2,1)S(1)} %add_convert_fusion.1), channel_id=1, source_target_pairs={{0,4},{2,6},{4,0},{6,2},{8,12},{10,14},{12,8},{14,10},{16,20},{18,... | collective-permute-start | bytes 2654216 | tf_op jit(solution)/shard_map/ppermute | solution.py:490
  143.0 21.6 %collective-permute-start.28 = (bf16[384,1152]{1,0:T(8,128)(2,1)S(1)}, bf16[384,1152]{1,0:T(8,128)(2,1)S(1)}, u32[]{:S(2)}, u32[]{:S(2)}) collective-permute-start(bf16[384,1152]{1,0:T(8,128)(2,1)S(1)} %add_convert_fusion), channel_id=1, source_target_pairs={{0,2},{2,0},{4,6},{6,4},{8,10},{10,8},{12,14},{14,12},{16,18},{18,... | collective-permute-start | bytes 2654216 | tf_op jit(solution)/shard_map/ppermute | solution.py:490
  170.6 20.0 %collective-permute-start.29 = (bf16[192,1152]{1,0:T(8,128)(2,1)S(1)}, bf16[192,1152]{1,0:T(8,128)(2,1)S(1)}, u32[]{:S(2)}, u32[]{:S(2)}) collective-permute-start(bf16[192,1152]{1,0:T(8,128)(2,1)S(1)} %add_convert_fusion.4), channel_id=1, source_target_pairs={{0,2},{2,0},{4,6},{6,4},{8,10},{10,8},{12,14},{14,12},{16,18},{18,... | collective-permute-start | bytes 1327112 | tf_op jit(solution)/shard_map/ppermute | solution.py:490
  171.3 19.4 %collective-permute-start.30 = (bf16[192,1152]{1,0:T(8,128)(2,1)S(1)}, bf16[192,1152]{1,0:T(8,128)(2,1)S(1)}, u32[]{:S(2)}, u32[]{:S(2)}) collective-permute-start(bf16[192,1152]{1,0:T(8,128)(2,1)S(1)} %add_convert_fusion.3), channel_id=1, source_target_pairs={{0,4},{2,6},{4,0},{6,2},{8,12},{10,14},{12,8},{14,10},{16,20},{18,... | collective-permute-start | bytes 1327112 | tf_op jit(solution)/shard_map/ppermute | solution.py:490
  173.4 17.3 %collective-permute-start.32 = (bf16[768,512]{1,0:T(8,128)(2,1)S(1)}, bf16[768,512]{1,0:T(8,128)(2,1)S(1)}, u32[]{:S(2)}, u32[]{:S(2)}) collective-permute-start(bf16[768,512]{1,0:T(8,128)(2,1)S(1)} %get-tuple-element.237), channel_id=1, source_target_pairs={{0,1},{1,0},{2,3},{3,2},{4,5},{5,4},{6,7},{7,6},{8,9},{9,8},{10,11... | collective-permute-start | bytes 2359304 | tf_op jit(solution)/shard_map/ppermute | solution.py:486
  173.4 17.3 %collective-permute-start.31 = (bf16[768,640]{1,0:T(8,128)(2,1)S(1)}, bf16[768,640]{1,0:T(8,128)(2,1)S(1)}, u32[]{:S(2)}, u32[]{:S(2)}) collective-permute-start(bf16[768,640]{1,0:T(8,128)(2,1)S(1)} %get-tuple-element.236), channel_id=1, source_target_pairs={{0,1},{1,0},{2,3},{3,2},{4,5},{5,4},{6,7},{7,6},{8,9},{9,8},{10,11... | collective-permute-start | bytes 2949128 | tf_op jit(solution)/shard_map/ppermute | solution.py:486
  193.4 11.9 %copy-start.9 = (bf16[384,640]{1,0:T(8,128)(2,1)S(1)}, bf16[384,640]{1,0:T(8,128)(2,1)}, u32[]{:S(2)}) copy-start(bf16[384,640]{1,0:T(8,128)(2,1)} %copy-done.8) | copy-start | bytes 1474564
  193.4 11.9 %copy-start.11 = (bf16[384,640]{1,0:T(8,128)(2,1)S(1)}, bf16[384,640]{1,0:T(8,128)(2,1)}, u32[]{:S(2)}) copy-start(bf16[384,640]{1,0:T(8,128)(2,1)} %copy-done.10) | copy-start | bytes 1474564
  193.5 11.9 %copy-start.13 = (bf16[384,640]{1,0:T(8,128)(2,1)S(1)}, bf16[384,640]{1,0:T(8,128)(2,1)}, u32[]{:S(2)}) copy-start(bf16[384,640]{1,0:T(8,128)(2,1)} %copy-done.12) | copy-start | bytes 1474564
  193.5 11.9 %copy-start.15 = (bf16[384,640]{1,0:T(8,128)(2,1)S(1)}, bf16[384,640]{1,0:T(8,128)(2,1)}, u32[]{:S(2)}) copy-start(bf16[384,640]{1,0:T(8,128)(2,1)} %copy-done.14) | copy-start | bytes 1474564
  193.5 11.9 %copy-start.17 = (bf16[384,640]{1,0:T(8,128)(2,1)S(1)}, bf16[384,640]{1,0:T(8,128)(2,1)}, u32[]{:S(2)}) copy-start(bf16[384,640]{1,0:T(8,128)(2,1)} %copy-done.16) | copy-start | bytes 1474564
  193.5 11.9 %copy-start.19 = (bf16[384,640]{1,0:T(8,128)(2,1)S(1)}, bf16[384,640]{1,0:T(8,128)(2,1)}, u32[]{:S(2)}) copy-start(bf16[384,640]{1,0:T(8,128)(2,1)} %copy-done.18) | copy-start | bytes 1474564
  193.5 11.9 %copy-start.20 = (f32[1024,768]{1,0:T(8,128)S(1)}, f32[1024,768]{1,0:T(8,128)}, u32[]{:S(2)}) copy-start(f32[1024,768]{1,0:T(8,128)} %get-tuple-element.252.refs_14_) | copy-start | bytes 9437188
  196.7 17.0 %collective-permute-start.33 = (bf16[48,2304]{1,0:T(8,128)(2,1)S(1)}, bf16[48,2304]{1,0:T(8,128)(2,1)S(1)}, u32[]{:S(2)}, u32[]{:S(2)}) collective-permute-start(bf16[48,2304]{1,0:T(8,128)(2,1)S(1)} %get-tuple-element.257), channel_id=1, source_target_pairs={{0,8},{2,10},{4,12},{6,14},{8,0},{10,2},{12,4},{14,6},{16,24},{18,... | collective-permute-start | bytes 663560 | tf_op jit(solution)/shard_map/ppermute | solution.py:490
  196.8 16.9 %collective-permute-start.34 = (bf16[48,2304]{1,0:T(8,128)(2,1)S(1)}, bf16[48,2304]{1,0:T(8,128)(2,1)S(1)}, u32[]{:S(2)}, u32[]{:S(2)}) collective-permute-start(bf16[48,2304]{1,0:T(8,128)(2,1)S(1)} %get-tuple-element.258), channel_id=1, source_target_pairs={{0,16},{2,18},{4,20},{6,22},{8,24},{10,26},{12,28},{14,30},{16,0},... | collective-permute-start | bytes 663560 | tf_op jit(solution)/shard_map/ppermute | solution.py:490
  201.3 12.7 %collective-permute-start.35 = (bf16[48,2304]{1,0:T(8,128)(2,1)S(1)}, bf16[48,2304]{1,0:T(8,128)(2,1)S(1)}, u32[]{:S(2)}, u32[]{:S(2)}) collective-permute-start(bf16[48,2304]{1,0:T(8,128)(2,1)S(1)} %get-tuple-element.259), channel_id=1, source_target_pairs={{0,24},{2,26},{4,28},{6,30},{8,16},{10,18},{12,20},{14,22},{16,8},... | collective-permute-start | bytes 663560 | tf_op jit(solution)/shard_map/ppermute | solution.py:490
  201.3 12.7 %collective-permute-start.37 = (bf16[384,512]{1,0:T(8,128)(2,1)S(1)}, bf16[384,512]{1,0:T(8,128)(2,1)S(1)}, u32[]{:S(2)}, u32[]{:S(2)}) collective-permute-start(bf16[384,512]{1,0:T(8,128)(2,1)S(1)} %add_convert_fusion.5), channel_id=1, source_target_pairs={{0,2},{2,0},{4,6},{6,4},{8,10},{10,8},{12,14},{14,12},{16,18},{18,... | collective-permute-start | bytes 1179656 | tf_op jit(solution)/shard_map/ppermute | solution.py:490
  203.2 13.8 %collective-permute-start.36 = (bf16[384,640]{1,0:T(8,128)(2,1)S(1)}, bf16[384,640]{1,0:T(8,128)(2,1)S(1)}, u32[]{:S(2)}, u32[]{:S(2)}) collective-permute-start(bf16[384,640]{1,0:T(8,128)(2,1)S(1)} %add_convert_fusion.2), channel_id=1, source_target_pairs={{0,4},{2,6},{4,0},{6,2},{8,12},{10,14},{12,8},{14,10},{16,20},{18,... | collective-permute-start | bytes 1474568 | tf_op jit(solution)/shard_map/ppermute | solution.py:490
  217.2 1.8 collective-permute-start.38
  217.9 13.1 %collective-permute-start.43 = (f32[512,768]{1,0:T(8,128)S(1)}, f32[512,768]{1,0:T(8,128)S(1)}, u32[]{:S(2)}, u32[]{:S(2)}) collective-permute-start(f32[512,768]{1,0:T(8,128)S(1)} %get-tuple-element.270), channel_id=1, source_target_pairs={{0,1},{1,0},{2,3},{3,2},{4,5},{5,4},{6,7},{7,6},{8,9},{9,8},{10,11... | collective-permute-start | bytes 4718600 | tf_op jit(solution)/shard_map/ppermute | solution.py:486
  219.1 5.1 %collective-permute-start.39 = (bf16[384,128]{1,0:T(8,128)(2,1)S(1)}, bf16[384,128]{1,0:T(8,128)(2,1)S(1)}, u32[]{:S(2)}, u32[]{:S(2)}) collective-permute-start(bf16[384,128]{1,0:T(8,128)(2,1)S(1)} %slice.376), channel_id=1, source_target_pairs={{0,2},{2,0},{4,6},{6,4},{8,10},{10,8},{12,14},{14,12},{16,18},{18,... | collective-permute-start | bytes 294920 | tf_op jit(solution)/shard_map/ppermute | solution.py:490
  220.9 8.6 %collective-permute-start.42 = (bf16[192,512]{1,0:T(8,128)(2,1)S(1)}, bf16[192,512]{1,0:T(8,128)(2,1)S(1)}, u32[]{:S(2)}, u32[]{:S(2)}) collective-permute-start(bf16[192,512]{1,0:T(8,128)(2,1)S(1)} %add_convert_fusion.7), channel_id=1, source_target_pairs={{0,4},{2,6},{4,0},{6,2},{8,12},{10,14},{12,8},{14,10},{16,20},{18,... | collective-permute-start | bytes 589832 | tf_op jit(solution)/shard_map/ppermute | solution.py:490
  223.5 7.4 %collective-permute-start.41 = (bf16[192,640]{1,0:T(8,128)(2,1)S(1)}, bf16[192,640]{1,0:T(8,128)(2,1)S(1)}, u32[]{:S(2)}, u32[]{:S(2)}) collective-permute-start(bf16[192,640]{1,0:T(8,128)(2,1)S(1)} %add_convert_fusion.6), channel_id=1, source_target_pairs={{0,2},{2,0},{4,6},{6,4},{8,10},{10,8},{12,14},{14,12},{16,18},{18,... | collective-permute-start | bytes 737288 | tf_op jit(solution)/shard_map/ppermute | solution.py:490
  224.2 5.3 %collective-permute-start.40 = (bf16[192,128]{1,0:T(8,128)(2,1)S(1)}, bf16[192,128]{1,0:T(8,128)(2,1)S(1)}, u32[]{:S(2)}, u32[]{:S(2)}) collective-permute-start(bf16[192,128]{1,0:T(8,128)(2,1)S(1)} %slice.377), channel_id=1, source_target_pairs={{0,4},{2,6},{4,0},{6,2},{8,12},{10,14},{12,8},{14,10},{16,20},{18,... | collective-permute-start | bytes 147464 | tf_op jit(solution)/shard_map/ppermute | solution.py:490
  231.4 10.0 %collective-permute-start.44 = (bf16[48,1280]{1,0:T(8,128)(2,1)S(1)}, bf16[48,1280]{1,0:T(8,128)(2,1)S(1)}, u32[]{:S(2)}, u32[]{:S(2)}) collective-permute-start(bf16[48,1280]{1,0:T(8,128)(2,1)S(1)} %get-tuple-element.276), channel_id=1, source_target_pairs={{0,8},{2,10},{4,12},{6,14},{8,0},{10,2},{12,4},{14,6},{16,24},{18,... | collective-permute-start | bytes 368648 | tf_op jit(solution)/shard_map/ppermute | solution.py:490
  236.7 11.1 %collective-permute-start.45 = (bf16[48,1280]{1,0:T(8,128)(2,1)S(1)}, bf16[48,1280]{1,0:T(8,128)(2,1)S(1)}, u32[]{:S(2)}, u32[]{:S(2)}) collective-permute-start(bf16[48,1280]{1,0:T(8,128)(2,1)S(1)} %get-tuple-element.277), channel_id=1, source_target_pairs={{0,16},{2,18},{4,20},{6,22},{8,24},{10,26},{12,28},{14,30},{16,0},... | collective-permute-start | bytes 368648 | tf_op jit(solution)/shard_map/ppermute | solution.py:490
  237.5 10.3 %collective-permute-start.46 = (bf16[48,1280]{1,0:T(8,128)(2,1)S(1)}, bf16[48,1280]{1,0:T(8,128)(2,1)S(1)}, u32[]{:S(2)}, u32[]{:S(2)}) collective-permute-start(bf16[48,1280]{1,0:T(8,128)(2,1)S(1)} %get-tuple-element.278), channel_id=1, source_target_pairs={{0,24},{2,26},{4,28},{6,30},{8,16},{10,18},{12,20},{14,22},{16,8},... | collective-permute-start | bytes 368648 | tf_op jit(solution)/shard_map/ppermute | solution.py:490
  (31 other events, 163.9 us)
